TPU v7x, 32 devices: a whole 2x2x4 slice. The times are simulated.
32 devices in a mesh: sta: 8 (over y, x, core), hour: 4 (over z).
Axes of the slice: x: 2, y: 2, z: 4, core: 2. Of those that a mesh axis runs over, the one named last changes fastest.
Arguments:
- spectra: bfloat16 [128, 4, 30, 2, 1024], P('sta', 'hour'), may hold values from -1000 to 1000
- band_weight: float32 [1024], replicated, may hold values from 0.5 to 4
- station_order: int32 [8, 16], P('sta'), may hold values from 0 to 15, each once within a row
- pair_blocks: int32 [16, 2], P('sta'), may hold values from 0 to 7, as said below
Outputs:
- cross: float32 [16, 16, 16, 2, 1024], P('sta', None, None, None, 'hour')
Inputs may be any that keep to these rules, and one draw needn't show every extreme that they name: `pair_blocks`: the first block of each pair block belongs to the station group that owns the pair block (pair p to group p // 2); the second belongs to that group or to a group next to it, and every group asks at least once for a block of each group next to it.
All inputs are finite; a program needn't handle non-finite values.
Results may differ from a plain program's by a relative error of at most 0.0041.
Values may be sent and summed in bfloat16 or wider, within the bound.
No kernel may reach another device: no remote copies, remote signals or barrier semaphores. Data moves between devices by JAX's collectives and lax.ppermute only.
A program may use at most 192 MiB of HBM per device.

v0:
```python
import jax
import jax.numpy as jnp
from jax import lax
from jax.sharding import PartitionSpec as P

WINDOWS = 30
STATION_BLOCK = 16


def padded(value, sides, width):
    for axis, dim in sides:
        peers, length = (lax.axis_size(axis), value.shape[dim])
        up = [(i, (i + 1) % peers) for i in range(peers - 1)]
        down = [(j, i) for i, j in up]
        last = lax.slice_in_dim(value, length - width, length, axis=dim)
        first = lax.slice_in_dim(value, 0, width, axis=dim)
        before = lax.ppermute(last, axis, up)
        after = lax.ppermute(first, axis, down)
        value = jnp.concatenate([before, value, after], axis=dim)
    return value


def per_device(spectra, band_weight, station_order, pair_blocks):
    sta_count, hour_count, window_count, parts_count, bin_count = spectra.shape
    values = spectra.astype(jnp.float32)
    energy = jnp.mean(values * values, axis=(3, 4), keepdims=True)
    white = (values * lax.rsqrt(energy + 1e-06) * band_weight).astype(jnp.bfloat16)
    white = white[station_order[0]]
    blocks_here = sta_count // STATION_BLOCK
    white = white.reshape(
        blocks_here, STATION_BLOCK, hour_count, window_count, parts_count, bin_count
    )
    window = padded(white, (("sta", 0),), blocks_here)
    base = (lax.axis_index("sta") - 1) * blocks_here
    first = pair_blocks[:, 0] - base
    second = pair_blocks[:, 1] - base
    left = jnp.take(window, first, axis=0)
    right = jnp.take(window, second, axis=0)
    form = "pshwf,pthwf->pstf"
    real_part = jnp.einsum(
        form, left[:, :, :, :, 0], right[:, :, :, :, 0], preferred_element_type=jnp.float32
    ) + jnp.einsum(
        form, left[:, :, :, :, 1], right[:, :, :, :, 1], preferred_element_type=jnp.float32
    )
    imag_part = jnp.einsum(
        form, left[:, :, :, :, 0], right[:, :, :, :, 1], preferred_element_type=jnp.float32
    ) - jnp.einsum(
        form, left[:, :, :, :, 1], right[:, :, :, :, 0], preferred_element_type=jnp.float32
    )
    cross = jnp.stack([real_part, imag_part], axis=3)
    cross = lax.psum_scatter(cross, "hour", scatter_dimension=4, tiled=True)
    total_hours = hour_count * lax.axis_size("hour")
    return cross / (total_hours * WINDOWS)


def solution(mesh):
    return jax.shard_map(
        per_device,
        mesh=mesh,
        in_specs=(P("sta", "hour", None, None, None), P(), P("sta", None), P("sta", None)),
        out_specs=P("sta", None, None, None, "hour"),
        check_vma=False,
    )
```

profile of v0, /device:TPU:3, one launch (start us, length us, event | category | flops | bytes accessed | tf_op | source)
XLA Modules:
  0.0 377.6 jit_solution(6883062302397849899)
XLA Ops:
  6.5 0.0 copy-start.2
  6.5 0.0 reduce-scatter.4.cloned.1.call-start
  6.5 0.7 fusion.8
  7.2 4.5 %fusion.4 = f32[16,30]{1,0:T(8,128)S(1)} fusion(bf16[16,1,30,2,1024]{4,3,2,1,0:T(2,128)(2,1)} %param.6), kind=kLoop, calls=%fused_computation.22 | loop fusion | flops 2948640 | bytes 1968000 | tf_op jit(solution)/shard_map/reduce_sum | solution.py:26
  11.8 3.6 fusion.7
  15.4 5.6 %gather_fusion = bf16[16,30,2,1024]{3,2,1,0:T(2,128)(2,1)} fusion(bf16[16,30,2,1024]{3,2,1,0:T(2,128)(2,1)S(1)} %fusion.7, s32[1024]{0:T(1024)S(1)} %pad_clamp_fusion.2), kind=kCustom, calls=%fused_computation.4 | custom fusion | bytes 3932224 | tf_op jit(solution)/shard_map/gather | solution.py:28
  21.0 2.6 collective-permute-start.1
  23.6 4.1 %collective-permute-start = (bf16[1,16,1,30,2,1024]{5,4,3,1,2,0:T(2,128)(2,1)}, bf16[1,16,1,30,2,1024]{5,4,3,1,2,0:T(2,128)(2,1)}, u32[]{:S(2)}, u32[]{:S(2)}) collective-permute-start(bf16[1,16,1,30,2,1024]{5,4,3,1,2,0:T(2,128)(2,1)} %bitcast.65), channel_id=1, source_target_pairs={{0,4},{4,8},{8,12},{12,16},{16,20},{20,24},{24,28},{1,5},{5,9},{9,... | collective-permute-start | bytes 5898248 | tf_op jit(solution)/shard_map/ppermute | solution.py:17
  27.7 0.0 copy-done.2
  27.7 0.2 subtract_reduce_fusion
  27.9 39.2 %collective-permute-done.1 = bf16[1,16,1,30,2,1024]{5,4,3,1,2,0:T(2,128)(2,1)S(1)} collective-permute-done((bf16[1,16,1,30,2,1024]{5,4,3,1,2,0:T(2,128)(2,1)}, bf16[1,16,1,30,2,1024]{5,4,3,1,2,0:T(2,128)(2,1)S(1)}, u32[]{:S(2)}, u32[]{:S(2)}) %collective-permute-start.1) | collective-permute-done | bytes 1966112 | tf_op jit(solution)/shard_map/ppermute | solution.py:18
  67.1 0.0 collective-permute-done
  67.1 11.1 %pad_maximum_fusion.1 = bf16[3,16,1,30,2,1024]{5,4,3,1,2,0:T(2,128)(2,1)S(1)} fusion(bf16[1,16,1,30,2,1024]{5,4,3,1,2,0:T(2,128)(2,1)S(1)} %collective-permute-done.1, bf16[1,16,1,30,2,1024]{5,4,3,1,2,0:T(2,128)(2,1)} %bitcast.66, bf16[1,16,1,30,2,1024]{5,4,3,1,2,0:T(2,128)(2,1)} %collective-permute-done), kind=kLoop, calls=%fused_computation.19 | loop fusion | flops 5898240 | bytes 11796480 | tf_op jit(solution)/shard_map/concatenate | solution.py:19
  78.2 5.1 %slice_bitcast_fusion.21 = (bf16[3,16,30,2,512]{4,3,2,1,0:T(2,128)(2,1)S(1)}, bf16[3,16,30,2,512]{4,3,2,1,0:T(2,128)(2,1)}) fusion(bf16[3,16,1,30,2,1024]{5,4,3,1,2,0:T(2,128)(2,1)S(1)} %pad_maximum_fusion.1), kind=kLoop, calls=%fused_computation.26 | loop fusion | bytes 11796480 | tf_op jit(solution)/shard_map/jit(_take)/gather | solution.py:38
  83.3 0.8 copy.47
  84.1 2.0 gather_fusion.3
  86.1 2.0 gather_fusion.1
  88.1 2.6 copy.49
  90.8 2.0 gather_fusion.4
  92.7 2.0 gather_fusion.2
  94.8 10.9 %copy.50 = bf16[2,16,30,2,512]{2,1,4,0,3:T(8,128)(2,1)} copy(bf16[2,16,30,2,512]{4,1,3,2,0:T(8,128)(2,1)} %gather_fusion.2) | data formatting | bytes 3932160 | tf_op jit(solution)/shard_map/jit(_take)/gather | solution.py:38
  105.7 0.0 copy-start.1
  105.7 11.1 %copy.54 = bf16[2,16,30,2,512]{2,1,4,0,3:T(8,128)(2,1)} copy(bf16[2,16,30,2,512]{4,1,3,2,0:T(8,128)(2,1)} %gather_fusion.4) | data formatting | bytes 3932160 | tf_op jit(solution)/shard_map/jit(_take)/gather | solution.py:37
  116.7 10.9 %copy.48 = bf16[2,16,30,2,512]{2,1,4,0,3:T(8,128)(2,1)} copy(bf16[2,16,30,2,512]{4,1,3,2,0:T(8,128)(2,1)} %gather_fusion.1) | data formatting | bytes 3932160 | tf_op jit(solution)/shard_map/jit(_take)/gather | solution.py:38
  127.7 0.0 copy-done.1
  127.7 9.4 %copy.52 = bf16[2,16,30,2,512]{2,1,4,0,3:T(8,128)(2,1)} copy(bf16[2,16,30,2,512]{4,1,3,2,0:T(8,128)(2,1)S(1)} %copy-done.1) | data formatting | bytes 3932160 | tf_op jit(solution)/shard_map/jit(_take)/gather | solution.py:37
  137.1 0.0 copy-start
  137.1 15.5 %maximum_select_fusion = bf16[2,16,1,30,2,1024]{3,1,5,0,4,2:T(8,128)(2,1)} fusion(bf16[2,16,1,30,2,512]{3,1,5,0,4,2:T(8,128)(2,1)} %bitcast.60, bf16[2,16,1,30,2,512]{3,1,5,0,4,2:T(8,128)(2,1)} %bitcast.62, pred[2]{0:T(512)(128)(4,1)S(1)} %get-tuple-element.13), kind=kLoop, calls=%fused_computation.7 | loop fusion | flops 3932160 | bytes 7864322 | tf_op jit(solution)/shard_map/jit(_take)/select_n | solution.py:38
  152.6 0.0 copy-done
  152.6 11.8 %maximum_select_fusion.1 = bf16[2,16,1,30,2,1024]{3,1,5,0,4,2:T(8,128)(2,1)} fusion(bf16[2,16,1,30,2,512]{3,1,5,0,4,2:T(8,128)(2,1)} %bitcast.59, bf16[2,16,1,30,2,512]{3,1,5,0,4,2:T(8,128)(2,1)S(1)} %bitcast.61, pred[2]{0:T(512)(128)(4,1)S(1)} %get-tuple-element.12), kind=kLoop, calls=%fused_computation.8 | loop fusion | flops 3932160 | bytes 7864322 | tf_op jit(solution)/shard_map/jit(_take)/select_n | solution.py:37
  164.3 11.5 %fusion = f32[2,1024,16,16]{3,2,1,0:T(8,128)} fusion(bf16[2,16,1,30,2,1024]{3,1,5,0,4,2:T(8,128)(2,1)} %maximum_select_fusion, bf16[2,16,1,30,2,1024]{3,1,5,0,4,2:T(8,128)(2,1)} %maximum_select_fusion.1), kind=kOutput, calls=%fused_computation.15 | convolution fusion | flops 31457280 | bytes 18874368 | tf_op jit(solution)/shard_map/pshwf,pthwf->pstf/dot_general | solution.py:47
  175.8 11.5 %fusion.1 = f32[2,1024,16,16]{3,2,1,0:T(8,128)} fusion(bf16[2,16,1,30,2,1024]{3,1,5,0,4,2:T(8,128)(2,1)} %maximum_select_fusion, bf16[2,16,1,30,2,1024]{3,1,5,0,4,2:T(8,128)(2,1)} %maximum_select_fusion.1), kind=kOutput, calls=%fused_computation.16 | convolution fusion | flops 31457280 | bytes 18874368 | tf_op jit(solution)/shard_map/pshwf,pthwf->pstf/dot_general | solution.py:40
  187.3 18.6 %subtract_bitcast_fusion = f32[2,16,16,1,1024]{1,2,4,0,3:T(8,128)} fusion(f32[2,1024,16,16]{3,2,1,0:T(8,128)} %fusion, bf16[2,16,1,30,2,1024]{3,1,5,0,4,2:T(8,128)(2,1)} %maximum_select_fusion.1, bf16[2,16,1,30,2,1024]{3,1,5,0,4,2:T(8,128)(2,1)} %maximum_select_fusion), kind=kOutput, calls=%fused_computation.9 | convolution fusion | flops 31981568 | bytes 35651584 | tf_op jit(solution)/shard_map/pshwf,pthwf->pstf/dot_general | solution.py:45
  205.8 18.6 %add_bitcast_fusion = f32[2,16,16,1,1024]{1,2,4,0,3:T(8,128)} fusion(f32[2,1024,16,16]{3,2,1,0:T(8,128)} %fusion.1, bf16[2,16,1,30,2,1024]{3,1,5,0,4,2:T(8,128)(2,1)} %maximum_select_fusion.1, bf16[2,16,1,30,2,1024]{3,1,5,0,4,2:T(8,128)(2,1)} %maximum_select_fusion), kind=kOutput, calls=%fused_computation.10 | convolution fusion | flops 31981568 | bytes 35651584 | tf_op jit(solution)/shard_map/pshwf,pthwf->pstf/dot_general | solution.py:42
  224.4 23.9 %copy_bitcast_fusion = f32[1024,2,2,16,16]{4,3,2,1,0:T(8,128)} fusion(f32[2,16,16,1,1024]{1,2,4,0,3:T(8,128)} %subtract_bitcast_fusion, f32[2,16,16,1,1024]{1,2,4,0,3:T(8,128)} %add_bitcast_fusion), kind=kLoop, calls=%fused_computation.6 | loop fusion | flops 1048576 | bytes 8388608
  248.3 28.3 %reshape.164 = f32[1024,1024]{1,0:T(8,128)} reshape(f32[1024,2,2,16,16]{4,3,2,1,0:T(8,128)} %copy_bitcast_fusion) | data formatting | bytes 8388608
  276.6 0.0 reduce-scatter.4.cloned.1.call-update
  276.7 79.4 %reduce-scatter.4.cloned.1.call-done = f32[256,1024]{1,0:T(8,128)} async-done(((f32[1024,1024]{1,0:T(8,128)}), f32[256,1024]{1,0:T(8,128)}) %reduce-scatter.4.cloned.1.call-update) | async-done | bytes 1048592
  356.0 6.2 %reshape.165 = f32[256,2,2,16,16]{4,3,2,1,0:T(8,128)} reshape(f32[256,1024]{1,0:T(8,128)} %reduce-scatter.4.cloned.1.call-done) | data formatting | bytes 2097152
  362.2 6.7 %copy.55 = f32[2,16,16,2,256]{4,2,3,1,0:T(8,128)S(1)} copy(f32[2,16,16,2,256]{1,2,0,3,4:T(8,128)} %bitcast.63) | data formatting | bytes 2097152 | tf_op jit(solution)/shard_map/reduce_scatter | solution.py:51
  368.9 0.1 broadcast_multiply_fusion
  369.0 1.8 copy.56
  (6 shorter events, 0.0 us)
Async XLA Ops:
  6.5 21.1 %copy-start.2 = (s32[2,2]{1,0:T(2,128)S(1)}, s32[2,2]{1,0:T(2,128)}, u32[]{:S(2)}) copy-start(s32[2,2]{1,0:T(2,128)} %param.9) | copy-start | bytes 52
  6.5 349.5 %reduce-scatter.4.cloned.1.call-start = ((), (), s32[]{:S(2)}) async-start(), calls=%async_computation.1 | async-start | bytes 5242880
  21.0 46.1 %collective-permute-start.1 = (bf16[1,16,1,30,2,1024]{5,4,3,1,2,0:T(2,128)(2,1)}, bf16[1,16,1,30,2,1024]{5,4,3,1,2,0:T(2,128)(2,1)S(1)}, u32[]{:S(2)}, u32[]{:S(2)}) collective-permute-start(bf16[1,16,1,30,2,1024]{5,4,3,1,2,0:T(2,128)(2,1)} %bitcast.64), channel_id=1, source_target_pairs={{4,0},{8,4},{12,8},{16,12},{20,16},{24,20},{28,24},{5,1},{9,5},{13... | collective-permute-start | bytes 5898248 | tf_op jit(solution)/shard_map/ppermute | solution.py:18
  23.6 43.5 %collective-permute-start = (bf16[1,16,1,30,2,1024]{5,4,3,1,2,0:T(2,128)(2,1)}, bf16[1,16,1,30,2,1024]{5,4,3,1,2,0:T(2,128)(2,1)}, u32[]{:S(2)}, u32[]{:S(2)}) collective-permute-start(bf16[1,16,1,30,2,1024]{5,4,3,1,2,0:T(2,128)(2,1)} %bitcast.65), channel_id=1, source_target_pairs={{0,4},{4,8},{8,12},{12,16},{16,20},{20,24},{24,28},{1,5},{5,9},{9,... | collective-permute-start | bytes 5898248 | tf_op jit(solution)/shard_map/ppermute | solution.py:17
  105.7 22.0 %copy-start.1 = (bf16[2,16,30,2,512]{4,1,3,2,0:T(8,128)(2,1)S(1)}, bf16[2,16,30,2,512]{4,1,3,2,0:T(8,128)(2,1)}, u32[]{:S(2)}) copy-start(bf16[2,16,30,2,512]{4,1,3,2,0:T(8,128)(2,1)} %gather_fusion.3) | copy-start | bytes 5898244
  137.1 15.5 %copy-start = (bf16[2,16,30,2,512]{2,1,4,0,3:T(8,128)(2,1)S(1)}, bf16[2,16,30,2,512]{2,1,4,0,3:T(8,128)(2,1)}, u32[]{:S(2)}) copy-start(bf16[2,16,30,2,512]{2,1,4,0,3:T(8,128)(2,1)} %copy.52) | copy-start | bytes 5898244
Sparse Core Ops, SparseCore 0:
  276.8 79.1 reduce-scatter.3
where the time goes:
time: 381 us; the launch traced here: 378 us
  waiting for transfers between devices  119 us (31%)
  local copies, waits for them, and re-layouts  107 us (28%)
  other arithmetic  71.5 us (19%)
  matrix products  60.1 us (16%)
  between operations  13.5 us (4%)
  starting transfers between devices  6.63 us (2%)
    unnamed x2, waiting for transfers between devices  79.4 us
    ppermute x1, waiting for transfers between devices, padded(): after = lax.ppermute(first, axis, down)  39.2 us
    unnamed x8, local copies, waits for them, and re-layouts  34.5 us
    gather x7, local copies, waits for them, and re-layouts, per_device(): right = jnp.take(window, second, axis=0)  34.5 us
    gather x4, local copies, waits for them, and re-layouts, per_device(): left = jnp.take(window, first, axis=0)  24.4 us
    unnamed x1, other arithmetic  23.9 us
    dot_general x1, matrix products, per_device(): jnp.einsum(form, left[:, :, :, :, 1], right[:, :, :, :, 1], preferred_ele...  18.6 us
    dot_general x1, matrix products, per_device(): jnp.einsum(form, left[:, :, :, :, 0], right[:, :, :, :, 1], preferred_ele...  18.6 us
  transfers between devices with their start and end apart: 3, of which 2 were waited for; matrix products, arithmetic and copies ran while one was open for 0% of the time, Pallas kernels for 0%

commit v1 on v0

v1 whole, which is shorter than its diff:
```python
import jax
import jax.numpy as jnp
from jax import lax
from jax.experimental import pallas as pl
from jax.experimental.pallas import tpu as pltpu
from jax.sharding import PartitionSpec as P

LANES = 128
EPSILON = 1e-06
EDGES = 2
GROUPS = ((2,), (1,), (3,), (0,))


def whiten(spectra, band_weight, station_order):
    stations, windows, rows, _ = spectra.shape
    tiles = rows // 2
    step = 6
    hours = tiles // EDGES
    bins = tiles * LANES
    height = 2 * stations

    def body(order_ref, x_ref, band_ref, *refs):
        outs, (band, rowed) = refs[:-2], refs[-2:]

        @pl.when(pl.program_id(0) == 0)
        def _():
            for part in range(2):
                band[pl.ds(part, tiles, stride=2), :] = band_ref[...]

        weight = band[...]
        for w in range(step):
            for s in range(stations):
                x = x_ref[order_ref[0, s], w].astype(jnp.float32)
                energy = jnp.sum(x * x, axis=(0, 1), keepdims=True) / (2 * bins)
                white = x * lax.rsqrt(energy + EPSILON) * weight
                white = white.astype(jnp.bfloat16).astype(jnp.float32)
                rowed[pl.ds(w * rows * stations + s, rows, stride=stations), :] = white
        here = lax.axis_index("hour")
        k = 0
        for edge in range(EDGES):
            for group in GROUPS:
                for i, d in enumerate(group):
                    owner = lax.rem(here + d, hours)
                    for w in range(step):
                        start = (w * tiles + owner * EDGES + edge) * height
                        tile = rowed[pl.ds(pl.multiple_of(start, height), height), :]
                        outs[k][i, w] = tile.astype(jnp.bfloat16)
                k += 1

    shapes = [
        jax.ShapeDtypeStruct((len(group), windows, height, LANES), jnp.bfloat16)
        for _ in range(EDGES)
        for group in GROUPS
    ]
    outs = pl.pallas_call(
        body,
        grid=(windows // step,),
        in_specs=[
            pl.BlockSpec(memory_space=pltpu.SMEM),
            pl.BlockSpec((stations, step, rows, LANES), lambda i: (0, i, 0, 0)),
            pl.BlockSpec((tiles, LANES), lambda i: (0, 0)),
        ],
        out_specs=[
            pl.BlockSpec((len(group), step, height, LANES), lambda i: (0, i, 0, 0))
            for _ in range(EDGES)
            for group in GROUPS
        ],
        out_shape=shapes,
        scratch_shapes=[
            pltpu.VMEM((rows, LANES), jnp.float32),
            pltpu.VMEM((step * rows * stations, LANES), jnp.float32),
        ],
        name="whiten",
    )(station_order, spectra, band_weight)
    count = len(GROUPS)
    return outs[:count], outs[count:]


def unit(own_ref, other_ref, out_ref, wide):
    windows, height, _ = own_ref.shape
    stations = height // 2
    block = 8
    wide[...] = own_ref[...].astype(jnp.float32).reshape(windows * height, LANES)
    for first in range(0, stations, block):

        def body(w, sums):
            other = other_ref[w].astype(jnp.float32)
            re, im = other[:stations], other[stations:]
            new = []
            for i in range(block):
                row = w * height + first + i
                a_re = jnp.broadcast_to(wide[pl.ds(row, 1), :], re.shape)
                a_im = jnp.broadcast_to(wide[pl.ds(row + stations, 1), :], re.shape)
                new.append(sums[2 * i] + a_re * re + a_im * im)
                new.append(sums[2 * i + 1] + a_re * im - a_im * re)
            return tuple(new)

        zero = jnp.zeros((stations, LANES), jnp.float32)
        sums = lax.fori_loop(0, windows, body, (zero,) * (2 * block))
        for i in range(block):
            out_ref[first + i, :stations] = sums[2 * i].astype(out_ref.dtype)
            out_ref[first + i, stations:] = sums[2 * i + 1].astype(out_ref.dtype)


def products(pair_blocks, own, other, dtype):
    pieces, windows, height, _ = own[0].shape
    stations = height // 2

    def body(pairs_ref, *refs):
        own_refs, other_refs, outs = refs[:EDGES], refs[EDGES : 2 * EDGES], refs[2 * EDGES : -2]
        wide, twin = refs[-2:]
        me, count = lax.axis_index("sta"), lax.axis_size("sta")
        asked = pairs_ref[0, 1] == me
        for p in range(1, pairs_ref.shape[0]):
            asked = jnp.logical_or(asked, pairs_ref[p, 1] == me)
        for i in range(pieces):
            for edge in range(EDGES):
                alone = jnp.logical_and(asked, me == (count - 1 if edge else 0))
                out = outs[i].at[edge]

                @pl.when(jnp.logical_not(alone))
                def _(i=i, edge=edge, out=out):
                    unit(own_refs[edge].at[i], other_refs[edge].at[i], out, wide)

                @pl.when(alone)
                def _(i=i, edge=edge, out=out):
                    unit(own_refs[0].at[i], own_refs[0].at[i], twin.at[0], wide)
                    unit(own_refs[1].at[i], own_refs[1].at[i], twin.at[1], wide)
                    column = lax.broadcasted_iota(jnp.int32, (stations, LANES), 0)

                    @pl.loop(0, stations)
                    def _(a):
                        one, two = twin[0, a], twin[1, a]
                        re = jnp.where(column >= a, one[:stations], two[:stations])
                        im = jnp.where(column >= a, one[stations:], two[stations:])
                        im = jnp.where(column == a, two[:stations], im)
                        out[a, :stations] = re.astype(dtype)
                        out[a, stations:] = im.astype(dtype)

    whole = pl.BlockSpec((pieces, windows, height, LANES), lambda: (0, 0, 0, 0))
    shape = (EDGES, stations, height, LANES)
    flops = pieces * EDGES * stations * stations * LANES * windows * 8
    return pl.pallas_call(
        body,
        in_specs=[pl.BlockSpec(memory_space=pltpu.SMEM)] + [whole] * (2 * EDGES),
        out_specs=[pl.BlockSpec(shape, lambda: (0, 0, 0, 0))] * pieces,
        out_shape=[jax.ShapeDtypeStruct(shape, dtype)] * pieces,
        scratch_shapes=[
            pltpu.VMEM((windows * height, LANES), jnp.float32),
            pltpu.VMEM((2, stations, height, LANES), jnp.float32),
        ],
        cost_estimate=pl.CostEstimate(flops=flops, bytes_accessed=1 << 20, transcendentals=0),
        name="products",
    )(pair_blocks, *own, *other)


def add_hours(parts, scale):
    shape = parts[0].shape
    edges, stations, height, _ = shape

    def body(*refs):
        parts_refs, (own_out, turned_0, turned_1), buf = refs[: len(parts)], refs[len(parts) : -1], refs[-1]
        for edge in range(edges):
            for a in range(stations):
                total = parts_refs[0][edge, a].astype(jnp.float32)
                for ref in parts_refs[1:]:
                    total = total + ref[edge, a].astype(jnp.float32)
                total = total * scale
                own_out[edge, a] = total
                for part in range(2):
                    rows = total[part * stations : (part + 1) * stations]
                    if part:
                        rows = -rows
                    buf[edge, pl.ds(part * stations + a, stations, stride=height), :] = rows
        turned_0[...] = buf[0].reshape(stations, height, LANES).astype(turned_0.dtype)
        turned_1[...] = buf[1].reshape(stations, height, LANES).astype(turned_1.dtype)

    return pl.pallas_call(
        body,
        out_shape=[
            jax.ShapeDtypeStruct(shape, jnp.float32),
            jax.ShapeDtypeStruct(shape[1:], jnp.float32),
            jax.ShapeDtypeStruct(shape[1:], jnp.float32),
        ],
        scratch_shapes=[pltpu.VMEM((edges, stations * height, LANES), jnp.float32)],
        name="add_hours",
    )(*parts)


def assemble(pair_blocks, own, turned, other):
    edges, stations, height, _ = own.shape
    pairs = pair_blocks.shape[0]

    def body(pairs_ref, own_ref, turned_0, turned_1, other_0, other_1, out_ref):
        me, count = lax.axis_index("sta"), lax.axis_size("sta")
        turned_refs, other_refs = (turned_0, turned_1), (other_0, other_1)

        def put(p, a, tile, re, im):
            lanes = pl.ds(tile * LANES, LANES)
            out_ref[p, a, :, 0, lanes] = re
            out_ref[p, a, :, 1, lanes] = im

        for p in range(pairs):
            step = pairs_ref[p, 1] - me

            for edge in range(edges):

                @pl.when(step == 2 * edge - 1)
                def _(p=p, edge=edge):
                    for a in range(stations):
                        mine, theirs = own_ref[edge, a], other_refs[edge][a]
                        put(p, a, edge, mine[:stations], mine[stations:])
                        put(p, a, 1 - edge, theirs[:stations], theirs[stations:])

                @pl.when(jnp.logical_and(step == 0, me == (count - 1 if edge else 0)))
                def _(p=p, edge=edge):
                    column = lax.broadcasted_iota(jnp.int32, (stations, LANES), 0)
                    for a in range(stations):
                        mine, turned = own_ref[edge, a], turned_refs[edge][a]
                        m_re, m_im = mine[:stations], mine[stations:]
                        t_re, t_im = turned[:stations], turned[stations:]
                        zero = jnp.zeros_like(m_im)
                        put(
                            p, a, 0, jnp.where(column >= a, m_re, t_re),
                            jnp.where(column == a, zero, jnp.where(column > a, m_im, t_im)),
                        )
                        put(
                            p, a, 1,
                            jnp.where(column == a, m_im, jnp.where(column < a, m_re, t_re)),
                            jnp.where(column == a, zero, jnp.where(column < a, m_im, t_im)),
                        )

    vmem = pl.BlockSpec(memory_space=pltpu.VMEM)
    return pl.pallas_call(
        body,
        in_specs=[pl.BlockSpec(memory_space=pltpu.SMEM)] + [vmem] * 5,
        out_specs=vmem,
        out_shape=jax.ShapeDtypeStruct((pairs, stations, stations, 2, edges * LANES), jnp.float32),
        name="assemble",
    )(pair_blocks, own, *turned, *other)


def per_device(spectra, band_weight, station_order, pair_blocks):
    stations, _, windows, _, bins = spectra.shape
    tiles = bins // LANES
    count, hours = lax.axis_size("sta"), lax.axis_size("hour")
    rows = spectra.reshape(stations, windows, 2, tiles, LANES)
    rows = rows.transpose(0, 1, 3, 2, 4).reshape(stations, windows, 2 * tiles, LANES)
    own = whiten(rows, band_weight.reshape(tiles, LANES), station_order)

    up = [(i, i + 1) for i in range(count - 1)]
    down = [(j, i) for i, j in up]
    moved = [
        (lax.ppermute(own[0][k], "sta", up), lax.ppermute(own[1][k], "sta", down))
        for k in range(len(GROUPS))
    ]
    parts = []
    for k, group in enumerate(GROUPS):
        made = products(pair_blocks, (own[0][k], own[1][k]), moved[k], jnp.bfloat16)
        for d, piece in zip(group, made):
            if d:
                piece = lax.ppermute(piece, "hour", [(h, (h + d) % hours) for h in range(hours)])
            parts.append(piece)
    mine, turned_0, turned_1 = add_hours(parts, 1.0 / (hours * windows))
    other_0 = lax.ppermute(turned_1, "sta", up)
    other_1 = lax.ppermute(turned_0, "sta", down)
    return assemble(pair_blocks, mine, (turned_0, turned_1), (other_0, other_1))


def solution(mesh):
    return jax.shard_map(
        per_device,
        mesh=mesh,
        in_specs=(P("sta", "hour", None, None, None), P(), P("sta", None), P("sta", None)),
        out_specs=P("sta", None, None, None, "hour"),
        check_vma=False,
    )
```

time: 381 us -> 89.8 us (0.24)
  the two profiles are of different devices: /device:TPU:3 before, /device:TPU:12 now
where the time goes in v1:
time: 89.8 us; the launch traced here: 89.2 us
  starting transfers between devices  37.5 us (42%)
  Pallas kernels  33 us (37%)
  waiting for transfers between devices  11.4 us (13%)
  local copies, waits for them, and re-layouts  7.07 us (8%)
    pallas_call x4, Pallas kernels, products(): pl.pallas_call(body, in_specs=[pl.BlockSpec(memory_space=pltpu.SMEM)] + [...  21.7 us
    ppermute x4, starting transfers between devices, per_device(): lax.ppermute(own[1][k], 'sta', down)  18.2 us
    ppermute x4, starting transfers between devices, per_device(): lax.ppermute(own[0][k], 'sta', up)  7.8 us
    unnamed x30, local copies, waits for them, and re-layouts  7.07 us
    ppermute x3, starting transfers between devices, per_device(): lax.ppermute(piece, 'hour', [(h, (h + d) % hours) for h in range(hours)])  6.41 us
    pallas_call x1, Pallas kernels, whiten(): pl.pallas_call(body, grid=(windows // step,), in_specs=[pl.BlockSpec(memo...  5.82 us
    ppermute x1, waiting for transfers between devices, per_device(): other_1 = lax.ppermute(turned_0, 'sta', down)  4.7 us
    ppermute x4, waiting for transfers between devices, per_device(): lax.ppermute(own[0][k], 'sta', up)  4.51 us
  transfers between devices with their start and end apart: 13, of which 3 were waited for; matrix products, arithmetic and copies ran while one was open for 0% of the time, Pallas kernels for 24%

profile of v1, /device:TPU:12, one launch (start us, length us, event | category | flops | bytes accessed | tf_op | source)
XLA Modules:
  0.0 89.2 jit_solution(14022417578973568779)
XLA Ops:
  0.0 5.8 %whiten.1 = (bf16[1,30,32,128]{3,2,1,0:T(8,128)(2,1)}, bf16[1,30,32,128]{3,2,1,0:T(8,128)(2,1)}, bf16[1,30,32,128]{3,2,1,0:T(8,128)(2,1)}, bf16[1,30,32,128]{3,2...) custom-call(s32[1,16]{1,0:T(1,128)} %order_ref.1, ...), custom_call_target="tpu_custom_call" | custom-call | tf_op jit(solution)/shard_map/whiten/pallas_call | solution.py:55
  5.8 0.0 copy-start.6
  5.8 2.1 %collective-permute-start.6 = (bf16[1,30,32,128]{3,2,1,0:T(8,128)(2,1)}, bf16[1,30,32,128]{3,2,1,0:T(8,128)(2,1)S(1)}, u32[]{:S(2)}, u32[]{:S(2)}) collective-permute-start(bf16[1,30,32,128]{3,2,1,0:T(8,128)(2,1)} %get-tuple-element.20.refs_0_), channel_id=1, source_target_pairs={{0,4},{4,8},{8,12},{12,16},{16,20},{20,24},{24,28},{1,5},{5,9},{9,... | collective-permute-start | bytes 737288 | tf_op jit(solution)/shard_map/ppermute | solution.py:254
  7.9 4.5 %collective-permute-start.7 = (bf16[1,30,32,128]{3,2,1,0:T(8,128)(2,1)}, bf16[1,30,32,128]{3,2,1,0:T(8,128)(2,1)S(1)}, u32[]{:S(2)}, u32[]{:S(2)}) collective-permute-start(bf16[1,30,32,128]{3,2,1,0:T(8,128)(2,1)} %get-tuple-element.21.refs_1_), channel_id=1, source_target_pairs={{4,0},{8,4},{12,8},{16,12},{20,16},{24,20},{28,24},{5,1},{9,5},{13... | collective-permute-start | bytes 737288 | tf_op jit(solution)/shard_map/ppermute | solution.py:254
  12.4 1.9 %collective-permute-start.3 = (bf16[1,30,32,128]{3,2,1,0:T(8,128)(2,1)}, bf16[1,30,32,128]{3,2,1,0:T(8,128)(2,1)S(1)}, u32[]{:S(2)}, u32[]{:S(2)}) collective-permute-start(bf16[1,30,32,128]{3,2,1,0:T(8,128)(2,1)} %get-tuple-element.18.refs_0_), channel_id=1, source_target_pairs={{0,4},{4,8},{8,12},{12,16},{16,20},{20,24},{24,28},{1,5},{5,9},{9,... | collective-permute-start | bytes 737288 | tf_op jit(solution)/shard_map/ppermute | solution.py:254
  14.4 4.5 %collective-permute-start.4 = (bf16[1,30,32,128]{3,2,1,0:T(8,128)(2,1)}, bf16[1,30,32,128]{3,2,1,0:T(8,128)(2,1)S(1)}, u32[]{:S(2)}, u32[]{:S(2)}) collective-permute-start(bf16[1,30,32,128]{3,2,1,0:T(8,128)(2,1)} %get-tuple-element.19.refs_1_), channel_id=1, source_target_pairs={{4,0},{8,4},{12,8},{16,12},{20,16},{24,20},{28,24},{5,1},{9,5},{13... | collective-permute-start | bytes 737288 | tf_op jit(solution)/shard_map/ppermute | solution.py:254
  18.9 1.9 %collective-permute-start = (bf16[1,30,32,128]{3,2,1,0:T(8,128)(2,1)}, bf16[1,30,32,128]{3,2,1,0:T(8,128)(2,1)S(1)}, u32[]{:S(2)}, u32[]{:S(2)}) collective-permute-start(bf16[1,30,32,128]{3,2,1,0:T(8,128)(2,1)} %get-tuple-element.16.refs_0_), channel_id=1, source_target_pairs={{0,4},{4,8},{8,12},{12,16},{16,20},{20,24},{24,28},{1,5},{5,9},{9,... | collective-permute-start | bytes 737288 | tf_op jit(solution)/shard_map/ppermute | solution.py:254
  20.8 0.0 collective-permute-done.6.refs_2_
  20.9 0.0 copy-start.11
  20.9 4.5 %collective-permute-start.1 = (bf16[1,30,32,128]{3,2,1,0:T(8,128)(2,1)}, bf16[1,30,32,128]{3,2,1,0:T(8,128)(2,1)S(1)}, u32[]{:S(2)}, u32[]{:S(2)}) collective-permute-start(bf16[1,30,32,128]{3,2,1,0:T(8,128)(2,1)} %get-tuple-element.17.refs_1_), channel_id=1, source_target_pairs={{4,0},{8,4},{12,8},{16,12},{20,16},{24,20},{28,24},{5,1},{9,5},{13... | collective-permute-start | bytes 737288 | tf_op jit(solution)/shard_map/ppermute | solution.py:254
  25.4 0.0 collective-permute-done.7.refs_3_
  25.4 0.0 copy-done.11
  25.4 0.7 copy-done.12
  26.1 5.4 %products.6 = bf16[2,16,32,128]{3,2,1,0:T(8,128)(2,1)} custom-call(s32[2,2]{1,0:T(2,128)} %pairs_ref.9, bf16[1,30,32,128]{3,2,1,0:T(8,128)(2,1)} %get-tuple-element.20.refs_0_, bf16[1,30,32,128]{3,2,1,0:T(8,128)(2,1)} %get-tuple-element.21.refs_1_, bf16[1,30,32,128]{3,2,1,0:T(8,128)(2,1)} %copy-done.11, bf16[1,30,32,128]{3,2,1,0:T(8,128)(2,1)} %copy-done.12), custom_call_target="tpu_custom_call" | custom-call | flops 15728640 | bytes 1048576 | tf_op jit(solution)/shard_map/products/pallas_call | solution.py:143
  31.5 0.4 collective-permute-start.8
  32.0 0.0 collective-permute-done.3.refs_2_
  32.0 0.0 collective-permute-done.4.refs_3_
  32.0 0.7 copy-done.9
  32.7 0.7 copy-done.10
  33.4 5.4 %products.5 = bf16[2,16,32,128]{3,2,1,0:T(8,128)(2,1)} custom-call(s32[2,2]{1,0:T(2,128)} %pairs_ref.9, bf16[1,30,32,128]{3,2,1,0:T(8,128)(2,1)} %get-tuple-element.18.refs_0_, bf16[1,30,32,128]{3,2,1,0:T(8,128)(2,1)} %get-tuple-element.19.refs_1_, bf16[1,30,32,128]{3,2,1,0:T(8,128)(2,1)} %copy-done.9, bf16[1,30,32,128]{3,2,1,0:T(8,128)(2,1)} %copy-done.10), custom_call_target="tpu_custom_call" | custom-call | flops 15728640 | bytes 1048576 | tf_op jit(solution)/shard_map/products/pallas_call | solution.py:143
  38.8 1.6 %collective-permute-start.5 = (bf16[2,16,32,128]{3,2,1,0:T(8,128)(2,1)}, bf16[2,16,32,128]{3,2,1,0:T(8,128)(2,1)S(1)}, u32[]{:S(2)}, u32[]{:S(2)}) collective-permute-start(bf16[2,16,32,128]{3,2,1,0:T(8,128)(2,1)} %products.5), channel_id=1, source_target_pairs={{0,1},{1,2},{2,3},{3,0},{4,5},{5,6},{6,7},{7,4},{8,9},{9,10},{10,1... | collective-permute-start | bytes 786440 | tf_op jit(solution)/shard_map/ppermute | solution.py:262
  40.4 0.0 collective-permute-done.refs_2_
  40.4 0.0 collective-permute-done.1.refs_3_
  40.4 0.7 copy-done.7
  41.1 0.7 copy-done.8
  41.8 5.4 %products.4 = bf16[2,16,32,128]{3,2,1,0:T(8,128)(2,1)} custom-call(s32[2,2]{1,0:T(2,128)} %pairs_ref.9, bf16[1,30,32,128]{3,2,1,0:T(8,128)(2,1)} %get-tuple-element.16.refs_0_, bf16[1,30,32,128]{3,2,1,0:T(8,128)(2,1)} %get-tuple-element.17.refs_1_, bf16[1,30,32,128]{3,2,1,0:T(8,128)(2,1)} %copy-done.7, bf16[1,30,32,128]{3,2,1,0:T(8,128)(2,1)} %copy-done.8), custom_call_target="tpu_custom_call" | custom-call | flops 15728640 | bytes 1048576 | tf_op jit(solution)/shard_map/products/pallas_call | solution.py:143
  47.2 4.4 %collective-permute-start.2 = (bf16[2,16,32,128]{3,2,1,0:T(8,128)(2,1)}, bf16[2,16,32,128]{3,2,1,0:T(8,128)(2,1)S(1)}, u32[]{:S(2)}, u32[]{:S(2)}) collective-permute-start(bf16[2,16,32,128]{3,2,1,0:T(8,128)(2,1)} %products.4), channel_id=1, source_target_pairs={{0,2},{1,3},{2,0},{3,1},{4,6},{5,7},{6,4},{7,5},{8,10},{9,11},{10,... | collective-permute-start | bytes 786440 | tf_op jit(solution)/shard_map/ppermute | solution.py:262
  51.6 1.9 %collective-permute-start.9 = (bf16[1,30,32,128]{3,2,1,0:T(8,128)(2,1)S(1)}, bf16[1,30,32,128]{3,2,1,0:T(8,128)(2,1)S(1)}, u32[]{:S(2)}, u32[]{:S(2)}) collective-permute-start(bf16[1,30,32,128]{3,2,1,0:T(8,128)(2,1)S(1)} %copy-done.5), channel_id=1, source_target_pairs={{0,4},{4,8},{8,12},{12,16},{16,20},{20,24},{24,28},{1,5},{5,9},{9,... | collective-permute-start | bytes 737288 | tf_op jit(solution)/shard_map/ppermute | solution.py:254
  53.5 4.5 %collective-permute-start.10 = (bf16[1,30,32,128]{3,2,1,0:T(8,128)(2,1)S(1)}, bf16[1,30,32,128]{3,2,1,0:T(8,128)(2,1)S(1)}, u32[]{:S(2)}, u32[]{:S(2)}) collective-permute-start(bf16[1,30,32,128]{3,2,1,0:T(8,128)(2,1)S(1)} %copy-done.6), channel_id=1, source_target_pairs={{4,0},{8,4},{12,8},{16,12},{20,16},{24,20},{28,24},{5,1},{9,5},{13... | collective-permute-start | bytes 737288 | tf_op jit(solution)/shard_map/ppermute | solution.py:254
  58.1 4.5 %collective-permute-done.9.refs_2_ = bf16[1,30,32,128]{3,2,1,0:T(8,128)(2,1)S(1)} collective-permute-done((bf16[1,30,32,128]{3,2,1,0:T(8,128)(2,1)S(1)}, bf16[1,30,32,128]{3,2,1,0:T(8,128)(2,1)S(1)}, u32[]{:S(2)}, u32[]{:S(2)}) %collective-permute-start.9) | collective-permute-done | bytes 245792 | tf_op jit(solution)/shard_map/ppermute | solution.py:254
  62.6 0.0 collective-permute-done.10.refs_3_
  62.6 0.7 copy-done.13
  63.3 0.7 copy-done.14
  64.0 5.4 %products.7.refs_3_ = bf16[2,16,32,128]{3,2,1,0:T(8,128)(2,1)} custom-call(s32[2,2]{1,0:T(2,128)} %pairs_ref.9, bf16[1,30,32,128]{3,2,1,0:T(8,128)(2,1)} %get-tuple-element.22.refs_0_, bf16[1,30,32,128]{3,2,1,0:T(8,128)(2,1)} %get-tuple-element.23.refs_1_, bf16[1,30,32,128]{3,2,1,0:T(8,128)(2,1)} %copy-done.13, bf16[1,30,32,128]{3,2,1,0:T(8,128)(2,1)} %copy-done.14), custom_call_target="tpu_custom_call" | custom-call | flops 15728640 | bytes 1048576 | tf_op jit(solution)/shard_map/products/pallas_call | solution.py:143
  69.4 0.0 collective-permute-done.8.refs_2_
  69.4 0.0 collective-permute-done.5.refs_1_
  69.4 0.0 copy-start.3
  69.4 0.0 collective-permute-done.2.refs_0_
  69.4 0.7 copy-done.2
  70.1 0.1 copy-done.3
  70.2 0.7 copy-done.4
  70.9 2.6 %add_hours.1 = (f32[2,16,32,128]{3,2,1,0:T(8,128)}, f32[16,32,128]{2,1,0:T(8,128)}, f32[16,32,128]{2,1,0:T(8,128)}) custom-call(bf16[2,16,32,128]{3,2,1,0:T(8,128)(2,1)} %copy-done.4, bf16[2,16,32,128]{3,2,1,0:T(8,128)(2,1)} %copy-done.3, bf16[2,16,32,128]{3,2,1,0:T(8,128)(2,1)} %copy-done.2, bf16[2,16,32,128]{3,2,1,0:T(8,128)(2,1)} %products.7.refs_3_), custom_call_target="tpu_custom_call" | custom-call | tf_op jit(solution)/shard_map/add_hours/pallas_call | solution.py:178
  73.5 3.2 %collective-permute-start.12 = (f32[16,32,128]{2,1,0:T(8,128)}, f32[16,32,128]{2,1,0:T(8,128)S(1)}, u32[]{:S(2)}, u32[]{:S(2)}) collective-permute-start(f32[16,32,128]{2,1,0:T(8,128)} %get-tuple-element.25.turned_0), channel_id=1, source_target_pairs={{4,0},{8,4},{12,8},{16,12},{20,16},{24,20},{28,24},{5,1},{9,5},{13... | collective-permute-start | bytes 786440 | tf_op jit(solution)/shard_map/ppermute | solution.py:266
  76.7 1.9 %collective-permute-start.11 = (f32[16,32,128]{2,1,0:T(8,128)}, f32[16,32,128]{2,1,0:T(8,128)S(1)}, u32[]{:S(2)}, u32[]{:S(2)}) collective-permute-start(f32[16,32,128]{2,1,0:T(8,128)} %get-tuple-element.26.turned_1), channel_id=1, source_target_pairs={{0,4},{4,8},{8,12},{12,16},{16,20},{20,24},{24,28},{1,5},{5,9},{9,... | collective-permute-start | bytes 786440 | tf_op jit(solution)/shard_map/ppermute | solution.py:265
  78.6 4.7 %collective-permute-done.12.other_1 = f32[16,32,128]{2,1,0:T(8,128)S(1)} collective-permute-done((f32[16,32,128]{2,1,0:T(8,128)}, f32[16,32,128]{2,1,0:T(8,128)S(1)}, u32[]{:S(2)}, u32[]{:S(2)}) %collective-permute-start.12) | collective-permute-done | bytes 262176 | tf_op jit(solution)/shard_map/ppermute | solution.py:266
  83.3 2.2 %collective-permute-done.11.other_0 = f32[16,32,128]{2,1,0:T(8,128)S(1)} collective-permute-done((f32[16,32,128]{2,1,0:T(8,128)}, f32[16,32,128]{2,1,0:T(8,128)S(1)}, u32[]{:S(2)}, u32[]{:S(2)}) %collective-permute-start.11) | collective-permute-done | bytes 262176 | tf_op jit(solution)/shard_map/ppermute | solution.py:265
  85.5 0.7 copy-done.1
  86.2 2.9 %assemble.1 = f32[2,16,16,2,256]{4,3,2,1,0:T(2,128)} custom-call(s32[2,2]{1,0:T(2,128)} %pairs_ref.9, f32[2,16,32,128]{3,2,1,0:T(8,128)} %get-tuple-element.24.own_ref, f32[16,32,128]{2,1,0:T(8,128)} %get-tuple-element.25.turned_0, f32[16,32,128]{2,1,0:T(8,128)} %get-tuple-element.26.turned_1, f32[16,32,128]{2,1,0:T(8,128)} %copy-done.1, f32[16,32,128]{2,1,0:T(8,128)} %copy-done), custom_call_target="tpu_custom_call" | custom-call | tf_op jit(solution)/shard_map/assemble/pallas_call | solution.py:234
  (15 shorter events, 0.0 us)
Async XLA Ops:
  5.8 45.8 %copy-start.5 = (bf16[1,30,32,128]{3,2,1,0:T(8,128)(2,1)S(1)}, bf16[1,30,32,128]{3,2,1,0:T(8,128)(2,1)}, u32[]{:S(2)}) copy-start(bf16[1,30,32,128]{3,2,1,0:T(8,128)(2,1)} %get-tuple-element.22.refs_0_) | copy-start | bytes 737284
  5.8 47.7 %copy-start.6 = (bf16[1,30,32,128]{3,2,1,0:T(8,128)(2,1)S(1)}, bf16[1,30,32,128]{3,2,1,0:T(8,128)(2,1)}, u32[]{:S(2)}) copy-start(bf16[1,30,32,128]{3,2,1,0:T(8,128)(2,1)} %get-tuple-element.23.refs_1_) | copy-start | bytes 737284
  5.8 15.0 %collective-permute-start.6 = (bf16[1,30,32,128]{3,2,1,0:T(8,128)(2,1)}, bf16[1,30,32,128]{3,2,1,0:T(8,128)(2,1)S(1)}, u32[]{:S(2)}, u32[]{:S(2)}) collective-permute-start(bf16[1,30,32,128]{3,2,1,0:T(8,128)(2,1)} %get-tuple-element.20.refs_0_), channel_id=1, source_target_pairs={{0,4},{4,8},{8,12},{12,16},{16,20},{20,24},{24,28},{1,5},{5,9},{9,... | collective-permute-start | bytes 737288 | tf_op jit(solution)/shard_map/ppermute | solution.py:254
  7.9 17.5 %collective-permute-start.7 = (bf16[1,30,32,128]{3,2,1,0:T(8,128)(2,1)}, bf16[1,30,32,128]{3,2,1,0:T(8,128)(2,1)S(1)}, u32[]{:S(2)}, u32[]{:S(2)}) collective-permute-start(bf16[1,30,32,128]{3,2,1,0:T(8,128)(2,1)} %get-tuple-element.21.refs_1_), channel_id=1, source_target_pairs={{4,0},{8,4},{12,8},{16,12},{20,16},{24,20},{28,24},{5,1},{9,5},{13... | collective-permute-start | bytes 737288 | tf_op jit(solution)/shard_map/ppermute | solution.py:254
  12.4 19.6 %collective-permute-start.3 = (bf16[1,30,32,128]{3,2,1,0:T(8,128)(2,1)}, bf16[1,30,32,128]{3,2,1,0:T(8,128)(2,1)S(1)}, u32[]{:S(2)}, u32[]{:S(2)}) collective-permute-start(bf16[1,30,32,128]{3,2,1,0:T(8,128)(2,1)} %get-tuple-element.18.refs_0_), channel_id=1, source_target_pairs={{0,4},{4,8},{8,12},{12,16},{16,20},{20,24},{24,28},{1,5},{5,9},{9,... | collective-permute-start | bytes 737288 | tf_op jit(solution)/shard_map/ppermute | solution.py:254
  14.4 17.6 %collective-permute-start.4 = (bf16[1,30,32,128]{3,2,1,0:T(8,128)(2,1)}, bf16[1,30,32,128]{3,2,1,0:T(8,128)(2,1)S(1)}, u32[]{:S(2)}, u32[]{:S(2)}) collective-permute-start(bf16[1,30,32,128]{3,2,1,0:T(8,128)(2,1)} %get-tuple-element.19.refs_1_), channel_id=1, source_target_pairs={{4,0},{8,4},{12,8},{16,12},{20,16},{24,20},{28,24},{5,1},{9,5},{13... | collective-permute-start | bytes 737288 | tf_op jit(solution)/shard_map/ppermute | solution.py:254
  18.9 21.5 %collective-permute-start = (bf16[1,30,32,128]{3,2,1,0:T(8,128)(2,1)}, bf16[1,30,32,128]{3,2,1,0:T(8,128)(2,1)S(1)}, u32[]{:S(2)}, u32[]{:S(2)}) collective-permute-start(bf16[1,30,32,128]{3,2,1,0:T(8,128)(2,1)} %get-tuple-element.16.refs_0_), channel_id=1, source_target_pairs={{0,4},{4,8},{8,12},{12,16},{16,20},{20,24},{24,28},{1,5},{5,9},{9,... | collective-permute-start | bytes 737288 | tf_op jit(solution)/shard_map/ppermute | solution.py:254
  20.9 4.6 %copy-start.11 = (bf16[1,30,32,128]{3,2,1,0:T(8,128)(2,1)}, bf16[1,30,32,128]{3,2,1,0:T(8,128)(2,1)S(1)}, u32[]{:S(2)}) copy-start(bf16[1,30,32,128]{3,2,1,0:T(8,128)(2,1)S(1)} %collective-permute-done.6.refs_2_) | copy-start | bytes 737284
  20.9 19.5 %collective-permute-start.1 = (bf16[1,30,32,128]{3,2,1,0:T(8,128)(2,1)}, bf16[1,30,32,128]{3,2,1,0:T(8,128)(2,1)S(1)}, u32[]{:S(2)}, u32[]{:S(2)}) collective-permute-start(bf16[1,30,32,128]{3,2,1,0:T(8,128)(2,1)} %get-tuple-element.17.refs_1_), channel_id=1, source_target_pairs={{4,0},{8,4},{12,8},{16,12},{20,16},{24,20},{28,24},{5,1},{9,5},{13... | collective-permute-start | bytes 737288 | tf_op jit(solution)/shard_map/ppermute | solution.py:254
  25.4 0.7 copy-start.12
  31.5 37.8 %collective-permute-start.8 = (bf16[2,16,32,128]{3,2,1,0:T(8,128)(2,1)}, bf16[2,16,32,128]{3,2,1,0:T(8,128)(2,1)S(1)}, u32[]{:S(2)}, u32[]{:S(2)}) collective-permute-start(bf16[2,16,32,128]{3,2,1,0:T(8,128)(2,1)} %products.6), channel_id=1, source_target_pairs={{0,3},{1,0},{2,1},{3,2},{4,7},{5,4},{6,5},{7,6},{8,11},{9,8},{10,9... | collective-permute-start | bytes 786440 | tf_op jit(solution)/shard_map/ppermute | solution.py:262
  32.0 0.7 copy-start.9
  32.7 0.7 copy-start.10
  38.8 30.6 %collective-permute-start.5 = (bf16[2,16,32,128]{3,2,1,0:T(8,128)(2,1)}, bf16[2,16,32,128]{3,2,1,0:T(8,128)(2,1)S(1)}, u32[]{:S(2)}, u32[]{:S(2)}) collective-permute-start(bf16[2,16,32,128]{3,2,1,0:T(8,128)(2,1)} %products.5), channel_id=1, source_target_pairs={{0,1},{1,2},{2,3},{3,0},{4,5},{5,6},{6,7},{7,4},{8,9},{9,10},{10,1... | collective-permute-start | bytes 786440 | tf_op jit(solution)/shard_map/ppermute | solution.py:262
  40.4 0.7 copy-start.7
  41.1 0.7 copy-start.8
  47.2 22.2 %collective-permute-start.2 = (bf16[2,16,32,128]{3,2,1,0:T(8,128)(2,1)}, bf16[2,16,32,128]{3,2,1,0:T(8,128)(2,1)S(1)}, u32[]{:S(2)}, u32[]{:S(2)}) collective-permute-start(bf16[2,16,32,128]{3,2,1,0:T(8,128)(2,1)} %products.4), channel_id=1, source_target_pairs={{0,2},{1,3},{2,0},{3,1},{4,6},{5,7},{6,4},{7,5},{8,10},{9,11},{10,... | collective-permute-start | bytes 786440 | tf_op jit(solution)/shard_map/ppermute | solution.py:262
  51.6 11.0 %collective-permute-start.9 = (bf16[1,30,32,128]{3,2,1,0:T(8,128)(2,1)S(1)}, bf16[1,30,32,128]{3,2,1,0:T(8,128)(2,1)S(1)}, u32[]{:S(2)}, u32[]{:S(2)}) collective-permute-start(bf16[1,30,32,128]{3,2,1,0:T(8,128)(2,1)S(1)} %copy-done.5), channel_id=1, source_target_pairs={{0,4},{4,8},{8,12},{12,16},{16,20},{20,24},{24,28},{1,5},{5,9},{9,... | collective-permute-start | bytes 737288 | tf_op jit(solution)/shard_map/ppermute | solution.py:254
  53.5 9.1 %collective-permute-start.10 = (bf16[1,30,32,128]{3,2,1,0:T(8,128)(2,1)S(1)}, bf16[1,30,32,128]{3,2,1,0:T(8,128)(2,1)S(1)}, u32[]{:S(2)}, u32[]{:S(2)}) collective-permute-start(bf16[1,30,32,128]{3,2,1,0:T(8,128)(2,1)S(1)} %copy-done.6), channel_id=1, source_target_pairs={{4,0},{8,4},{12,8},{16,12},{20,16},{24,20},{28,24},{5,1},{9,5},{13... | collective-permute-start | bytes 737288 | tf_op jit(solution)/shard_map/ppermute | solution.py:254
  62.6 0.7 copy-start.13
  63.3 0.7 copy-start.14
  69.4 0.7 copy-start.2
  69.4 0.8 copy-start.3
  70.2 0.7 copy-start.4
  73.5 9.8 %collective-permute-start.12 = (f32[16,32,128]{2,1,0:T(8,128)}, f32[16,32,128]{2,1,0:T(8,128)S(1)}, u32[]{:S(2)}, u32[]{:S(2)}) collective-permute-start(f32[16,32,128]{2,1,0:T(8,128)} %get-tuple-element.25.turned_0), channel_id=1, source_target_pairs={{4,0},{8,4},{12,8},{16,12},{20,16},{24,20},{28,24},{5,1},{9,5},{13... | collective-permute-start | bytes 786440 | tf_op jit(solution)/shard_map/ppermute | solution.py:266
  76.7 8.8 %collective-permute-start.11 = (f32[16,32,128]{2,1,0:T(8,128)}, f32[16,32,128]{2,1,0:T(8,128)S(1)}, u32[]{:S(2)}, u32[]{:S(2)}) collective-permute-start(f32[16,32,128]{2,1,0:T(8,128)} %get-tuple-element.26.turned_1), channel_id=1, source_target_pairs={{0,4},{4,8},{8,12},{12,16},{16,20},{20,24},{24,28},{1,5},{5,9},{9,... | collective-permute-start | bytes 786440 | tf_op jit(solution)/shard_map/ppermute | solution.py:265
  83.3 2.2 %copy-start = (f32[16,32,128]{2,1,0:T(8,128)}, f32[16,32,128]{2,1,0:T(8,128)S(1)}, u32[]{:S(2)}) copy-start(f32[16,32,128]{2,1,0:T(8,128)S(1)} %collective-permute-done.12.other_1) | copy-start | bytes 786436
  85.5 0.7 copy-start.1

commit v2 on v0

v2 whole, which is shorter than its diff:
```python
import jax
import jax.numpy as jnp
from jax import lax
from jax.experimental import pallas as pl
from jax.experimental.pallas import tpu as pltpu
from jax.sharding import PartitionSpec as P

LANES = 128
EPSILON = 1e-06
BLOCK = 8
WIDE = jnp.float32
SMEM = pl.BlockSpec(memory_space=pltpu.SMEM)
VMEM = pl.BlockSpec(memory_space=pltpu.VMEM)


def limits(mib):
    return pltpu.CompilerParams(vmem_limit_bytes=mib << 20)


def asks_itself(pairs_ref, me):
    asked = pairs_ref[0, 1] == me
    for p in range(1, pairs_ref.shape[0]):
        asked = jnp.logical_or(asked, pairs_ref[p, 1] == me)
    return asked


def whiten(spectra, band_weight, station_order, pair_blocks, hours):
    stations, windows, rows, _ = spectra.shape
    tiles = rows // 2
    mine = tiles // hours
    step = windows // 5
    chunks = windows // step
    height = 2 * stations

    def body(order_ref, pairs_ref, band_ref, x_hbm, *refs):
        outs, (band, rowed, x_ref, sems) = refs[:hours], refs[hours:]

        def fetch(c):
            part = pl.ds(c * step, step)
            return pltpu.make_async_copy(x_hbm.at[:, part], x_ref.at[:, part], sems.at[c])

        for c in range(chunks):
            fetch(c).start()
        for part in range(2):
            band[pl.ds(part, tiles, stride=2), :] = band_ref[...]
        weight = band[...]
        here = lax.axis_index("hour")
        asked = asks_itself(pairs_ref, lax.axis_index("sta"))
        flag = jnp.where(asked, 1.0, 0.0)
        for out in outs:
            out[mine * windows] = jnp.full((height, LANES), flag, WIDE).astype(jnp.bfloat16)

        @pl.loop(0, chunks)
        def _(c):
            fetch(c).wait()
            for w in range(step):
                for first in range(0, stations, BLOCK):
                    xs, squares = [], []
                    for k in range(BLOCK):
                        x = x_ref[order_ref[0, first + k], c * step + w].astype(WIDE)
                        xs.append(x)
                        squares.append(jnp.sum(x * x, axis=0, keepdims=True))
                    energy = jnp.sum(jnp.concatenate(squares, axis=0), axis=1, keepdims=True)
                    scale = lax.rsqrt(energy / (rows * LANES) + EPSILON)
                    scale = jnp.broadcast_to(scale, (BLOCK, LANES))
                    for k, x in enumerate(xs):
                        factor = jnp.broadcast_to(scale[k : k + 1], (rows, LANES))
                        place = pl.ds(w * rows * stations + first + k, rows, stride=stations)
                        rowed[place, :] = x * factor * weight
            for d in range(hours):
                owner = lax.rem(here + d, hours)
                for tile in range(mine):
                    for w in range(step):
                        start = (w * tiles + owner * mine + tile) * height
                        white = rowed[pl.ds(pl.multiple_of(start, height), height), :]
                        outs[d][tile * windows + c * step + w] = white.astype(jnp.bfloat16)

    shape = (mine * windows + 1, height, LANES)
    return pl.pallas_call(
        body,
        in_specs=[SMEM, SMEM, VMEM, pl.BlockSpec(memory_space=pltpu.HBM)],
        out_specs=[VMEM] * hours,
        out_shape=[jax.ShapeDtypeStruct(shape, jnp.bfloat16)] * hours,
        scratch_shapes=[
            pltpu.VMEM((rows, LANES), WIDE),
            pltpu.VMEM((step * rows * stations, LANES), WIDE),
            pltpu.VMEM(spectra.shape, jnp.bfloat16),
            pltpu.SemaphoreType.DMA((chunks,)),
        ],
        compiler_params=limits(8),
        name="whiten",
    )(station_order, pair_blocks, band_weight, spectra)


def unit(first_row, windows, own_ref, other_ref, out_ref, wide):
    stations = own_ref.shape[1] // 2
    rows = pl.ds(first_row, windows)
    wide[...] = own_ref[rows].astype(WIDE)
    for first in range(0, stations, BLOCK):

        def body(w, sums):
            other = other_ref[first_row + w].astype(WIDE)
            re, im = other[:stations], other[stations:]
            new = []
            for k in range(BLOCK):
                a = first + k
                a_re = jnp.broadcast_to(wide[w, a : a + 1, :], re.shape)
                a_im = jnp.broadcast_to(wide[w, stations + a : stations + a + 1, :], re.shape)
                new.append(sums[2 * k] + (a_re * re + a_im * im))
                new.append(sums[2 * k + 1] + (a_re * im - a_im * re))
            return tuple(new)

        zero = jnp.zeros((stations, LANES), WIDE)
        sums = lax.fori_loop(0, windows, body, (zero,) * (2 * BLOCK), unroll=6)
        for k in range(BLOCK):
            out_ref[first + k, :stations] = sums[2 * k].astype(out_ref.dtype)
            out_ref[first + k, stations:] = sums[2 * k + 1].astype(out_ref.dtype)


def products(pair_blocks, own, other, windows, dtype):
    entries, height, _ = own.shape
    tiles, stations = (entries - 1) // windows, height // 2

    def body(pairs_ref, own_ref, other_ref, out_ref, wide, twin):
        me = lax.axis_index("sta")
        last = me == lax.axis_size("sta") - 1
        flags = other_ref[entries - 1].astype(WIDE)
        asked = jnp.logical_or(asks_itself(pairs_ref, me), jnp.max(flags) > 0.5)
        alone = jnp.logical_and(last, asked)

        @pl.when(jnp.logical_not(alone))
        def _():
            for tile in range(tiles):
                unit(tile * windows, windows, own_ref, other_ref, out_ref.at[tile], wide)

        @pl.when(alone)
        def _():
            column = lax.broadcasted_iota(jnp.int32, (stations, LANES), 0)
            for tile in range(tiles):
                for k, ref in enumerate((own_ref, other_ref)):
                    unit(tile * windows, windows, ref, ref, twin.at[k], wide)

                @pl.loop(0, stations)
                def _(a, tile=tile):
                    one, two = twin[0, a], twin[1, a]
                    re = jnp.where(column >= a, one[:stations], two[:stations])
                    im = jnp.where(column >= a, one[stations:], two[stations:])
                    im = jnp.where(column == a, two[:stations], im)
                    out_ref[tile, a, :stations] = re.astype(dtype)
                    out_ref[tile, a, stations:] = im.astype(dtype)

    flops = tiles * stations * stations * LANES * windows * 8
    return pl.pallas_call(
        body,
        in_specs=[SMEM, VMEM, VMEM],
        out_specs=VMEM,
        out_shape=jax.ShapeDtypeStruct((tiles, stations, height, LANES), dtype),
        scratch_shapes=[
            pltpu.VMEM((windows, height, LANES), WIDE),
            pltpu.VMEM((2, stations, height, LANES), WIDE),
        ],
        compiler_params=limits(4),
        cost_estimate=pl.CostEstimate(flops=flops, bytes_accessed=1 << 20, transcendentals=0),
        name="products",
    )(pair_blocks, own, other)


def turn(a, value, buf_ref):
    height = value.shape[0]
    stations = height // 2
    for part in range(2):
        rows = value[part * stations : (part + 1) * stations]
        buf_ref[pl.ds(part * stations + a, stations, stride=height), :] = -rows if part else rows


def add_hours(parts, scale):
    shape = parts[0].shape
    tiles, stations, height, _ = shape

    def body(*refs):
        part_refs, (mine_ref, turned_ref, buf) = refs[: len(parts)], refs[len(parts) :]
        for tile in range(tiles):
            for a in range(stations):
                total = part_refs[0][tile, a].astype(WIDE)
                for ref in part_refs[1:]:
                    total = total + ref[tile, a].astype(WIDE)
                total = total * scale
                mine_ref[tile, a] = total
                turn(a, total, buf.at[tile])
            for c in range(stations):
                rows = buf[tile, pl.ds(c * height, height), :]
                turned_ref[tile, c] = rows.astype(turned_ref.dtype)

    return pl.pallas_call(
        body,
        in_specs=[VMEM] * len(parts),
        out_specs=[VMEM] * 2,
        out_shape=[jax.ShapeDtypeStruct(shape, WIDE), jax.ShapeDtypeStruct(shape, jnp.bfloat16)],
        scratch_shapes=[pltpu.VMEM((tiles, stations * height, LANES), WIDE)],
        compiler_params=limits(4),
        name="add_hours",
    )(*parts)


def assemble(pair_blocks, mine, turned, other):
    tiles, stations, height, _ = mine.shape
    pairs = pair_blocks.shape[0]

    def body(pairs_ref, mine_ref, turned_ref, other_ref, out_ref, buf):
        me, count = lax.axis_index("sta"), lax.axis_size("sta")
        column = lax.broadcasted_iota(jnp.int32, (stations, LANES), 0)

        def put(p, a, tile, value):
            for part in range(2):
                rows = value[part * stations : (part + 1) * stations]
                out_ref[p, a, pl.ds(tile * 2 + part, stations, stride=2 * tiles), :] = rows

        def hermitian(p, a, tile, above, below, middle):
            re = jnp.where(column > a, above[:stations], below[:stations])
            im = jnp.where(column > a, above[stations:], below[stations:])
            re = jnp.where(column == a, middle, re)
            im = jnp.where(column == a, jnp.zeros_like(im), im)
            put(p, a, tile, jnp.concatenate([re, im], axis=0))

        for p in range(pairs):
            step = pairs_ref[p, 1] - me

            @pl.when(step == 1)
            def _(p=p):
                for tile in range(tiles):
                    for a in range(stations):
                        put(p, a, tile, mine_ref[tile, a])

            @pl.when(step == -1)
            def _(p=p):
                for tile in range(tiles):
                    for a in range(stations):
                        put(p, a, tile, other_ref[tile, a].astype(WIDE))

            @pl.when(jnp.logical_and(step == 0, me == count - 1))
            def _(p=p):
                for tile in range(tiles):
                    for a in range(stations):
                        own = mine_ref[tile, a]
                        back = turned_ref[tile, a].astype(WIDE)
                        hermitian(p, a, tile, own, back, own[:stations])

            @pl.when(jnp.logical_and(step == 0, me == 0))
            def _(p=p):
                for tile in range(tiles):
                    for a in range(stations):
                        turn(a, other_ref[tile, a].astype(WIDE), buf.at[tile])
                    for a in range(stations):
                        theirs = other_ref[tile, a].astype(WIDE)
                        back = buf[tile, pl.ds(a * height, height), :]
                        hermitian(p, a, tile, theirs, back, -theirs[stations:])

    rows = stations * tiles * 2
    return pl.pallas_call(
        body,
        in_specs=[SMEM, VMEM, VMEM, VMEM],
        out_specs=VMEM,
        out_shape=jax.ShapeDtypeStruct((pairs, stations, rows, LANES), WIDE),
        scratch_shapes=[pltpu.VMEM((tiles, stations * height, LANES), WIDE)],
        compiler_params=limits(4),
        name="assemble",
    )(pair_blocks, mine, turned, other)


def per_device(spectra, band_weight, station_order, pair_blocks):
    stations, _, windows, _, bins = spectra.shape
    tiles, pairs = bins // LANES, pair_blocks.shape[0]
    count, hours = lax.axis_size("sta"), lax.axis_size("hour")
    rows = spectra.reshape(stations, windows, 2, tiles, LANES)
    rows = rows.transpose(0, 1, 3, 2, 4).reshape(stations, windows, 2 * tiles, LANES)
    own = whiten(rows, band_weight.reshape(tiles, LANES), station_order, pair_blocks, hours)

    down = [((i + 1) % count, i) for i in range(count)]
    up = [(j, i) for i, j in down]
    order = [2, 1, 3, 0]
    other = {d: lax.ppermute(own[d], "sta", down) for d in order}
    parts = []
    for d in order:
        piece = products(pair_blocks, own[d], other[d], windows, jnp.bfloat16 if d else WIDE)
        if d:
            piece = lax.ppermute(piece, "hour", [(h, (h + d) % hours) for h in range(hours)])
        parts.append(piece)
    mine, turned = add_hours(parts, 1.0 / (hours * windows))
    theirs = lax.ppermute(turned, "sta", up)
    cross = assemble(pair_blocks, mine, turned, theirs)
    cross = cross.reshape(pairs, stations, stations, tiles // hours, 2, LANES)
    return cross.transpose(0, 1, 2, 4, 3, 5).reshape(pairs, stations, stations, 2, bins // hours)


def solution(mesh):
    return jax.shard_map(
        per_device,
        mesh=mesh,
        in_specs=(P("sta", "hour", None, None, None), P(), P("sta", None), P("sta", None)),
        out_specs=P("sta", None, None, None, "hour"),
        check_vma=False,
    )
```

time: 381 us -> 54.8 us (0.14)
  the two profiles are of different devices: /device:TPU:3 before, /device:TPU:0 now
where the time goes in v2:
time: 54.8 us; the launch traced here: 54.6 us
  waiting for transfers between devices  20.5 us (37%)
  Pallas kernels  17.6 us (32%)
  starting transfers between devices  12.8 us (23%)
  local copies, waits for them, and re-layouts  3.56 us (6%)
    pallas_call x4, Pallas kernels, products(): pl.pallas_call(body, in_specs=[SMEM, VMEM, VMEM], out_specs=VMEM, out_sha...  12.2 us
    ppermute x3, waiting for transfers between devices, per_device(): lax.ppermute(piece, 'hour', [(h, (h + d) % hours) for h in range(hours)])  8.46 us
    ppermute x3, starting transfers between devices, per_device(): lax.ppermute(piece, 'hour', [(h, (h + d) % hours) for h in range(hours)])  8.01 us
    ppermute x1, waiting for transfers between devices, per_device(): theirs = lax.ppermute(turned, 'sta', up)  6.66 us
    ppermute x4, waiting for transfers between devices, per_device(): other = {d: lax.ppermute(own[d], 'sta', down) for d in order}  5.41 us
    ppermute x4, starting transfers between devices, per_device(): other = {d: lax.ppermute(own[d], 'sta', down) for d in order}  4.71 us
    unnamed x8, local copies, waits for them, and re-layouts  3.56 us
    pallas_call x1, Pallas kernels, whiten(): pl.pallas_call(body, in_specs=[SMEM, SMEM, VMEM, pl.BlockSpec(memory_spac...  3.29 us
  transfers between devices with their start and end apart: 8, of which 5 were waited for; matrix products, arithmetic and copies ran while one was open for 0% of the time, Pallas kernels for 22%

profile of v2, /device:TPU:0, one launch (start us, length us, event | category | flops | bytes accessed | tf_op | source)
XLA Modules:
  0.0 54.6 jit_solution(15835313510944182554)
XLA Ops:
  0.0 0.0 copy-start
  0.0 1.5 %copy-done = bf16[16,1,30,2,1024]{4,3,2,1,0:T(2,128)(2,1)S(1)} copy-done((bf16[16,1,30,2,1024]{4,3,2,1,0:T(2,128)(2,1)S(1)}, bf16[16,1,30,2,1024]{4,3,2,1,0:T(2,128)(2,1)}, u32[]{:S(2)}) %copy-start) | copy-done | bytes 1966104
  1.5 0.0 copy-start.1
  1.5 0.7 %copy-done.1 = s32[2,2]{1,0:T(2,128)S(1)} copy-done((s32[2,2]{1,0:T(2,128)S(1)}, s32[2,2]{1,0:T(2,128)}, u32[]{:S(2)}) %copy-start.1) | copy-done | bytes 40
  2.2 0.0 copy-start.2
  2.2 0.7 %copy-done.2 = f32[1024]{0:T(1024)S(1)} copy-done((f32[1024]{0:T(1024)S(1)}, f32[1024]{0:T(1024)}, u32[]{:S(2)}) %copy-start.2) | copy-done | bytes 4120
  2.9 0.0 copy-start.3
  2.9 0.7 %copy-done.3 = s32[1,16]{1,0:T(1,128)S(1)} copy-done((s32[1,16]{1,0:T(1,128)S(1)}, s32[1,16]{1,0:T(1,128)}, u32[]{:S(2)}) %copy-start.3) | copy-done | bytes 88
  3.6 3.3 %whiten.1 = (bf16[61,32,128]{2,1,0:T(8,128)(2,1)S(1)}, bf16[61,32,128]{2,1,0:T(8,128)(2,1)S(1)}, bf16[61,32,128]{2,1,0:T(8,128)(2,1)S(1)}, bf16[61,32,128]{2,1,0:T(8,128)(2,1)S(1)}) custom-call(s32[1,16]{1,0:T(1,128)S(1)} %copy-done.3, s32[2,2]{1,0:T(2,128)S(1)} %copy-done.1, f32[8,128]{1,0:T(8,128)S(1)} %bitcast.12, bf16[16,30,16,128]{3,2,1,0:T(8,128)(2,1)S(1)} %bitcast.11), custom_call_target="tpu_custom_call" | custom-call | tf_op jit(solution)/shard_map/whiten/pallas_call | solution.py:79
  6.9 3.4 %collective-permute-start = (bf16[61,32,128]{2,1,0:T(8,128)(2,1)S(1)}, bf16[61,32,128]{2,1,0:T(8,128)(2,1)S(1)}, u32[]{:S(2)}, u32[]{:S(2)}) collective-permute-start(bf16[61,32,128]{2,1,0:T(8,128)(2,1)S(1)} %get-tuple-element.11.own_ref), channel_id=1, source_target_pairs={{4,0},{8,4},{12,8},{16,12},{20,16},{24,20},{28,24},{0,28},{5,1},{9... | collective-permute-start | bytes 1499144 | tf_op jit(solution)/shard_map/ppermute | solution.py:281
  10.2 0.7 %collective-permute-start.2 = (bf16[61,32,128]{2,1,0:T(8,128)(2,1)S(1)}, bf16[61,32,128]{2,1,0:T(8,128)(2,1)S(1)}, u32[]{:S(2)}, u32[]{:S(2)}) collective-permute-start(bf16[61,32,128]{2,1,0:T(8,128)(2,1)S(1)} %get-tuple-element.12.own_ref), channel_id=1, source_target_pairs={{4,0},{8,4},{12,8},{16,12},{20,16},{24,20},{28,24},{0,28},{5,1},{9... | collective-permute-start | bytes 1499144 | tf_op jit(solution)/shard_map/ppermute | solution.py:281
  10.9 0.1 collective-permute-start.4
  11.0 0.6 %collective-permute-start.6 = (bf16[61,32,128]{2,1,0:T(8,128)(2,1)S(1)}, bf16[61,32,128]{2,1,0:T(8,128)(2,1)S(1)}, u32[]{:S(2)}, u32[]{:S(2)}) collective-permute-start(bf16[61,32,128]{2,1,0:T(8,128)(2,1)S(1)} %get-tuple-element.14.own_ref), channel_id=1, source_target_pairs={{4,0},{8,4},{12,8},{16,12},{20,16},{24,20},{28,24},{0,28},{5,1},{9... | collective-permute-start | bytes 1499144 | tf_op jit(solution)/shard_map/ppermute | solution.py:281
  11.6 5.1 %collective-permute-done.other_ref = bf16[61,32,128]{2,1,0:T(8,128)(2,1)S(1)} collective-permute-done((bf16[61,32,128]{2,1,0:T(8,128)(2,1)S(1)}, bf16[61,32,128]{2,1,0:T(8,128)(2,1)S(1)}, u32[]{:S(2)}, u32[]{:S(2)}) %collective-permute-start) | collective-permute-done | bytes 499744 | tf_op jit(solution)/shard_map/ppermute | solution.py:281
  16.7 3.0 %products.4 = bf16[2,16,32,128]{3,2,1,0:T(8,128)(2,1)S(1)} custom-call(s32[2,2]{1,0:T(2,128)S(1)} %copy-done.1, bf16[61,32,128]{2,1,0:T(8,128)(2,1)S(1)} %get-tuple-element.11.own_ref, bf16[61,32,128]{2,1,0:T(8,128)(2,1)S(1)} %collective-permute-done.other_ref), custom_call_target="tpu_custom_call" | custom-call | flops 15728640 | bytes 1048576 | tf_op jit(solution)/shard_map/products/pallas_call | solution.py:153
  19.7 2.7 %collective-permute-start.1 = (bf16[2,16,32,128]{3,2,1,0:T(8,128)(2,1)S(1)}, bf16[2,16,32,128]{3,2,1,0:T(8,128)(2,1)S(1)}, u32[]{:S(2)}, u32[]{:S(2)}) collective-permute-start(bf16[2,16,32,128]{3,2,1,0:T(8,128)(2,1)S(1)} %products.4), channel_id=1, source_target_pairs={{0,2},{1,3},{2,0},{3,1},{4,6},{5,7},{6,4},{7,5},{8,10},{9,11},{10,... | collective-permute-start | bytes 786440 | tf_op jit(solution)/shard_map/ppermute | solution.py:286
  22.4 0.0 collective-permute-done.2.other_ref
  22.4 3.0 %products.5 = bf16[2,16,32,128]{3,2,1,0:T(8,128)(2,1)S(1)} custom-call(s32[2,2]{1,0:T(2,128)S(1)} %copy-done.1, bf16[61,32,128]{2,1,0:T(8,128)(2,1)S(1)} %get-tuple-element.12.own_ref, bf16[61,32,128]{2,1,0:T(8,128)(2,1)S(1)} %collective-permute-done.2.other_ref), custom_call_target="tpu_custom_call" | custom-call | flops 15728640 | bytes 1048576 | tf_op jit(solution)/shard_map/products/pallas_call | solution.py:153
  25.5 1.6 %collective-permute-start.3 = (bf16[2,16,32,128]{3,2,1,0:T(8,128)(2,1)S(1)}, bf16[2,16,32,128]{3,2,1,0:T(8,128)(2,1)S(1)}, u32[]{:S(2)}, u32[]{:S(2)}) collective-permute-start(bf16[2,16,32,128]{3,2,1,0:T(8,128)(2,1)S(1)} %products.5), channel_id=1, source_target_pairs={{0,1},{1,2},{2,3},{3,0},{4,5},{5,6},{6,7},{7,4},{8,9},{9,10},{10,1... | collective-permute-start | bytes 786440 | tf_op jit(solution)/shard_map/ppermute | solution.py:286
  27.1 0.3 collective-permute-done.4.other_ref
  27.4 3.0 %products.6 = bf16[2,16,32,128]{3,2,1,0:T(8,128)(2,1)S(1)} custom-call(s32[2,2]{1,0:T(2,128)S(1)} %copy-done.1, bf16[61,32,128]{2,1,0:T(8,128)(2,1)S(1)} %get-tuple-element.13.own_ref, bf16[61,32,128]{2,1,0:T(8,128)(2,1)S(1)} %collective-permute-done.4.other_ref), custom_call_target="tpu_custom_call" | custom-call | flops 15728640 | bytes 1048576 | tf_op jit(solution)/shard_map/products/pallas_call | solution.py:153
  30.4 3.7 %collective-permute-start.5 = (bf16[2,16,32,128]{3,2,1,0:T(8,128)(2,1)S(1)}, bf16[2,16,32,128]{3,2,1,0:T(8,128)(2,1)S(1)}, u32[]{:S(2)}, u32[]{:S(2)}) collective-permute-start(bf16[2,16,32,128]{3,2,1,0:T(8,128)(2,1)S(1)} %products.6), channel_id=1, source_target_pairs={{0,3},{1,0},{2,1},{3,2},{4,7},{5,4},{6,5},{7,6},{8,11},{9,8},{10,9... | collective-permute-start | bytes 786440 | tf_op jit(solution)/shard_map/ppermute | solution.py:286
  34.1 0.0 collective-permute-done.6.other_ref
  34.1 3.0 %products.7.refs_3_ = f32[2,16,32,128]{3,2,1,0:T(8,128)S(1)} custom-call(s32[2,2]{1,0:T(2,128)S(1)} %copy-done.1, bf16[61,32,128]{2,1,0:T(8,128)(2,1)S(1)} %get-tuple-element.14.own_ref, bf16[61,32,128]{2,1,0:T(8,128)(2,1)S(1)} %collective-permute-done.6.other_ref), custom_call_target="tpu_custom_call" | custom-call | flops 15728640 | bytes 1048576 | tf_op jit(solution)/shard_map/products/pallas_call | solution.py:153
  37.2 4.0 %collective-permute-done.1.refs_0_ = bf16[2,16,32,128]{3,2,1,0:T(8,128)(2,1)S(1)} collective-permute-done((bf16[2,16,32,128]{3,2,1,0:T(8,128)(2,1)S(1)}, bf16[2,16,32,128]{3,2,1,0:T(8,128)(2,1)S(1)}, u32[]{:S(2)}, u32[]{:S(2)}) %collective-permute-start.1) | collective-permute-done | bytes 262176 | tf_op jit(solution)/shard_map/ppermute | solution.py:286
  41.2 0.0 collective-permute-done.3.refs_1_
  41.2 4.5 %collective-permute-done.5.refs_2_ = bf16[2,16,32,128]{3,2,1,0:T(8,128)(2,1)S(1)} collective-permute-done((bf16[2,16,32,128]{3,2,1,0:T(8,128)(2,1)S(1)}, bf16[2,16,32,128]{3,2,1,0:T(8,128)(2,1)S(1)}, u32[]{:S(2)}, u32[]{:S(2)}) %collective-permute-start.5) | collective-permute-done | bytes 262176 | tf_op jit(solution)/shard_map/ppermute | solution.py:286
  45.6 0.5 add_hours.1
  46.2 0.1 collective-permute-start.7
  46.3 6.7 %collective-permute-done.7.other_ref = bf16[2,16,32,128]{3,2,1,0:T(8,128)(2,1)S(1)} collective-permute-done((bf16[2,16,32,128]{3,2,1,0:T(8,128)(2,1)S(1)}, bf16[2,16,32,128]{3,2,1,0:T(8,128)(2,1)S(1)}, u32[]{:S(2)}, u32[]{:S(2)}) %collective-permute-start.7) | collective-permute-done | bytes 262176 | tf_op jit(solution)/shard_map/ppermute | solution.py:289
  52.9 1.6 %assemble.1 = f32[2,16,64,128]{3,2,1,0:T(8,128)} custom-call(s32[2,2]{1,0:T(2,128)S(1)} %copy-done.1, f32[2,16,32,128]{3,2,1,0:T(8,128)S(1)} %get-tuple-element.15.mine_ref, bf16[2,16,32,128]{3,2,1,0:T(8,128)(2,1)S(1)} %get-tuple-element.16.turned_ref, bf16[2,16,32,128]{3,2,1,0:T(8,128)(2,1)S(1)} %collective-permute-done.7.other_ref), custom_call_target="tpu_custom_call" | custom-call | tf_op jit(solution)/shard_map/assemble/pallas_call | solution.py:259
Async XLA Ops:
  0.0 1.5 %copy-start = (bf16[16,1,30,2,1024]{4,3,2,1,0:T(2,128)(2,1)S(1)}, bf16[16,1,30,2,1024]{4,3,2,1,0:T(2,128)(2,1)}, u32[]{:S(2)}) copy-start(bf16[16,1,30,2,1024]{4,3,2,1,0:T(2,128)(2,1)} %param.4) | copy-start | bytes 5898244
  1.5 0.7 %copy-start.1 = (s32[2,2]{1,0:T(2,128)S(1)}, s32[2,2]{1,0:T(2,128)}, u32[]{:S(2)}) copy-start(s32[2,2]{1,0:T(2,128)} %pairs_ref.11) | copy-start | bytes 52
  2.2 0.7 %copy-start.2 = (f32[1024]{0:T(1024)S(1)}, f32[1024]{0:T(1024)}, u32[]{:S(2)}) copy-start(f32[1024]{0:T(1024)} %param.5) | copy-start | bytes 12292
  2.9 0.7 %copy-start.3 = (s32[1,16]{1,0:T(1,128)S(1)}, s32[1,16]{1,0:T(1,128)}, u32[]{:S(2)}) copy-start(s32[1,16]{1,0:T(1,128)} %order_ref.1) | copy-start | bytes 196
  6.9 9.8 %collective-permute-start = (bf16[61,32,128]{2,1,0:T(8,128)(2,1)S(1)}, bf16[61,32,128]{2,1,0:T(8,128)(2,1)S(1)}, u32[]{:S(2)}, u32[]{:S(2)}) collective-permute-start(bf16[61,32,128]{2,1,0:T(8,128)(2,1)S(1)} %get-tuple-element.11.own_ref), channel_id=1, source_target_pairs={{4,0},{8,4},{12,8},{16,12},{20,16},{24,20},{28,24},{0,28},{5,1},{9... | collective-permute-start | bytes 1499144 | tf_op jit(solution)/shard_map/ppermute | solution.py:281
  10.2 12.2 %collective-permute-start.2 = (bf16[61,32,128]{2,1,0:T(8,128)(2,1)S(1)}, bf16[61,32,128]{2,1,0:T(8,128)(2,1)S(1)}, u32[]{:S(2)}, u32[]{:S(2)}) collective-permute-start(bf16[61,32,128]{2,1,0:T(8,128)(2,1)S(1)} %get-tuple-element.12.own_ref), channel_id=1, source_target_pairs={{4,0},{8,4},{12,8},{16,12},{20,16},{24,20},{28,24},{0,28},{5,1},{9... | collective-permute-start | bytes 1499144 | tf_op jit(solution)/shard_map/ppermute | solution.py:281
  10.9 16.5 %collective-permute-start.4 = (bf16[61,32,128]{2,1,0:T(8,128)(2,1)S(1)}, bf16[61,32,128]{2,1,0:T(8,128)(2,1)S(1)}, u32[]{:S(2)}, u32[]{:S(2)}) collective-permute-start(bf16[61,32,128]{2,1,0:T(8,128)(2,1)S(1)} %get-tuple-element.13.own_ref), channel_id=1, source_target_pairs={{4,0},{8,4},{12,8},{16,12},{20,16},{24,20},{28,24},{0,28},{5,1},{9... | collective-permute-start | bytes 1499144 | tf_op jit(solution)/shard_map/ppermute | solution.py:281
  11.0 23.1 %collective-permute-start.6 = (bf16[61,32,128]{2,1,0:T(8,128)(2,1)S(1)}, bf16[61,32,128]{2,1,0:T(8,128)(2,1)S(1)}, u32[]{:S(2)}, u32[]{:S(2)}) collective-permute-start(bf16[61,32,128]{2,1,0:T(8,128)(2,1)S(1)} %get-tuple-element.14.own_ref), channel_id=1, source_target_pairs={{4,0},{8,4},{12,8},{16,12},{20,16},{24,20},{28,24},{0,28},{5,1},{9... | collective-permute-start | bytes 1499144 | tf_op jit(solution)/shard_map/ppermute | solution.py:281
  19.7 21.4 %collective-permute-start.1 = (bf16[2,16,32,128]{3,2,1,0:T(8,128)(2,1)S(1)}, bf16[2,16,32,128]{3,2,1,0:T(8,128)(2,1)S(1)}, u32[]{:S(2)}, u32[]{:S(2)}) collective-permute-start(bf16[2,16,32,128]{3,2,1,0:T(8,128)(2,1)S(1)} %products.4), channel_id=1, source_target_pairs={{0,2},{1,3},{2,0},{3,1},{4,6},{5,7},{6,4},{7,5},{8,10},{9,11},{10,... | collective-permute-start | bytes 786440 | tf_op jit(solution)/shard_map/ppermute | solution.py:286
  25.5 15.7 %collective-permute-start.3 = (bf16[2,16,32,128]{3,2,1,0:T(8,128)(2,1)S(1)}, bf16[2,16,32,128]{3,2,1,0:T(8,128)(2,1)S(1)}, u32[]{:S(2)}, u32[]{:S(2)}) collective-permute-start(bf16[2,16,32,128]{3,2,1,0:T(8,128)(2,1)S(1)} %products.5), channel_id=1, source_target_pairs={{0,1},{1,2},{2,3},{3,0},{4,5},{5,6},{6,7},{7,4},{8,9},{9,10},{10,1... | collective-permute-start | bytes 786440 | tf_op jit(solution)/shard_map/ppermute | solution.py:286
  30.4 15.2 %collective-permute-start.5 = (bf16[2,16,32,128]{3,2,1,0:T(8,128)(2,1)S(1)}, bf16[2,16,32,128]{3,2,1,0:T(8,128)(2,1)S(1)}, u32[]{:S(2)}, u32[]{:S(2)}) collective-permute-start(bf16[2,16,32,128]{3,2,1,0:T(8,128)(2,1)S(1)} %products.6), channel_id=1, source_target_pairs={{0,3},{1,0},{2,1},{3,2},{4,7},{5,4},{6,5},{7,6},{8,11},{9,8},{10,9... | collective-permute-start | bytes 786440 | tf_op jit(solution)/shard_map/ppermute | solution.py:286
  46.2 6.7 %collective-permute-start.7 = (bf16[2,16,32,128]{3,2,1,0:T(8,128)(2,1)S(1)}, bf16[2,16,32,128]{3,2,1,0:T(8,128)(2,1)S(1)}, u32[]{:S(2)}, u32[]{:S(2)}) collective-permute-start(bf16[2,16,32,128]{3,2,1,0:T(8,128)(2,1)S(1)} %get-tuple-element.16.turned_ref), channel_id=1, source_target_pairs={{0,4},{4,8},{8,12},{12,16},{16,20},{20,24},{24,28},{28,0},{1,5},{5... | collective-permute-start | bytes 786440 | tf_op jit(solution)/shard_map/ppermute | solution.py:289

commit v3 on v2

--- a/solution.py
+++ b/solution.py
@@ -8,6 +8,7 @@
 LANES = 128
 EPSILON = 1e-06
 BLOCK = 8
+PIECES = (((0, 2), (1, 2)), ((0, 1), (1, 1)), ((0, 3), (1, 3)), ((0, 0), (1, 0)))
 WIDE = jnp.float32
 SMEM = pl.BlockSpec(memory_space=pltpu.SMEM)
 VMEM = pl.BlockSpec(memory_space=pltpu.VMEM)
@@ -28,27 +29,38 @@
     stations, windows, rows, _ = spectra.shape
     tiles = rows // 2
     mine = tiles // hours
-    step = windows // 5
-    chunks = windows // step
+    chunks = 5
+    step = windows // chunks
     height = 2 * stations
 
-    def body(order_ref, pairs_ref, band_ref, x_hbm, *refs):
-        outs, (band, rowed, x_ref, sems) = refs[:hours], refs[hours:]
+    def body(order_hbm, pairs_hbm, band_hbm, x_hbm, *refs):
+        outs = refs[: len(PIECES)]
+        order_ref, pairs_ref, band_ref, band, rowed, x_ref, sems, small = refs[len(PIECES) :]
 
         def fetch(c):
             part = pl.ds(c * step, step)
             return pltpu.make_async_copy(x_hbm.at[:, part], x_ref.at[:, part], sems.at[c])
 
-        for c in range(chunks):
+        fetch(0).start()
+        copies = [
+            pltpu.make_async_copy(order_hbm, order_ref, small.at[0]),
+            pltpu.make_async_copy(pairs_hbm, pairs_ref, small.at[1]),
+            pltpu.make_async_copy(band_hbm, band_ref, small.at[2]),
+        ]
+        for copy in copies:
+            copy.start()
+        for c in range(1, chunks):
             fetch(c).start()
+        for copy in copies:
+            copy.wait()
         for part in range(2):
             band[pl.ds(part, tiles, stride=2), :] = band_ref[...]
         weight = band[...]
         here = lax.axis_index("hour")
         asked = asks_itself(pairs_ref, lax.axis_index("sta"))
         flag = jnp.where(asked, 1.0, 0.0)
-        for out in outs:
-            out[mine * windows] = jnp.full((height, LANES), flag, WIDE).astype(jnp.bfloat16)
+        for piece, out in zip(PIECES, outs):
+            out[len(piece) * windows] = jnp.full((height, LANES), flag, WIDE).astype(jnp.bfloat16)
 
         @pl.loop(0, chunks)
         def _(c):
@@ -67,35 +79,43 @@
                         factor = jnp.broadcast_to(scale[k : k + 1], (rows, LANES))
                         place = pl.ds(w * rows * stations + first + k, rows, stride=stations)
                         rowed[place, :] = x * factor * weight
-            for d in range(hours):
-                owner = lax.rem(here + d, hours)
-                for tile in range(mine):
+            for piece, out in zip(PIECES, outs):
+                for i, (tile, d) in enumerate(piece):
+                    owner = lax.rem(here + d, hours)
                     for w in range(step):
                         start = (w * tiles + owner * mine + tile) * height
                         white = rowed[pl.ds(pl.multiple_of(start, height), height), :]
-                        outs[d][tile * windows + c * step + w] = white.astype(jnp.bfloat16)
-
-    shape = (mine * windows + 1, height, LANES)
+                        out[i * windows + c * step + w] = white.astype(jnp.bfloat16)
+
+    hbm = pl.BlockSpec(memory_space=pltpu.HBM)
+    inputs = (station_order, pair_blocks, band_weight, spectra)
     return pl.pallas_call(
         body,
-        in_specs=[SMEM, SMEM, VMEM, pl.BlockSpec(memory_space=pltpu.HBM)],
-        out_specs=[VMEM] * hours,
-        out_shape=[jax.ShapeDtypeStruct(shape, jnp.bfloat16)] * hours,
+        in_specs=[hbm] * 4,
+        out_specs=[VMEM] * len(PIECES),
+        out_shape=[
+            jax.ShapeDtypeStruct((len(piece) * windows + 1, height, LANES), jnp.bfloat16)
+            for piece in PIECES
+        ],
         scratch_shapes=[
+            pltpu.SMEM(station_order.shape, jnp.int32),
+            pltpu.SMEM(pair_blocks.shape, jnp.int32),
+            pltpu.VMEM((tiles, LANES), WIDE),
             pltpu.VMEM((rows, LANES), WIDE),
             pltpu.VMEM((step * rows * stations, LANES), WIDE),
             pltpu.VMEM(spectra.shape, jnp.bfloat16),
             pltpu.SemaphoreType.DMA((chunks,)),
+            pltpu.SemaphoreType.DMA((3,)),
         ],
         compiler_params=limits(8),
         name="whiten",
-    )(station_order, pair_blocks, band_weight, spectra)
-
-
-def unit(first_row, windows, own_ref, other_ref, out_ref, wide):
+    )(*[pltpu.with_memory_space_constraint(value, pltpu.HBM) for value in inputs])
+
+
+def unit(first_row, own_ref, other_ref, out_ref, wide):
     stations = own_ref.shape[1] // 2
-    rows = pl.ds(first_row, windows)
-    wide[...] = own_ref[rows].astype(WIDE)
+    windows = wide.shape[0]
+    wide[...] = own_ref[pl.ds(first_row, windows)].astype(WIDE)
     for first in range(0, stations, BLOCK):
 
         def body(w, sums):
@@ -117,9 +137,10 @@
             out_ref[first + k, stations:] = sums[2 * k + 1].astype(out_ref.dtype)
 
 
-def products(pair_blocks, own, other, windows, dtype):
+def products(pair_blocks, own, other, windows, place, dtype):
     entries, height, _ = own.shape
-    tiles, stations = (entries - 1) // windows, height // 2
+    stations = height // 2
+    row = place * windows
 
     def body(pairs_ref, own_ref, other_ref, out_ref, wide, twin):
         me = lax.axis_index("sta")
@@ -130,37 +151,35 @@
 
         @pl.when(jnp.logical_not(alone))
         def _():
-            for tile in range(tiles):
-                unit(tile * windows, windows, own_ref, other_ref, out_ref.at[tile], wide)
+            unit(row, own_ref, other_ref, out_ref, wide)
 
         @pl.when(alone)
         def _():
             column = lax.broadcasted_iota(jnp.int32, (stations, LANES), 0)
-            for tile in range(tiles):
-                for k, ref in enumerate((own_ref, other_ref)):
-                    unit(tile * windows, windows, ref, ref, twin.at[k], wide)
-
-                @pl.loop(0, stations)
-                def _(a, tile=tile):
-                    one, two = twin[0, a], twin[1, a]
-                    re = jnp.where(column >= a, one[:stations], two[:stations])
-                    im = jnp.where(column >= a, one[stations:], two[stations:])
-                    im = jnp.where(column == a, two[:stations], im)
-                    out_ref[tile, a, :stations] = re.astype(dtype)
-                    out_ref[tile, a, stations:] = im.astype(dtype)
-
-    flops = tiles * stations * stations * LANES * windows * 8
+            for k, ref in enumerate((own_ref, other_ref)):
+                unit(row, ref, ref, twin.at[k], wide)
+
+            @pl.loop(0, stations)
+            def _(a):
+                one, two = twin[0, a], twin[1, a]
+                re = jnp.where(column >= a, one[:stations], two[:stations])
+                im = jnp.where(column >= a, one[stations:], two[stations:])
+                im = jnp.where(column == a, two[:stations], im)
+                out_ref[a, :stations] = re.astype(dtype)
+                out_ref[a, stations:] = im.astype(dtype)
+
+    flops = stations * stations * LANES * windows * 8
     return pl.pallas_call(
         body,
         in_specs=[SMEM, VMEM, VMEM],
         out_specs=VMEM,
-        out_shape=jax.ShapeDtypeStruct((tiles, stations, height, LANES), dtype),
+        out_shape=jax.ShapeDtypeStruct((stations, height, LANES), dtype),
         scratch_shapes=[
             pltpu.VMEM((windows, height, LANES), WIDE),
             pltpu.VMEM((2, stations, height, LANES), WIDE),
         ],
         compiler_params=limits(4),
-        cost_estimate=pl.CostEstimate(flops=flops, bytes_accessed=1 << 20, transcendentals=0),
+        cost_estimate=pl.CostEstimate(flops=flops, bytes_accessed=1 << 19, transcendentals=0),
         name="products",
     )(pair_blocks, own, other)
 
@@ -173,17 +192,18 @@
         buf_ref[pl.ds(part * stations + a, stations, stride=height), :] = -rows if part else rows
 
 
-def add_hours(parts, scale):
-    shape = parts[0].shape
-    tiles, stations, height, _ = shape
+def add_hours(parts, owned, tiles, scale):
+    stations, height, _ = parts[0].shape
+    shape = (tiles, stations, height, LANES)
 
     def body(*refs):
         part_refs, (mine_ref, turned_ref, buf) = refs[: len(parts)], refs[len(parts) :]
         for tile in range(tiles):
+            terms = [ref for ref, t in zip(part_refs, owned) if t == tile]
             for a in range(stations):
-                total = part_refs[0][tile, a].astype(WIDE)
-                for ref in part_refs[1:]:
-                    total = total + ref[tile, a].astype(WIDE)
+                total = terms[0][a].astype(WIDE)
+                for ref in terms[1:]:
+                    total = total + ref[a].astype(WIDE)
                 total = total * scale
                 mine_ref[tile, a] = total
                 turn(a, total, buf.at[tile])
@@ -277,15 +297,16 @@
 
     down = [((i + 1) % count, i) for i in range(count)]
     up = [(j, i) for i, j in down]
-    order = [2, 1, 3, 0]
-    other = {d: lax.ppermute(own[d], "sta", down) for d in order}
-    parts = []
-    for d in order:
-        piece = products(pair_blocks, own[d], other[d], windows, jnp.bfloat16 if d else WIDE)
-        if d:
-            piece = lax.ppermute(piece, "hour", [(h, (h + d) % hours) for h in range(hours)])
-        parts.append(piece)
-    mine, turned = add_hours(parts, 1.0 / (hours * windows))
+    other = [lax.ppermute(piece, "sta", down) for piece in own]
+    parts, owned = [], []
+    for piece, mine, theirs in zip(PIECES, own, other):
+        for place, (tile, d) in enumerate(piece):
+            part = products(pair_blocks, mine, theirs, windows, place, jnp.bfloat16 if d else WIDE)
+            if d:
+                part = lax.ppermute(part, "hour", [(h, (h + d) % hours) for h in range(hours)])
+            parts.append(part)
+            owned.append(tile)
+    mine, turned = add_hours(parts, owned, tiles // hours, 1.0 / (hours * windows))
     theirs = lax.ppermute(turned, "sta", up)
     cross = assemble(pair_blocks, mine, turned, theirs)
     cross = cross.reshape(pairs, stations, stations, tiles // hours, 2, LANES)

time: 54.8 us -> 50.5 us (0.922)
  waiting for transfers between devices: 20.5 us -> 16 us
  local copies, waits for them, and re-layouts: 3.56 us -> 0.01 us
  Pallas kernels: 17.6 us -> 20.8 us
  starting transfers between devices: 12.8 us -> 13.4 us
    ppermute x7 -> x10, waiting for transfers between devices: 13.9 us -> 9.28 us  [the longest x4 5.12 us: per_device(): other = [lax.ppermute(piece, 'sta', down) for piece in own]]
    unnamed x8 -> x2, local copies, waits for them, and re-layouts: 3.56 us -> 0.01 us
    pallas_call x4 -> x8, Pallas kernels: 12.2 us -> 14.9 us  [products(): pl.pallas_call(body, in_specs=[SMEM, VMEM, VMEM], out_specs=VMEM, out_sha...]
    ppermute x7 -> x10, starting transfers between devices: 12.7 us -> 13.3 us  [the longest x6 8.63 us: per_device(): lax.ppermute(part, 'hour', [(h, (h + d) % hours) for h in range(hours)])]
  transfers between devices with their start and end apart: 8 -> 11, of which waited for: 5 -> 5; matrix products, arithmetic and copies ran while one was open for 0% -> 0% of each run, Pallas kernels for 22% -> 30%
where the time goes in v3:
time: 50.5 us; the launch traced here: 50.3 us
  Pallas kernels  20.8 us (41%)
  waiting for transfers between devices  16 us (32%)
  starting transfers between devices  13.4 us (27%)
    pallas_call x8, Pallas kernels, products(): pl.pallas_call(body, in_specs=[SMEM, VMEM, VMEM], out_specs=VMEM, out_sha...  14.9 us
    ppermute x6, starting transfers between devices, per_device(): lax.ppermute(part, 'hour', [(h, (h + d) % hours) for h in range(hours)])  8.63 us
    ppermute x1, waiting for transfers between devices, per_device(): theirs = lax.ppermute(turned, 'sta', up)  6.68 us
    ppermute x4, waiting for transfers between devices, per_device(): other = [lax.ppermute(piece, 'sta', down) for piece in own]  5.12 us
    ppermute x4, starting transfers between devices, per_device(): other = [lax.ppermute(piece, 'sta', down) for piece in own]  4.71 us
    ppermute x6, waiting for transfers between devices, per_device(): lax.ppermute(part, 'hour', [(h, (h + d) % hours) for h in range(hours)])  4.16 us
    pallas_call x1, Pallas kernels, whiten(): pl.pallas_call(body, in_specs=[hbm] * 4, out_specs=[VMEM] * len(PIECES),...  3.8 us
    pallas_call x1, Pallas kernels, assemble(): pl.pallas_call(body, in_specs=[SMEM, VMEM, VMEM, VMEM], out_specs=VMEM, o...  1.63 us
  transfers between devices with their start and end apart: 11, of which 5 were waited for; matrix products, arithmetic and copies ran while one was open for 0% of the time, Pallas kernels for 30%

profile of v3, /device:TPU:0, one launch (start us, length us, event | category | flops | bytes accessed | tf_op | source)
XLA Modules:
  0.0 50.3 jit_solution(12778628592064607117)
XLA Ops:
  0.0 0.0 copy-start
  0.0 3.8 %whiten.1 = (bf16[61,32,128]{2,1,0:T(8,128)(2,1)S(1)}, bf16[61,32,128]{2,1,0:T(8,128)(2,1)S(1)}, bf16[61,32,128]{2,1,0:T(8,128)(2,1)S(1)}, bf16[61,32,128]{2,1,0:T(8,128)(2,1)S(1)}) custom-call(s32[1,16]{1,0:T(1,128)} %order_hbm.1, s32[2,2]{1,0:T(2,128)} %pairs_ref.17, f32[8,128]{1,0:T(8,128)} %bitcast.12, bf16[16,30,16,128]{3,2,1,0:T(8,128)(2,1)} %bitcast.11), custom_call_target="tpu_custom_call" | custom-call | tf_op jit(solution)/shard_map/whiten/pallas_call | solution.py:92
  3.8 3.4 %collective-permute-start = (bf16[61,32,128]{2,1,0:T(8,128)(2,1)S(1)}, bf16[61,32,128]{2,1,0:T(8,128)(2,1)S(1)}, u32[]{:S(2)}, u32[]{:S(2)}) collective-permute-start(bf16[61,32,128]{2,1,0:T(8,128)(2,1)S(1)} %get-tuple-element.11.own_ref), channel_id=1, source_target_pairs={{4,0},{8,4},{12,8},{16,12},{20,16},{24,20},{28,24},{0,28},{5,1},{9... | collective-permute-start | bytes 1499144 | tf_op jit(solution)/shard_map/ppermute | solution.py:300
  7.2 0.7 %collective-permute-start.3 = (bf16[61,32,128]{2,1,0:T(8,128)(2,1)S(1)}, bf16[61,32,128]{2,1,0:T(8,128)(2,1)S(1)}, u32[]{:S(2)}, u32[]{:S(2)}) collective-permute-start(bf16[61,32,128]{2,1,0:T(8,128)(2,1)S(1)} %get-tuple-element.12.own_ref), channel_id=1, source_target_pairs={{4,0},{8,4},{12,8},{16,12},{20,16},{24,20},{28,24},{0,28},{5,1},{9... | collective-permute-start | bytes 1499144 | tf_op jit(solution)/shard_map/ppermute | solution.py:300
  7.9 0.1 collective-permute-start.6
  7.9 0.6 %collective-permute-start.9 = (bf16[61,32,128]{2,1,0:T(8,128)(2,1)S(1)}, bf16[61,32,128]{2,1,0:T(8,128)(2,1)S(1)}, u32[]{:S(2)}, u32[]{:S(2)}) collective-permute-start(bf16[61,32,128]{2,1,0:T(8,128)(2,1)S(1)} %get-tuple-element.14.own_ref), channel_id=1, source_target_pairs={{4,0},{8,4},{12,8},{16,12},{20,16},{24,20},{28,24},{0,28},{5,1},{9... | collective-permute-start | bytes 1499144 | tf_op jit(solution)/shard_map/ppermute | solution.py:300
  8.5 5.1 %collective-permute-done.other_ref = bf16[61,32,128]{2,1,0:T(8,128)(2,1)S(1)} collective-permute-done((bf16[61,32,128]{2,1,0:T(8,128)(2,1)S(1)}, bf16[61,32,128]{2,1,0:T(8,128)(2,1)S(1)}, u32[]{:S(2)}, u32[]{:S(2)}) %collective-permute-start) | collective-permute-done | bytes 499744 | tf_op jit(solution)/shard_map/ppermute | solution.py:300
  13.6 0.0 copy-done
  13.6 1.9 %products.8 = bf16[16,32,128]{2,1,0:T(8,128)(2,1)S(1)} custom-call(s32[2,2]{1,0:T(2,128)S(1)} %copy-done, bf16[61,32,128]{2,1,0:T(8,128)(2,1)S(1)} %get-tuple-element.11.own_ref, bf16[61,32,128]{2,1,0:T(8,128)(2,1)S(1)} %collective-permute-done.other_ref), custom_call_target="tpu_custom_call" | custom-call | flops 7864320 | bytes 524288 | tf_op jit(solution)/shard_map/products/pallas_call | solution.py:172
  15.5 2.7 %collective-permute-start.1 = (bf16[16,32,128]{2,1,0:T(8,128)(2,1)S(1)}, bf16[16,32,128]{2,1,0:T(8,128)(2,1)S(1)}, u32[]{:S(2)}, u32[]{:S(2)}) collective-permute-start(bf16[16,32,128]{2,1,0:T(8,128)(2,1)S(1)} %products.8), channel_id=1, source_target_pairs={{0,2},{1,3},{2,0},{3,1},{4,6},{5,7},{6,4},{7,5},{8,10},{9,11},{10,... | collective-permute-start | bytes 393224 | tf_op jit(solution)/shard_map/ppermute | solution.py:306
  18.2 1.9 %products.9 = bf16[16,32,128]{2,1,0:T(8,128)(2,1)S(1)} custom-call(s32[2,2]{1,0:T(2,128)S(1)} %copy-done, bf16[61,32,128]{2,1,0:T(8,128)(2,1)S(1)} %get-tuple-element.11.own_ref, bf16[61,32,128]{2,1,0:T(8,128)(2,1)S(1)} %collective-permute-done.other_ref), custom_call_target="tpu_custom_call" | custom-call | flops 7864320 | bytes 524288 | tf_op jit(solution)/shard_map/products/pallas_call | solution.py:172
  20.0 0.4 collective-permute-start.2
  20.4 0.0 collective-permute-done.3.other_ref
  20.4 1.9 %products.10 = bf16[16,32,128]{2,1,0:T(8,128)(2,1)S(1)} custom-call(s32[2,2]{1,0:T(2,128)S(1)} %copy-done, bf16[61,32,128]{2,1,0:T(8,128)(2,1)S(1)} %get-tuple-element.12.own_ref, bf16[61,32,128]{2,1,0:T(8,128)(2,1)S(1)} %collective-permute-done.3.other_ref), custom_call_target="tpu_custom_call" | custom-call | flops 7864320 | bytes 524288 | tf_op jit(solution)/shard_map/products/pallas_call | solution.py:172
  22.3 1.6 %collective-permute-start.4 = (bf16[16,32,128]{2,1,0:T(8,128)(2,1)S(1)}, bf16[16,32,128]{2,1,0:T(8,128)(2,1)S(1)}, u32[]{:S(2)}, u32[]{:S(2)}) collective-permute-start(bf16[16,32,128]{2,1,0:T(8,128)(2,1)S(1)} %products.10), channel_id=1, source_target_pairs={{0,1},{1,2},{2,3},{3,0},{4,5},{5,6},{6,7},{7,4},{8,9},{9,10},{10,1... | collective-permute-start | bytes 393224 | tf_op jit(solution)/shard_map/ppermute | solution.py:306
  23.9 1.9 %products.11 = bf16[16,32,128]{2,1,0:T(8,128)(2,1)S(1)} custom-call(s32[2,2]{1,0:T(2,128)S(1)} %copy-done, bf16[61,32,128]{2,1,0:T(8,128)(2,1)S(1)} %get-tuple-element.12.own_ref, bf16[61,32,128]{2,1,0:T(8,128)(2,1)S(1)} %collective-permute-done.3.other_ref), custom_call_target="tpu_custom_call" | custom-call | flops 7864320 | bytes 524288 | tf_op jit(solution)/shard_map/products/pallas_call | solution.py:172
  25.8 0.0 collective-permute-done.6.other_ref
  25.8 1.6 %collective-permute-start.5 = (bf16[16,32,128]{2,1,0:T(8,128)(2,1)S(1)}, bf16[16,32,128]{2,1,0:T(8,128)(2,1)S(1)}, u32[]{:S(2)}, u32[]{:S(2)}) collective-permute-start(bf16[16,32,128]{2,1,0:T(8,128)(2,1)S(1)} %products.11), channel_id=1, source_target_pairs={{0,1},{1,2},{2,3},{3,0},{4,5},{5,6},{6,7},{7,4},{8,9},{9,10},{10,1... | collective-permute-start | bytes 393224 | tf_op jit(solution)/shard_map/ppermute | solution.py:306
  27.4 1.9 %products.13 = bf16[16,32,128]{2,1,0:T(8,128)(2,1)S(1)} custom-call(s32[2,2]{1,0:T(2,128)S(1)} %copy-done, bf16[61,32,128]{2,1,0:T(8,128)(2,1)S(1)} %get-tuple-element.13.own_ref, bf16[61,32,128]{2,1,0:T(8,128)(2,1)S(1)} %collective-permute-done.6.other_ref), custom_call_target="tpu_custom_call" | custom-call | flops 7864320 | bytes 524288 | tf_op jit(solution)/shard_map/products/pallas_call | solution.py:172
  29.3 1.9 %products.12 = bf16[16,32,128]{2,1,0:T(8,128)(2,1)S(1)} custom-call(s32[2,2]{1,0:T(2,128)S(1)} %copy-done, bf16[61,32,128]{2,1,0:T(8,128)(2,1)S(1)} %get-tuple-element.13.own_ref, bf16[61,32,128]{2,1,0:T(8,128)(2,1)S(1)} %collective-permute-done.6.other_ref), custom_call_target="tpu_custom_call" | custom-call | flops 7864320 | bytes 524288 | tf_op jit(solution)/shard_map/products/pallas_call | solution.py:172
  31.2 0.0 collective-permute-done.9.other_ref
  31.2 2.3 %collective-permute-start.7 = (bf16[16,32,128]{2,1,0:T(8,128)(2,1)S(1)}, bf16[16,32,128]{2,1,0:T(8,128)(2,1)S(1)}, u32[]{:S(2)}, u32[]{:S(2)}) collective-permute-start(bf16[16,32,128]{2,1,0:T(8,128)(2,1)S(1)} %products.12), channel_id=1, source_target_pairs={{0,3},{1,0},{2,1},{3,2},{4,7},{5,4},{6,5},{7,6},{8,11},{9,8},{10,9... | collective-permute-start | bytes 393224 | tf_op jit(solution)/shard_map/ppermute | solution.py:306
  33.5 0.7 %collective-permute-done.1.refs_0_ = bf16[16,32,128]{2,1,0:T(8,128)(2,1)S(1)} collective-permute-done((bf16[16,32,128]{2,1,0:T(8,128)(2,1)S(1)}, bf16[16,32,128]{2,1,0:T(8,128)(2,1)S(1)}, u32[]{:S(2)}, u32[]{:S(2)}) %collective-permute-start.1) | collective-permute-done | bytes 131104 | tf_op jit(solution)/shard_map/ppermute | solution.py:306
  34.2 0.0 collective-permute-start.8
  34.2 1.9 %products.15.refs_7_ = f32[16,32,128]{2,1,0:T(8,128)S(1)} custom-call(s32[2,2]{1,0:T(2,128)S(1)} %copy-done, bf16[61,32,128]{2,1,0:T(8,128)(2,1)S(1)} %get-tuple-element.14.own_ref, bf16[61,32,128]{2,1,0:T(8,128)(2,1)S(1)} %collective-permute-done.9.other_ref), custom_call_target="tpu_custom_call" | custom-call | flops 7864320 | bytes 524288 | tf_op jit(solution)/shard_map/products/pallas_call | solution.py:172
  36.0 1.9 %products.14.refs_6_ = f32[16,32,128]{2,1,0:T(8,128)S(1)} custom-call(s32[2,2]{1,0:T(2,128)S(1)} %copy-done, bf16[61,32,128]{2,1,0:T(8,128)(2,1)S(1)} %get-tuple-element.14.own_ref, bf16[61,32,128]{2,1,0:T(8,128)(2,1)S(1)} %collective-permute-done.9.other_ref), custom_call_target="tpu_custom_call" | custom-call | flops 7864320 | bytes 524288 | tf_op jit(solution)/shard_map/products/pallas_call | solution.py:172
  37.9 0.0 collective-permute-done.2.refs_1_
  37.9 0.0 collective-permute-done.4.refs_2_
  37.9 0.0 collective-permute-done.5.refs_3_
  37.9 0.8 %collective-permute-done.7.refs_4_ = bf16[16,32,128]{2,1,0:T(8,128)(2,1)S(1)} collective-permute-done((bf16[16,32,128]{2,1,0:T(8,128)(2,1)S(1)}, bf16[16,32,128]{2,1,0:T(8,128)(2,1)S(1)}, u32[]{:S(2)}, u32[]{:S(2)}) %collective-permute-start.7) | collective-permute-done | bytes 131104 | tf_op jit(solution)/shard_map/ppermute | solution.py:306
  38.7 2.7 %collective-permute-done.8.refs_5_ = bf16[16,32,128]{2,1,0:T(8,128)(2,1)S(1)} collective-permute-done((bf16[16,32,128]{2,1,0:T(8,128)(2,1)S(1)}, bf16[16,32,128]{2,1,0:T(8,128)(2,1)S(1)}, u32[]{:S(2)}, u32[]{:S(2)}) %collective-permute-start.8) | collective-permute-done | bytes 131104 | tf_op jit(solution)/shard_map/ppermute | solution.py:306
  41.4 0.5 %add_hours.1 = (f32[2,16,32,128]{3,2,1,0:T(8,128)S(1)}, bf16[2,16,32,128]{3,2,1,0:T(8,128)(2,1)S(1)}) custom-call(bf16[16,32,128]{2,1,0:T(8,128)(2,1)S(1)} %collective-permute-done.1.refs_0_, bf16[16,32,128]{2,1,0:T(8,128)(2,1)S(1)} %collective-permute-done.2.refs_1_, bf16[16,32,128]{2,1,0:T(8,128)(2,1)S(1)} %collective-permute-done.4.refs_2_, ...), custom_call_target="tpu_custom_call" | custom-call | tf_op jit(solution)/shard_map/add_hours/pallas_call | solution.py:214
  42.0 0.1 collective-permute-start.10
  42.0 6.7 %collective-permute-done.10.other_ref = bf16[2,16,32,128]{3,2,1,0:T(8,128)(2,1)S(1)} collective-permute-done((bf16[2,16,32,128]{3,2,1,0:T(8,128)(2,1)S(1)}, bf16[2,16,32,128]{3,2,1,0:T(8,128)(2,1)S(1)}, u32[]{:S(2)}, u32[]{:S(2)}) %collective-permute-start.10) | collective-permute-done | bytes 262176 | tf_op jit(solution)/shard_map/ppermute | solution.py:310
  48.7 1.6 %assemble.1 = f32[2,16,64,128]{3,2,1,0:T(8,128)} custom-call(s32[2,2]{1,0:T(2,128)S(1)} %copy-done, f32[2,16,32,128]{3,2,1,0:T(8,128)S(1)} %get-tuple-element.15.mine_ref, bf16[2,16,32,128]{3,2,1,0:T(8,128)(2,1)S(1)} %get-tuple-element.16.turned_ref, bf16[2,16,32,128]{3,2,1,0:T(8,128)(2,1)S(1)} %collective-permute-done.10.other_ref), custom_call_target="tpu_custom_call" | custom-call | tf_op jit(solution)/shard_map/assemble/pallas_call | solution.py:279
Async XLA Ops:
  0.0 13.6 %copy-start = (s32[2,2]{1,0:T(2,128)S(1)}, s32[2,2]{1,0:T(2,128)}, u32[]{:S(2)}) copy-start(s32[2,2]{1,0:T(2,128)} %pairs_ref.17) | copy-start | bytes 52
  3.8 9.8 %collective-permute-start = (bf16[61,32,128]{2,1,0:T(8,128)(2,1)S(1)}, bf16[61,32,128]{2,1,0:T(8,128)(2,1)S(1)}, u32[]{:S(2)}, u32[]{:S(2)}) collective-permute-start(bf16[61,32,128]{2,1,0:T(8,128)(2,1)S(1)} %get-tuple-element.11.own_ref), channel_id=1, source_target_pairs={{4,0},{8,4},{12,8},{16,12},{20,16},{24,20},{28,24},{0,28},{5,1},{9... | collective-permute-start | bytes 1499144 | tf_op jit(solution)/shard_map/ppermute | solution.py:300
  7.2 13.2 %collective-permute-start.3 = (bf16[61,32,128]{2,1,0:T(8,128)(2,1)S(1)}, bf16[61,32,128]{2,1,0:T(8,128)(2,1)S(1)}, u32[]{:S(2)}, u32[]{:S(2)}) collective-permute-start(bf16[61,32,128]{2,1,0:T(8,128)(2,1)S(1)} %get-tuple-element.12.own_ref), channel_id=1, source_target_pairs={{4,0},{8,4},{12,8},{16,12},{20,16},{24,20},{28,24},{0,28},{5,1},{9... | collective-permute-start | bytes 1499144 | tf_op jit(solution)/shard_map/ppermute | solution.py:300
  7.9 17.9 %collective-permute-start.6 = (bf16[61,32,128]{2,1,0:T(8,128)(2,1)S(1)}, bf16[61,32,128]{2,1,0:T(8,128)(2,1)S(1)}, u32[]{:S(2)}, u32[]{:S(2)}) collective-permute-start(bf16[61,32,128]{2,1,0:T(8,128)(2,1)S(1)} %get-tuple-element.13.own_ref), channel_id=1, source_target_pairs={{4,0},{8,4},{12,8},{16,12},{20,16},{24,20},{28,24},{0,28},{5,1},{9... | collective-permute-start | bytes 1499144 | tf_op jit(solution)/shard_map/ppermute | solution.py:300
  7.9 23.2 %collective-permute-start.9 = (bf16[61,32,128]{2,1,0:T(8,128)(2,1)S(1)}, bf16[61,32,128]{2,1,0:T(8,128)(2,1)S(1)}, u32[]{:S(2)}, u32[]{:S(2)}) collective-permute-start(bf16[61,32,128]{2,1,0:T(8,128)(2,1)S(1)} %get-tuple-element.14.own_ref), channel_id=1, source_target_pairs={{4,0},{8,4},{12,8},{16,12},{20,16},{24,20},{28,24},{0,28},{5,1},{9... | collective-permute-start | bytes 1499144 | tf_op jit(solution)/shard_map/ppermute | solution.py:300
  15.5 18.7 %collective-permute-start.1 = (bf16[16,32,128]{2,1,0:T(8,128)(2,1)S(1)}, bf16[16,32,128]{2,1,0:T(8,128)(2,1)S(1)}, u32[]{:S(2)}, u32[]{:S(2)}) collective-permute-start(bf16[16,32,128]{2,1,0:T(8,128)(2,1)S(1)} %products.8), channel_id=1, source_target_pairs={{0,2},{1,3},{2,0},{3,1},{4,6},{5,7},{6,4},{7,5},{8,10},{9,11},{10,... | collective-permute-start | bytes 393224 | tf_op jit(solution)/shard_map/ppermute | solution.py:306
  20.0 17.9 %collective-permute-start.2 = (bf16[16,32,128]{2,1,0:T(8,128)(2,1)S(1)}, bf16[16,32,128]{2,1,0:T(8,128)(2,1)S(1)}, u32[]{:S(2)}, u32[]{:S(2)}) collective-permute-start(bf16[16,32,128]{2,1,0:T(8,128)(2,1)S(1)} %products.9), channel_id=1, source_target_pairs={{0,2},{1,3},{2,0},{3,1},{4,6},{5,7},{6,4},{7,5},{8,10},{9,11},{10,... | collective-permute-start | bytes 393224 | tf_op jit(solution)/shard_map/ppermute | solution.py:306
  22.3 15.6 %collective-permute-start.4 = (bf16[16,32,128]{2,1,0:T(8,128)(2,1)S(1)}, bf16[16,32,128]{2,1,0:T(8,128)(2,1)S(1)}, u32[]{:S(2)}, u32[]{:S(2)}) collective-permute-start(bf16[16,32,128]{2,1,0:T(8,128)(2,1)S(1)} %products.10), channel_id=1, source_target_pairs={{0,1},{1,2},{2,3},{3,0},{4,5},{5,6},{6,7},{7,4},{8,9},{9,10},{10,1... | collective-permute-start | bytes 393224 | tf_op jit(solution)/shard_map/ppermute | solution.py:306
  25.8 12.1 %collective-permute-start.5 = (bf16[16,32,128]{2,1,0:T(8,128)(2,1)S(1)}, bf16[16,32,128]{2,1,0:T(8,128)(2,1)S(1)}, u32[]{:S(2)}, u32[]{:S(2)}) collective-permute-start(bf16[16,32,128]{2,1,0:T(8,128)(2,1)S(1)} %products.11), channel_id=1, source_target_pairs={{0,1},{1,2},{2,3},{3,0},{4,5},{5,6},{6,7},{7,4},{8,9},{9,10},{10,1... | collective-permute-start | bytes 393224 | tf_op jit(solution)/shard_map/ppermute | solution.py:306
  31.2 7.5 %collective-permute-start.7 = (bf16[16,32,128]{2,1,0:T(8,128)(2,1)S(1)}, bf16[16,32,128]{2,1,0:T(8,128)(2,1)S(1)}, u32[]{:S(2)}, u32[]{:S(2)}) collective-permute-start(bf16[16,32,128]{2,1,0:T(8,128)(2,1)S(1)} %products.12), channel_id=1, source_target_pairs={{0,3},{1,0},{2,1},{3,2},{4,7},{5,4},{6,5},{7,6},{8,11},{9,8},{10,9... | collective-permute-start | bytes 393224 | tf_op jit(solution)/shard_map/ppermute | solution.py:306
  34.2 7.2 %collective-permute-start.8 = (bf16[16,32,128]{2,1,0:T(8,128)(2,1)S(1)}, bf16[16,32,128]{2,1,0:T(8,128)(2,1)S(1)}, u32[]{:S(2)}, u32[]{:S(2)}) collective-permute-start(bf16[16,32,128]{2,1,0:T(8,128)(2,1)S(1)} %products.13), channel_id=1, source_target_pairs={{0,3},{1,0},{2,1},{3,2},{4,7},{5,4},{6,5},{7,6},{8,11},{9,8},{10,9... | collective-permute-start | bytes 393224 | tf_op jit(solution)/shard_map/ppermute | solution.py:306
  42.0 6.7 %collective-permute-start.10 = (bf16[2,16,32,128]{3,2,1,0:T(8,128)(2,1)S(1)}, bf16[2,16,32,128]{3,2,1,0:T(8,128)(2,1)S(1)}, u32[]{:S(2)}, u32[]{:S(2)}) collective-permute-start(bf16[2,16,32,128]{3,2,1,0:T(8,128)(2,1)S(1)} %get-tuple-element.16.turned_ref), channel_id=1, source_target_pairs={{0,4},{4,8},{8,12},{12,16},{16,20},{20,24},{24,28},{28,0},{1,5},{5... | collective-permute-start | bytes 786440 | tf_op jit(solution)/shard_map/ppermute | solution.py:310

commit v4 on v3

v4 whole, which is shorter than its diff:
```python
import jax
import jax.numpy as jnp
from jax import lax
from jax.experimental import pallas as pl
from jax.experimental.pallas import tpu as pltpu
from jax.sharding import PartitionSpec as P

LANES = 128
EPSILON = 1e-06
BLOCK = 8
ORDER = (2, 1, 3, 0)
BATCH = 2
WIDE = jnp.float32
VMEM = pl.BlockSpec(memory_space=pltpu.VMEM)


def limits(mib):
    return pltpu.CompilerParams(vmem_limit_bytes=mib << 20)


def near_tile():
    return 1 - lax.rem(lax.axis_index("sta"), 2)


def whiten(spectra, band_weight, station_order, pair_blocks, hours):
    stations, windows, rows, _ = spectra.shape
    tiles = rows // 2
    mine = tiles // hours
    chunks = 5
    step = windows // chunks
    batches = hours // BATCH
    height = 2 * stations

    def body(order_hbm, pairs_hbm, band_hbm, x_hbm, *refs):
        near_refs, (far_ref, steps_ref) = refs[:batches], refs[batches : batches + 2]
        order_ref, pairs_ref, band_ref, band, rowed, x_ref, sems, small = refs[batches + 2 :]

        def fetch(c):
            part = pl.ds(c * step, step)
            return pltpu.make_async_copy(x_hbm.at[:, part], x_ref.at[:, part], sems.at[c])

        fetch(0).start()
        copies = [
            pltpu.make_async_copy(order_hbm, order_ref, small.at[0]),
            pltpu.make_async_copy(pairs_hbm, pairs_ref, small.at[1]),
            pltpu.make_async_copy(band_hbm, band_ref, small.at[2]),
        ]
        for copy in copies:
            copy.start()
        for c in range(1, chunks):
            fetch(c).start()
        for copy in copies:
            copy.wait()
        for part in range(2):
            band[pl.ds(part, tiles, stride=2), :] = band_ref[...]
        weight = band[...]
        here, me, near = lax.axis_index("hour"), lax.axis_index("sta"), near_tile()
        asked = pairs_ref[0, 1] == me
        for p in range(pair_blocks.shape[0]):
            asked = jnp.logical_or(asked, pairs_ref[p, 1] == me)
            away = (pairs_ref[p, 1] - me).astype(WIDE)
            steps_ref[p] = jnp.full((8, LANES), away, WIDE)
        flag = jnp.where(asked, 1.0, 0.0)
        far_ref[hours * windows] = jnp.full((height, LANES), flag, WIDE).astype(jnp.bfloat16)

        @pl.loop(0, chunks)
        def _(c):
            fetch(c).wait()
            for w in range(step):
                for first in range(0, stations, BLOCK):
                    xs, squares = [], []
                    for k in range(BLOCK):
                        x = x_ref[order_ref[0, first + k], c * step + w].astype(WIDE)
                        xs.append(x)
                        squares.append(jnp.sum(x * x, axis=0, keepdims=True))
                    energy = jnp.sum(jnp.concatenate(squares, axis=0), axis=1, keepdims=True)
                    scale = lax.rsqrt(energy / (rows * LANES) + EPSILON)
                    scale = jnp.broadcast_to(scale, (BLOCK, LANES))
                    for k, x in enumerate(xs):
                        factor = jnp.broadcast_to(scale[k : k + 1], (rows, LANES))
                        place = pl.ds(w * rows * stations + first + k, rows, stride=stations)
                        rowed[place, :] = x * factor * weight
            for k, d in enumerate(ORDER):
                owner = lax.rem(here + d, hours)
                for w in range(step):
                    for tile, out, row in ((near, near_refs[k // BATCH], k % BATCH), (1 - near, far_ref, k)):
                        start = (w * tiles + owner * mine + tile) * height
                        white = rowed[pl.ds(pl.multiple_of(start, height), height), :]
                        out[row * windows + c * step + w] = white.astype(jnp.bfloat16)

    hbm = pl.BlockSpec(memory_space=pltpu.HBM)
    inputs = (station_order, pair_blocks, band_weight, spectra)
    outs = pl.pallas_call(
        body,
        in_specs=[hbm] * 4,
        out_specs=[VMEM] * (batches + 2),
        out_shape=[jax.ShapeDtypeStruct((BATCH * windows, height, LANES), jnp.bfloat16)] * batches
        + [
            jax.ShapeDtypeStruct((hours * windows + 1, height, LANES), jnp.bfloat16),
            jax.ShapeDtypeStruct((pair_blocks.shape[0], 8, LANES), WIDE),
        ],
        scratch_shapes=[
            pltpu.SMEM(station_order.shape, jnp.int32),
            pltpu.SMEM(pair_blocks.shape, jnp.int32),
            pltpu.VMEM((tiles, LANES), WIDE),
            pltpu.VMEM((rows, LANES), WIDE),
            pltpu.VMEM((step * rows * stations, LANES), WIDE),
            pltpu.VMEM(spectra.shape, jnp.bfloat16),
            pltpu.SemaphoreType.DMA((chunks,)),
            pltpu.SemaphoreType.DMA((3,)),
        ],
        compiler_params=limits(8),
        name="whiten",
    )(*[pltpu.with_memory_space_constraint(value, pltpu.HBM) for value in inputs])
    return outs[:batches], outs[batches], outs[batches + 1]


def unit(own_ref, own_row, other_ref, other_row, out_ref, wide):
    stations = own_ref.shape[1] // 2
    windows = wide.shape[0]
    wide[...] = own_ref[pl.ds(own_row, windows)].astype(WIDE)
    for first in range(0, stations, BLOCK):

        def body(w, sums):
            other = other_ref[other_row + w].astype(WIDE)
            re, im = other[:stations], other[stations:]
            new = []
            for k in range(BLOCK):
                a = first + k
                a_re = jnp.broadcast_to(wide[w, a : a + 1, :], re.shape)
                a_im = jnp.broadcast_to(wide[w, stations + a : stations + a + 1, :], re.shape)
                new.append(sums[2 * k] + (a_re * re + a_im * im))
                new.append(sums[2 * k + 1] + (a_re * im - a_im * re))
            return tuple(new)

        zero = jnp.zeros((stations, LANES), WIDE)
        sums = lax.fori_loop(0, windows, body, (zero,) * (2 * BLOCK), unroll=6)
        for k in range(BLOCK):
            out_ref[first + k, :stations] = sums[2 * k].astype(out_ref.dtype)
            out_ref[first + k, stations:] = sums[2 * k + 1].astype(out_ref.dtype)


def product_call(body, operands, windows, dtype, scratch_shapes):
    height = operands[0].shape[1]
    stations = height // 2
    return pl.pallas_call(
        body,
        in_specs=[VMEM] * len(operands),
        out_specs=VMEM,
        out_shape=jax.ShapeDtypeStruct((stations, height, LANES), dtype),
        scratch_shapes=[pltpu.VMEM((windows, height, LANES), WIDE)] + scratch_shapes,
        compiler_params=limits(4),
        cost_estimate=pl.CostEstimate(
            flops=stations * stations * LANES * windows * 8, bytes_accessed=1 << 19, transcendentals=0
        ),
        name="products",
    )(*operands)


def near_product(own, own_place, others, place, windows, dtype):
    def body(own_ref, other_ref, out_ref, wide):
        unit(own_ref, own_place * windows, other_ref, place * windows, out_ref, wide)

    return product_call(body, (own, others), windows, dtype, [])


def far_product(owns, place, other, near, near_place, windows, dtype):
    _, height, _ = other.shape
    stations = height // 2
    row, near_row = place * windows, near_place * windows

    def body(own_ref, other_ref, near_ref, out_ref, wide, twin):
        me = lax.axis_index("sta")
        end = jnp.logical_or(me == 0, me == lax.axis_size("sta") - 1)
        flags = own_ref[owns.shape[0] - 1, :8].astype(WIDE)
        alone = jnp.logical_and(end, jnp.max(flags) > 0.5)

        @pl.when(jnp.logical_not(alone))
        def _():
            unit(own_ref, row, other_ref, near_row, out_ref, wide)

        @pl.when(alone)
        def _():
            unit(own_ref, row, own_ref, row, twin.at[0], wide)
            unit(near_ref, near_row, near_ref, near_row, twin.at[1], wide)
            column = lax.broadcasted_iota(jnp.int32, (stations, LANES), 0)

            @pl.loop(0, stations)
            def _(a):
                one, two = twin[0, a], twin[1, a]
                re = jnp.where(column >= a, one[:stations], two[:stations])
                im = jnp.where(column >= a, one[stations:], two[stations:])
                im = jnp.where(column == a, two[:stations], im)
                out_ref[a, :stations] = re.astype(dtype)
                out_ref[a, stations:] = im.astype(dtype)

    twin = pltpu.VMEM((2, stations, height, LANES), WIDE)
    return product_call(body, (owns, other, near), windows, dtype, [twin])


def turn(a, value, buf_ref):
    height = value.shape[0]
    stations = height // 2
    for part in range(2):
        rows = value[part * stations : (part + 1) * stations]
        buf_ref[pl.ds(part * stations + a, stations, stride=height), :] = -rows if part else rows


def add_hours(parts, scale):
    shape = parts[0].shape
    stations, height, _ = shape

    def body(*refs):
        part_refs, (mine_ref, turned_ref, buf) = refs[: len(parts)], refs[len(parts) :]
        for a in range(stations):
            total = part_refs[0][a].astype(WIDE)
            for ref in part_refs[1:]:
                total = total + ref[a].astype(WIDE)
            total = total * scale
            mine_ref[a] = total
            turn(a, total, buf)
        for c in range(stations):
            turned_ref[c] = buf[pl.ds(c * height, height), :].astype(turned_ref.dtype)

    return pl.pallas_call(
        body,
        in_specs=[VMEM] * len(parts),
        out_specs=[VMEM] * 2,
        out_shape=[jax.ShapeDtypeStruct(shape, WIDE), jax.ShapeDtypeStruct(shape, jnp.bfloat16)],
        scratch_shapes=[pltpu.VMEM((stations * height, LANES), WIDE)],
        compiler_params=limits(4),
        name="add_hours",
    )(*parts)


def assemble(steps, near, far, turned):
    stations, height, _ = turned.shape
    pairs, tiles = steps.shape[0], 2

    def body(steps_ref, near_mine, near_theirs, far_mine, far_theirs, turned_ref, out_ref):
        first = near_tile()
        column = lax.broadcasted_iota(jnp.int32, (stations, LANES), 0)

        def put(p, a, tile, value):
            for part in range(2):
                rows = value[part * stations : (part + 1) * stations]
                out_ref[p, a, pl.ds(tile * 2 + part, stations, stride=2 * tiles), :] = rows

        def hermitian(p, a, tile, above, below, middle):
            re = jnp.where(column > a, above[:stations], below[:stations])
            im = jnp.where(column > a, above[stations:], below[stations:])
            re = jnp.where(column == a, middle, re)
            im = jnp.where(column == a, jnp.zeros_like(im), im)
            put(p, a, tile, jnp.concatenate([re, im], axis=0))

        for p in range(pairs):
            away = jnp.max(steps_ref[p])
            alone = jnp.abs(away) < 0.5
            inside = jnp.logical_and((away > 0.5) == (first == 1), jnp.logical_not(alone))
            outside = jnp.logical_not(jnp.logical_or(alone, inside))

            @pl.when(inside)
            def _(p=p):
                for a in range(stations):
                    put(p, a, first, near_mine[a])
                    put(p, a, 1 - first, near_theirs[a].astype(WIDE))

            @pl.when(outside)
            def _(p=p):
                for a in range(stations):
                    put(p, a, 1 - first, far_mine[a])
                    put(p, a, first, far_theirs[a].astype(WIDE))

            @pl.when(alone)
            def _(p=p):
                for a in range(stations):
                    own, back = far_mine[a], turned_ref[a].astype(WIDE)
                    hermitian(p, a, 1 - first, own, back, own[:stations])
                    hermitian(p, a, first, back, own, own[stations:])

    return pl.pallas_call(
        body,
        in_specs=[VMEM] * 6,
        out_specs=VMEM,
        out_shape=jax.ShapeDtypeStruct((pairs, stations, stations * tiles * 2, LANES), WIDE),
        compiler_params=limits(4),
        name="assemble",
    )(steps, *near, *far, turned)


def per_device(spectra, band_weight, station_order, pair_blocks):
    stations, _, windows, _, bins = spectra.shape
    tiles, pairs = bins // LANES, pair_blocks.shape[0]
    count, hours = lax.axis_size("sta"), lax.axis_size("hour")
    rows = spectra.reshape(stations, windows, 2, tiles, LANES)
    rows = rows.transpose(0, 1, 3, 2, 4).reshape(stations, windows, 2 * tiles, LANES)
    near, far, steps = whiten(rows, band_weight.reshape(tiles, LANES), station_order, pair_blocks, hours)

    on_chip = [(g, g ^ 1) for g in range(count)]
    across = [(g, h) for i in range(1, count - 1, 2) for g, h in ((i, i + 1), (i + 1, i))]

    def to_owner(part, d):
        return lax.ppermute(part, "hour", [(h, (h + d) % hours) for h in range(hours)]) if d else part

    def after(value, *earlier):
        return lax.optimization_barrier((value, earlier))[0]

    near_others = lax.ppermute(far, "sta", on_chip)
    far_others = [lax.ppermute(one, "sta", across) for one in near]
    dtypes = [jnp.bfloat16 if d else WIDE for d in ORDER]
    scale = 1.0 / (hours * windows)

    near_made = [
        near_product(near[k // BATCH], k % BATCH, near_others, k, windows, dtypes[k])
        for k in range(hours)
    ]
    near_parts = [to_owner(part, d) for part, d in zip(near_made, ORDER)]
    far_others[0] = after(far_others[0], *near_made)
    far_made = []
    for k in range(hours):
        batch, place = divmod(k, BATCH)
        if k == (hours // BATCH - 1) * BATCH:
            near_mine, turned = add_hours(after(near_parts, *far_made), scale)
            near_theirs = lax.ppermute(turned, "sta", on_chip)
            far_others[batch] = after(far_others[batch], near_mine)
        far_made.append(far_product(far, k, far_others[batch], near[batch], place, windows, dtypes[k]))
    far_parts = [to_owner(part, d) for part, d in zip(far_made, ORDER)]
    far_mine, turned = add_hours(far_parts, scale)
    far_theirs = lax.ppermute(turned, "sta", across)
    cross = assemble(steps, (near_mine, near_theirs), (far_mine, far_theirs), turned)
    cross = cross.reshape(pairs, stations, stations, tiles // hours, 2, LANES)
    return cross.transpose(0, 1, 2, 4, 3, 5).reshape(pairs, stations, stations, 2, bins // hours)


def solution(mesh):
    return jax.shard_map(
        per_device,
        mesh=mesh,
        in_specs=(P("sta", "hour", None, None, None), P(), P("sta", None), P("sta", None)),
        out_specs=P("sta", None, None, None, "hour"),
        check_vma=False,
    )
```

time: 50.5 us -> 52.1 us (1.032)
  the two profiles are of different devices: /device:TPU:0 before, /device:TPU:1 now
where the time goes in v4:
time: 52.1 us; the launch traced here: 52 us
  starting transfers between devices  24.1 us (46%)
  Pallas kernels  15.3 us (29%)
  waiting for transfers between devices  12.4 us (24%)
    ppermute x6, starting transfers between devices, to_owner(): lax.ppermute(part, 'hour', [(h, (h + d) % hours) for h in range(hours)])  10.6 us
    pallas_call x8, Pallas kernels, product_call(): pl.pallas_call(body, in_specs=[VMEM] * len(operands), out_specs=VMEM, out...  9.98 us
    ppermute x6, waiting for transfers between devices, to_owner(): lax.ppermute(part, 'hour', [(h, (h + d) % hours) for h in range(hours)])  8.37 us
    ppermute x1, starting transfers between devices, per_device(): far_theirs = lax.ppermute(turned, 'sta', across)  6.95 us
    ppermute x2, starting transfers between devices, per_device(): far_others = [lax.ppermute(one, 'sta', across) for one in near]  6.39 us
    ppermute x1, waiting for transfers between devices, per_device(): far_theirs = lax.ppermute(turned, 'sta', across)  3.99 us
    pallas_call x1, Pallas kernels, whiten(): pl.pallas_call(body, in_specs=[hbm] * 4, out_specs=[VMEM] * (batches + 2)...  3.53 us
    pallas_call x1, Pallas kernels, assemble(): pl.pallas_call(body, in_specs=[VMEM] * 6, out_specs=VMEM, out_shape=jax.S...  1.3 us
  transfers between devices with their start and end apart: 11, of which 3 were waited for; matrix products, arithmetic and copies ran while one was open for 0% of the time, Pallas kernels for 20%

profile of v4, /device:TPU:1, one launch (start us, length us, event | category | flops | bytes accessed | tf_op | source)
XLA Modules:
  0.0 52.0 jit_solution(14569379002218950182)
XLA Ops:
  0.0 3.5 %whiten.1 = (bf16[60,32,128]{2,1,0:T(8,128)(2,1)S(1)}, bf16[60,32,128]{2,1,0:T(8,128)(2,1)S(1)}, bf16[121,32,128]{2,1,0:T(8,128)(2,1)S(1)}, f32[2,8,128]{2,1,0:T(8,128)S(1)}) custom-call(s32[1,16]{1,0:T(1,128)} %order_hbm.1, s32[2,2]{1,0:T(2,128)} %pairs_hbm.1, f32[8,128]{1,0:T(8,128)} %bitcast.12, bf16[16,30,16,128]{3,2,1,0:T(8,128)(2,1)} %bitcast.11), custom_call_target="tpu_custom_call" | custom-call | tf_op jit(solution)/shard_map/whiten/pallas_call | solution.py:93
  3.5 0.1 collective-permute-start
  3.7 4.5 %collective-permute-start.4 = (bf16[60,32,128]{2,1,0:T(8,128)(2,1)S(1)}, bf16[60,32,128]{2,1,0:T(8,128)(2,1)S(1)}, u32[]{:S(2)}, u32[]{:S(2)}) collective-permute-start(bf16[60,32,128]{2,1,0:T(8,128)(2,1)S(1)} %get-tuple-element.20.own_ref.near_ref), channel_id=1, source_target_pairs={{4,8},{8,4},{12,16},{16,12},{20,24},{24,20},{5,9},{9,5},{13,17},{1... | collective-permute-start | bytes 1474568 | tf_op jit(solution)/shard_map/ppermute | solution.py:309
  8.1 1.9 %collective-permute-start.8 = (bf16[60,32,128]{2,1,0:T(8,128)(2,1)S(1)}, bf16[60,32,128]{2,1,0:T(8,128)(2,1)S(1)}, u32[]{:S(2)}, u32[]{:S(2)}) collective-permute-start(bf16[60,32,128]{2,1,0:T(8,128)(2,1)S(1)} %get-tuple-element.22.own_ref.near_ref), channel_id=1, source_target_pairs={{4,8},{8,4},{12,16},{16,12},{20,24},{24,20},{5,9},{9,5},{13,17},{1... | collective-permute-start | bytes 1474568 | tf_op jit(solution)/shard_map/ppermute | solution.py:309
  10.1 0.0 collective-permute-done.other_ref
  10.1 1.2 %products.10 = bf16[16,32,128]{2,1,0:T(8,128)(2,1)S(1)} custom-call(bf16[60,32,128]{2,1,0:T(8,128)(2,1)S(1)} %get-tuple-element.22.own_ref.near_ref, bf16[121,32,128]{2,1,0:T(8,128)(2,1)S(1)} %collective-permute-done.other_ref), custom_call_target="tpu_custom_call" | custom-call | flops 7864320 | bytes 524288 | tf_op jit(solution)/shard_map/products/pallas_call | solution.py:146
  11.3 4.0 %collective-permute-start.3 = (bf16[16,32,128]{2,1,0:T(8,128)(2,1)S(1)}, bf16[16,32,128]{2,1,0:T(8,128)(2,1)S(1)}, u32[]{:S(2)}, u32[]{:S(2)}) collective-permute-start(bf16[16,32,128]{2,1,0:T(8,128)(2,1)S(1)} %products.10), channel_id=1, source_target_pairs={{0,3},{1,0},{2,1},{3,2},{4,7},{5,4},{6,5},{7,6},{8,11},{9,8},{10,9... | collective-permute-start | bytes 393224 | tf_op jit(solution)/shard_map/ppermute | solution.py:303
  15.3 1.2 %products.9 = bf16[16,32,128]{2,1,0:T(8,128)(2,1)S(1)} custom-call(bf16[60,32,128]{2,1,0:T(8,128)(2,1)S(1)} %get-tuple-element.20.own_ref.near_ref, bf16[121,32,128]{2,1,0:T(8,128)(2,1)S(1)} %collective-permute-done.other_ref), custom_call_target="tpu_custom_call" | custom-call | flops 7864320 | bytes 524288 | tf_op jit(solution)/shard_map/products/pallas_call | solution.py:146
  16.4 0.1 collective-permute-start.2
  16.5 1.2 %products.8 = bf16[16,32,128]{2,1,0:T(8,128)(2,1)S(1)} custom-call(bf16[60,32,128]{2,1,0:T(8,128)(2,1)S(1)} %get-tuple-element.20.own_ref.near_ref, bf16[121,32,128]{2,1,0:T(8,128)(2,1)S(1)} %collective-permute-done.other_ref), custom_call_target="tpu_custom_call" | custom-call | flops 7864320 | bytes 524288 | tf_op jit(solution)/shard_map/products/pallas_call | solution.py:146
  17.7 0.5 collective-permute-start.1
  18.2 1.2 %products.11.refs_3_ = f32[16,32,128]{2,1,0:T(8,128)S(1)} custom-call(bf16[60,32,128]{2,1,0:T(8,128)(2,1)S(1)} %get-tuple-element.22.own_ref.near_ref, bf16[121,32,128]{2,1,0:T(8,128)(2,1)S(1)} %collective-permute-done.other_ref), custom_call_target="tpu_custom_call" | custom-call | flops 7864320 | bytes 524288 | tf_op jit(solution)/shard_map/products/pallas_call | solution.py:146
  19.4 0.0 collective-permute-done.4.other_ref
  19.4 1.3 %products.13 = bf16[16,32,128]{2,1,0:T(8,128)(2,1)S(1)} custom-call(bf16[121,32,128]{2,1,0:T(8,128)(2,1)S(1)} %get-tuple-element.21.own_ref, bf16[60,32,128]{2,1,0:T(8,128)(2,1)S(1)} %collective-permute-done.4.other_ref, bf16[60,32,128]{2,1,0:T(8,128)(2,1)S(1)} %get-tuple-element.20.own_ref.near_ref), custom_call_target="tpu_custom_call" | custom-call | flops 7864320 | bytes 524288 | tf_op jit(solution)/shard_map/products/pallas_call | solution.py:146
  20.7 3.1 %collective-permute-start.7 = (bf16[16,32,128]{2,1,0:T(8,128)(2,1)S(1)}, bf16[16,32,128]{2,1,0:T(8,128)(2,1)S(1)}, u32[]{:S(2)}, u32[]{:S(2)}) collective-permute-start(bf16[16,32,128]{2,1,0:T(8,128)(2,1)S(1)} %products.13), channel_id=1, source_target_pairs={{0,1},{1,2},{2,3},{3,0},{4,5},{5,6},{6,7},{7,4},{8,9},{9,10},{10,1... | collective-permute-start | bytes 393224 | tf_op jit(solution)/shard_map/ppermute | solution.py:303
  23.9 1.3 %products.12 = bf16[16,32,128]{2,1,0:T(8,128)(2,1)S(1)} custom-call(bf16[121,32,128]{2,1,0:T(8,128)(2,1)S(1)} %get-tuple-element.21.own_ref, bf16[60,32,128]{2,1,0:T(8,128)(2,1)S(1)} %collective-permute-done.4.other_ref, bf16[60,32,128]{2,1,0:T(8,128)(2,1)S(1)} %get-tuple-element.20.own_ref.near_ref), custom_call_target="tpu_custom_call" | custom-call | flops 7864320 | bytes 524288 | tf_op jit(solution)/shard_map/products/pallas_call | solution.py:146
  25.2 0.0 collective-permute-done.3.refs_2_
  25.2 1.7 %collective-permute-start.6 = (bf16[16,32,128]{2,1,0:T(8,128)(2,1)S(1)}, bf16[16,32,128]{2,1,0:T(8,128)(2,1)S(1)}, u32[]{:S(2)}, u32[]{:S(2)}) collective-permute-start(bf16[16,32,128]{2,1,0:T(8,128)(2,1)S(1)} %products.12), channel_id=1, source_target_pairs={{0,2},{1,3},{2,0},{3,1},{4,6},{5,7},{6,4},{7,5},{8,10},{9,11},{10,... | collective-permute-start | bytes 393224 | tf_op jit(solution)/shard_map/ppermute | solution.py:303
  26.9 0.0 collective-permute-done.2.refs_1_
  26.9 6.0 %collective-permute-done.1.refs_0_ = bf16[16,32,128]{2,1,0:T(8,128)(2,1)S(1)} collective-permute-done((bf16[16,32,128]{2,1,0:T(8,128)(2,1)S(1)}, bf16[16,32,128]{2,1,0:T(8,128)(2,1)S(1)}, u32[]{:S(2)}, u32[]{:S(2)}) %collective-permute-start.1) | collective-permute-done | bytes 131104 | tf_op jit(solution)/shard_map/ppermute | solution.py:303
  32.9 0.3 add_hours.2
  33.2 0.0 collective-permute-done.8.other_ref
  33.2 1.3 %products.14 = bf16[16,32,128]{2,1,0:T(8,128)(2,1)S(1)} custom-call(bf16[121,32,128]{2,1,0:T(8,128)(2,1)S(1)} %get-tuple-element.21.own_ref, bf16[60,32,128]{2,1,0:T(8,128)(2,1)S(1)} %collective-permute-done.8.other_ref, bf16[60,32,128]{2,1,0:T(8,128)(2,1)S(1)} %get-tuple-element.22.own_ref.near_ref), custom_call_target="tpu_custom_call" | custom-call | flops 7864320 | bytes 524288 | tf_op jit(solution)/shard_map/products/pallas_call | solution.py:146
  34.5 1.3 %collective-permute-start.9 = (bf16[16,32,128]{2,1,0:T(8,128)(2,1)S(1)}, bf16[16,32,128]{2,1,0:T(8,128)(2,1)S(1)}, u32[]{:S(2)}, u32[]{:S(2)}) collective-permute-start(bf16[16,32,128]{2,1,0:T(8,128)(2,1)S(1)} %products.14), channel_id=1, source_target_pairs={{0,3},{1,0},{2,1},{3,2},{4,7},{5,4},{6,5},{7,6},{8,11},{9,8},{10,9... | collective-permute-start | bytes 393224 | tf_op jit(solution)/shard_map/ppermute | solution.py:303
  35.7 0.0 collective-permute-start.5
  35.7 1.3 %products.15.refs_3_ = f32[16,32,128]{2,1,0:T(8,128)S(1)} custom-call(bf16[121,32,128]{2,1,0:T(8,128)(2,1)S(1)} %get-tuple-element.21.own_ref, bf16[60,32,128]{2,1,0:T(8,128)(2,1)S(1)} %collective-permute-done.8.other_ref, bf16[60,32,128]{2,1,0:T(8,128)(2,1)S(1)} %get-tuple-element.22.own_ref.near_ref), custom_call_target="tpu_custom_call" | custom-call | flops 7864320 | bytes 524288 | tf_op jit(solution)/shard_map/products/pallas_call | solution.py:146
  37.1 0.0 collective-permute-done.7.refs_1_
  37.1 0.0 collective-permute-done.6.refs_0_
  37.1 2.4 %collective-permute-done.9.refs_2_ = bf16[16,32,128]{2,1,0:T(8,128)(2,1)S(1)} collective-permute-done((bf16[16,32,128]{2,1,0:T(8,128)(2,1)S(1)}, bf16[16,32,128]{2,1,0:T(8,128)(2,1)S(1)}, u32[]{:S(2)}, u32[]{:S(2)}) %collective-permute-start.9) | collective-permute-done | bytes 131104 | tf_op jit(solution)/shard_map/ppermute | solution.py:303
  39.4 0.3 add_hours.3
  39.7 7.0 %collective-permute-start.10 = (bf16[16,32,128]{2,1,0:T(8,128)(2,1)S(1)}, bf16[16,32,128]{2,1,0:T(8,128)(2,1)S(1)}, u32[]{:S(2)}, u32[]{:S(2)}) collective-permute-start(bf16[16,32,128]{2,1,0:T(8,128)(2,1)S(1)} %get-tuple-element.32.turned_ref), channel_id=1, source_target_pairs={{4,8},{8,4},{12,16},{16,12},{20,24},{24,20},{5,9},{9,5},{13,17},{1... | collective-permute-start | bytes 393224 | tf_op jit(solution)/shard_map/ppermute | solution.py:329
  46.7 0.0 collective-permute-done.5.near_theirs
  46.7 4.0 %collective-permute-done.10.far_theirs = bf16[16,32,128]{2,1,0:T(8,128)(2,1)S(1)} collective-permute-done((bf16[16,32,128]{2,1,0:T(8,128)(2,1)S(1)}, bf16[16,32,128]{2,1,0:T(8,128)(2,1)S(1)}, u32[]{:S(2)}, u32[]{:S(2)}) %collective-permute-start.10) | collective-permute-done | bytes 131104 | tf_op jit(solution)/shard_map/ppermute | solution.py:329
  50.7 1.3 %assemble.1 = f32[2,16,64,128]{3,2,1,0:T(8,128)} custom-call(f32[2,8,128]{2,1,0:T(8,128)S(1)} %get-tuple-element.19.steps_ref, f32[16,32,128]{2,1,0:T(8,128)S(1)} %get-tuple-element.28.near_mine, bf16[16,32,128]{2,1,0:T(8,128)(2,1)S(1)} %collective-permute-done.5.near_theirs, f32[16,32,128]{2,1,0:T(8,128)S(1)} %get-tuple-element.31.far_mine, ...), custom_call_target="tpu_custom_call" | custom-call | tf_op jit(solution)/shard_map/assemble/pallas_call | solution.py:281
Async XLA Ops:
  3.5 6.5 %collective-permute-start = (bf16[121,32,128]{2,1,0:T(8,128)(2,1)S(1)}, bf16[121,32,128]{2,1,0:T(8,128)(2,1)S(1)}, u32[]{:S(2)}, u32[]{:S(2)}) collective-permute-start(bf16[121,32,128]{2,1,0:T(8,128)(2,1)S(1)} %get-tuple-element.21.own_ref), channel_id=1, source_target_pairs={{0,4},{4,0},{8,12},{12,8},{16,20},{20,16},{24,28},{28,24},{1,5},{5... | collective-permute-start | bytes 2973704 | tf_op jit(solution)/shard_map/ppermute | solution.py:308
  3.7 15.7 %collective-permute-start.4 = (bf16[60,32,128]{2,1,0:T(8,128)(2,1)S(1)}, bf16[60,32,128]{2,1,0:T(8,128)(2,1)S(1)}, u32[]{:S(2)}, u32[]{:S(2)}) collective-permute-start(bf16[60,32,128]{2,1,0:T(8,128)(2,1)S(1)} %get-tuple-element.20.own_ref.near_ref), channel_id=1, source_target_pairs={{4,8},{8,4},{12,16},{16,12},{20,24},{24,20},{5,9},{9,5},{13,17},{1... | collective-permute-start | bytes 1474568 | tf_op jit(solution)/shard_map/ppermute | solution.py:309
  8.1 25.0 %collective-permute-start.8 = (bf16[60,32,128]{2,1,0:T(8,128)(2,1)S(1)}, bf16[60,32,128]{2,1,0:T(8,128)(2,1)S(1)}, u32[]{:S(2)}, u32[]{:S(2)}) collective-permute-start(bf16[60,32,128]{2,1,0:T(8,128)(2,1)S(1)} %get-tuple-element.22.own_ref.near_ref), channel_id=1, source_target_pairs={{4,8},{8,4},{12,16},{16,12},{20,24},{24,20},{5,9},{9,5},{13,17},{1... | collective-permute-start | bytes 1474568 | tf_op jit(solution)/shard_map/ppermute | solution.py:309
  11.3 13.9 %collective-permute-start.3 = (bf16[16,32,128]{2,1,0:T(8,128)(2,1)S(1)}, bf16[16,32,128]{2,1,0:T(8,128)(2,1)S(1)}, u32[]{:S(2)}, u32[]{:S(2)}) collective-permute-start(bf16[16,32,128]{2,1,0:T(8,128)(2,1)S(1)} %products.10), channel_id=1, source_target_pairs={{0,3},{1,0},{2,1},{3,2},{4,7},{5,4},{6,5},{7,6},{8,11},{9,8},{10,9... | collective-permute-start | bytes 393224 | tf_op jit(solution)/shard_map/ppermute | solution.py:303
  16.4 10.4 %collective-permute-start.2 = (bf16[16,32,128]{2,1,0:T(8,128)(2,1)S(1)}, bf16[16,32,128]{2,1,0:T(8,128)(2,1)S(1)}, u32[]{:S(2)}, u32[]{:S(2)}) collective-permute-start(bf16[16,32,128]{2,1,0:T(8,128)(2,1)S(1)} %products.9), channel_id=1, source_target_pairs={{0,1},{1,2},{2,3},{3,0},{4,5},{5,6},{6,7},{7,4},{8,9},{9,10},{10,1... | collective-permute-start | bytes 393224 | tf_op jit(solution)/shard_map/ppermute | solution.py:303
  17.7 15.2 %collective-permute-start.1 = (bf16[16,32,128]{2,1,0:T(8,128)(2,1)S(1)}, bf16[16,32,128]{2,1,0:T(8,128)(2,1)S(1)}, u32[]{:S(2)}, u32[]{:S(2)}) collective-permute-start(bf16[16,32,128]{2,1,0:T(8,128)(2,1)S(1)} %products.8), channel_id=1, source_target_pairs={{0,2},{1,3},{2,0},{3,1},{4,6},{5,7},{6,4},{7,5},{8,10},{9,11},{10,... | collective-permute-start | bytes 393224 | tf_op jit(solution)/shard_map/ppermute | solution.py:303
  20.7 16.3 %collective-permute-start.7 = (bf16[16,32,128]{2,1,0:T(8,128)(2,1)S(1)}, bf16[16,32,128]{2,1,0:T(8,128)(2,1)S(1)}, u32[]{:S(2)}, u32[]{:S(2)}) collective-permute-start(bf16[16,32,128]{2,1,0:T(8,128)(2,1)S(1)} %products.13), channel_id=1, source_target_pairs={{0,1},{1,2},{2,3},{3,0},{4,5},{5,6},{6,7},{7,4},{8,9},{9,10},{10,1... | collective-permute-start | bytes 393224 | tf_op jit(solution)/shard_map/ppermute | solution.py:303
  25.2 11.9 %collective-permute-start.6 = (bf16[16,32,128]{2,1,0:T(8,128)(2,1)S(1)}, bf16[16,32,128]{2,1,0:T(8,128)(2,1)S(1)}, u32[]{:S(2)}, u32[]{:S(2)}) collective-permute-start(bf16[16,32,128]{2,1,0:T(8,128)(2,1)S(1)} %products.12), channel_id=1, source_target_pairs={{0,2},{1,3},{2,0},{3,1},{4,6},{5,7},{6,4},{7,5},{8,10},{9,11},{10,... | collective-permute-start | bytes 393224 | tf_op jit(solution)/shard_map/ppermute | solution.py:303
  34.5 5.0 %collective-permute-start.9 = (bf16[16,32,128]{2,1,0:T(8,128)(2,1)S(1)}, bf16[16,32,128]{2,1,0:T(8,128)(2,1)S(1)}, u32[]{:S(2)}, u32[]{:S(2)}) collective-permute-start(bf16[16,32,128]{2,1,0:T(8,128)(2,1)S(1)} %products.14), channel_id=1, source_target_pairs={{0,3},{1,0},{2,1},{3,2},{4,7},{5,4},{6,5},{7,6},{8,11},{9,8},{10,9... | collective-permute-start | bytes 393224 | tf_op jit(solution)/shard_map/ppermute | solution.py:303
  35.7 10.9 %collective-permute-start.5 = (bf16[16,32,128]{2,1,0:T(8,128)(2,1)S(1)}, bf16[16,32,128]{2,1,0:T(8,128)(2,1)S(1)}, u32[]{:S(2)}, u32[]{:S(2)}) collective-permute-start(bf16[16,32,128]{2,1,0:T(8,128)(2,1)S(1)} %get-tuple-element.29), channel_id=1, source_target_pairs={{0,4},{4,0},{8,12},{12,8},{16,20},{20,16},{24,28},{28,24},{1,5},{5... | collective-permute-start | bytes 393224 | tf_op jit(solution)/shard_map/ppermute | solution.py:324
  39.7 11.0 %collective-permute-start.10 = (bf16[16,32,128]{2,1,0:T(8,128)(2,1)S(1)}, bf16[16,32,128]{2,1,0:T(8,128)(2,1)S(1)}, u32[]{:S(2)}, u32[]{:S(2)}) collective-permute-start(bf16[16,32,128]{2,1,0:T(8,128)(2,1)S(1)} %get-tuple-element.32.turned_ref), channel_id=1, source_target_pairs={{4,8},{8,4},{12,16},{16,12},{20,24},{24,20},{5,9},{9,5},{13,17},{1... | collective-permute-start | bytes 393224 | tf_op jit(solution)/shard_map/ppermute | solution.py:329

commit v5 on v4

v5 whole, which is shorter than its diff:
```python
import jax
import jax.numpy as jnp
from jax import lax
from jax.experimental import pallas as pl
from jax.experimental.pallas import tpu as pltpu
from jax.sharding import PartitionSpec as P

LANES = 128
EPSILON = 1e-06
BLOCK = 8
ORDER = (2, 1, 3, 0)
BATCH = 2
WIDE = jnp.float32
VMEM = pl.BlockSpec(memory_space=pltpu.VMEM)


def limits(mib):
    return pltpu.CompilerParams(vmem_limit_bytes=mib << 20)


def whiten(spectra, band_weight, station_order, pair_blocks, hours):
    stations, windows, rows, _ = spectra.shape
    tiles = rows // 2
    mine = tiles // hours
    chunks = 5
    step = windows // chunks
    batches = hours // BATCH
    height = 2 * stations

    def body(order_hbm, pairs_hbm, band_hbm, x_hbm, *refs):
        piece_refs, (whole_ref, steps_ref) = refs[:batches], refs[batches : batches + 2]
        order_ref, pairs_ref, band_ref, band, rowed, x_ref, sems, small = refs[batches + 2 :]

        def fetch(c):
            part = pl.ds(c * step, step)
            return pltpu.make_async_copy(x_hbm.at[:, part], x_ref.at[:, part], sems.at[c])

        fetch(0).start()
        copies = [
            pltpu.make_async_copy(order_hbm, order_ref, small.at[0]),
            pltpu.make_async_copy(pairs_hbm, pairs_ref, small.at[1]),
            pltpu.make_async_copy(band_hbm, band_ref, small.at[2]),
        ]
        for copy in copies:
            copy.start()
        for c in range(1, chunks):
            fetch(c).start()
        for copy in copies:
            copy.wait()
        for part in range(2):
            band[pl.ds(part, tiles, stride=2), :] = band_ref[...]
        weight = band[...]
        here, me = lax.axis_index("hour"), lax.axis_index("sta")
        even = lax.rem(me, 2) == 0
        asked = pairs_ref[0, 1] == me
        for p in range(pair_blocks.shape[0]):
            asked = jnp.logical_or(asked, pairs_ref[p, 1] == me)
            away = (pairs_ref[p, 1] - me).astype(WIDE)
            steps_ref[p] = jnp.full((8, LANES), away, WIDE)
        flag = jnp.where(asked, 1.0, 0.0)
        for out in (*piece_refs, whole_ref):
            out[out.shape[0] - 1] = jnp.full((height, LANES), flag, WIDE).astype(jnp.bfloat16)

        @pl.loop(0, chunks)
        def _(c):
            fetch(c).wait()
            for w in range(step):
                for first in range(0, stations, BLOCK):
                    xs, squares = [], []
                    for k in range(BLOCK):
                        x = x_ref[order_ref[0, first + k], c * step + w].astype(WIDE)
                        xs.append(x)
                        squares.append(jnp.sum(x * x, axis=0, keepdims=True))
                    energy = jnp.sum(jnp.concatenate(squares, axis=0), axis=1, keepdims=True)
                    scale = lax.rsqrt(energy / (rows * LANES) + EPSILON)
                    scale = jnp.broadcast_to(scale, (BLOCK, LANES))
                    for k, x in enumerate(xs):
                        factor = jnp.broadcast_to(scale[k : k + 1], (rows, LANES))
                        place = pl.ds(w * rows * stations + first + k, rows, stride=stations)
                        rowed[place, :] = x * factor * weight

            def write(k, out, row):
                owner = lax.rem(here + ORDER[k], hours)
                for tile in range(mine):
                    for w in range(step):
                        start = (w * tiles + owner * mine + tile) * height
                        white = rowed[pl.ds(pl.multiple_of(start, height), height), :]
                        out[row + tile * windows + c * step + w] = white.astype(jnp.bfloat16)

            @pl.when(even)
            def _():
                for k in range(hours):
                    write(k, piece_refs[k // BATCH], k % BATCH * mine * windows)

            @pl.when(jnp.logical_not(even))
            def _():
                for k in range(hours):
                    write(k, whole_ref, k * mine * windows)

    hbm = pl.BlockSpec(memory_space=pltpu.HBM)
    inputs = (station_order, pair_blocks, band_weight, spectra)
    outs = pl.pallas_call(
        body,
        in_specs=[hbm] * 4,
        out_specs=[VMEM] * (batches + 2),
        out_shape=[jax.ShapeDtypeStruct((BATCH * mine * windows + 1, height, LANES), jnp.bfloat16)] * batches
        + [
            jax.ShapeDtypeStruct((tiles * windows + 1, height, LANES), jnp.bfloat16),
            jax.ShapeDtypeStruct((pair_blocks.shape[0], 8, LANES), WIDE),
        ],
        scratch_shapes=[
            pltpu.SMEM(station_order.shape, jnp.int32),
            pltpu.SMEM(pair_blocks.shape, jnp.int32),
            pltpu.VMEM((tiles, LANES), WIDE),
            pltpu.VMEM((rows, LANES), WIDE),
            pltpu.VMEM((step * rows * stations, LANES), WIDE),
            pltpu.VMEM(spectra.shape, jnp.bfloat16),
            pltpu.SemaphoreType.DMA((chunks,)),
            pltpu.SemaphoreType.DMA((3,)),
        ],
        compiler_params=limits(8),
        name="whiten",
    )(*[pltpu.with_memory_space_constraint(value, pltpu.HBM) for value in inputs])
    return outs[:batches], outs[batches], outs[batches + 1]


def unit(own_ref, own_row, other_ref, other_row, out_ref, wide):
    stations = own_ref.shape[1] // 2
    windows = wide.shape[0]
    wide[...] = own_ref[pl.ds(own_row, windows)].astype(WIDE)
    for first in range(0, stations, BLOCK):

        def body(w, sums):
            other = other_ref[other_row + w].astype(WIDE)
            re, im = other[:stations], other[stations:]
            new = []
            for k in range(BLOCK):
                a = first + k
                a_re = jnp.broadcast_to(wide[w, a : a + 1, :], re.shape)
                a_im = jnp.broadcast_to(wide[w, stations + a : stations + a + 1, :], re.shape)
                new.append(sums[2 * k] + (a_re * re + a_im * im))
                new.append(sums[2 * k + 1] + (a_re * im - a_im * re))
            return tuple(new)

        zero = jnp.zeros((stations, LANES), WIDE)
        sums = lax.fori_loop(0, windows, body, (zero,) * (2 * BLOCK), unroll=6)
        for k in range(BLOCK):
            out_ref[first + k, :stations] = sums[2 * k].astype(out_ref.dtype)
            out_ref[first + k, stations:] = sums[2 * k + 1].astype(out_ref.dtype)


def product_call(body, operands, tiles, windows, dtype, scratch_shapes):
    height = operands[0].shape[1]
    stations = height // 2
    flops = tiles * stations * stations * LANES * windows * 8
    return pl.pallas_call(
        body,
        in_specs=[VMEM] * len(operands),
        out_specs=VMEM,
        out_shape=jax.ShapeDtypeStruct((tiles, stations, height, LANES), dtype),
        scratch_shapes=[pltpu.VMEM((windows, height, LANES), WIDE)] + scratch_shapes,
        compiler_params=limits(4),
        cost_estimate=pl.CostEstimate(flops=flops, bytes_accessed=1 << 20, transcendentals=0),
        name="products",
    )(*operands)


def near_product(piece, piece_place, others, place, tiles, windows, dtype):
    def body(own_ref, other_ref, out_ref, wide):
        @pl.when(lax.rem(lax.axis_index("sta"), 2) == 0)
        def _():
            for tile in range(tiles):
                row = (place * tiles + tile) * windows
                own_row = (piece_place * tiles + tile) * windows
                unit(own_ref, own_row, other_ref, row, out_ref.at[tile], wide)

    return product_call(body, (piece, others), tiles, windows, dtype, [])


def far_product(whole, place, piece, piece_place, tiles, windows, dtype):
    entries, height, _ = piece.shape
    stations = height // 2

    def body(own_ref, other_ref, out_ref, wide, twin):
        me = lax.axis_index("sta")
        flags = own_ref[whole.shape[0] - 1, :8].astype(WIDE) + other_ref[entries - 1, :8].astype(WIDE)
        last = me == lax.axis_size("sta") - 1
        alone = jnp.logical_and(last, jnp.max(flags) > 0.5)

        @pl.when(jnp.logical_and(lax.rem(me, 2) == 1, jnp.logical_not(alone)))
        def _():
            for tile in range(tiles):
                row = (place * tiles + tile) * windows
                other_row = (piece_place * tiles + tile) * windows
                unit(own_ref, row, other_ref, other_row, out_ref.at[tile], wide)

        @pl.when(alone)
        def _():
            column = lax.broadcasted_iota(jnp.int32, (stations, LANES), 0)
            for tile in range(tiles):
                row = (place * tiles + tile) * windows
                unit(own_ref, row, own_ref, row, twin.at[0], wide)
                other_row = (piece_place * tiles + tile) * windows
                unit(other_ref, other_row, other_ref, other_row, twin.at[1], wide)

                @pl.loop(0, stations)
                def _(a, tile=tile):
                    one, two = twin[0, a], twin[1, a]
                    re = jnp.where(column >= a, one[:stations], two[:stations])
                    im = jnp.where(column >= a, one[stations:], two[stations:])
                    im = jnp.where(column == a, two[:stations], im)
                    out_ref[tile, a, :stations] = re.astype(dtype)
                    out_ref[tile, a, stations:] = im.astype(dtype)

    twin = pltpu.VMEM((2, stations, height, LANES), WIDE)
    return product_call(body, (whole, piece), tiles, windows, dtype, [twin])


def turn(a, value, buf_ref):
    height = value.shape[0]
    stations = height // 2
    for part in range(2):
        rows = value[part * stations : (part + 1) * stations]
        buf_ref[pl.ds(part * stations + a, stations, stride=height), :] = -rows if part else rows


def add_hours(parts, parity, scale):
    shape = parts[0].shape
    tiles, stations, height, _ = shape

    def body(*refs):
        part_refs, (mine_ref, turned_ref, buf) = refs[: len(parts)], refs[len(parts) :]

        @pl.when(lax.rem(lax.axis_index("sta"), 2) == parity)
        def _():
            for tile in range(tiles):
                for a in range(stations):
                    total = part_refs[0][tile, a].astype(WIDE)
                    for ref in part_refs[1:]:
                        total = total + ref[tile, a].astype(WIDE)
                    total = total * scale
                    mine_ref[tile, a] = total
                    turn(a, total, buf.at[tile])
                for c in range(stations):
                    rows = buf[tile, pl.ds(c * height, height), :]
                    turned_ref[tile, c] = rows.astype(turned_ref.dtype)

    return pl.pallas_call(
        body,
        in_specs=[VMEM] * len(parts),
        out_specs=[VMEM] * 2,
        out_shape=[jax.ShapeDtypeStruct(shape, WIDE), jax.ShapeDtypeStruct(shape, jnp.bfloat16)],
        scratch_shapes=[pltpu.VMEM((tiles, stations * height, LANES), WIDE)],
        compiler_params=limits(4),
        name="add_hours",
    )(*parts)


def assemble(steps, near, far, turned):
    tiles, stations, height, _ = turned.shape
    pairs = steps.shape[0]

    def body(steps_ref, near_mine, near_theirs, far_mine, far_theirs, turned_ref, out_ref, buf):
        me = lax.axis_index("sta")
        even = lax.rem(me, 2) == 0
        odd = jnp.logical_not(even)
        column = lax.broadcasted_iota(jnp.int32, (stations, LANES), 0)

        def put(p, a, tile, value):
            for part in range(2):
                rows = value[part * stations : (part + 1) * stations]
                out_ref[p, a, pl.ds(tile * 2 + part, stations, stride=2 * tiles), :] = rows

        def hermitian(p, a, tile, above, below, middle):
            re = jnp.where(column > a, above[:stations], below[:stations])
            im = jnp.where(column > a, above[stations:], below[stations:])
            re = jnp.where(column == a, middle, re)
            im = jnp.where(column == a, jnp.zeros_like(im), im)
            put(p, a, tile, jnp.concatenate([re, im], axis=0))

        for p in range(pairs):
            away = jnp.max(steps_ref[p])
            before, after, alone = away < -0.5, away > 0.5, jnp.abs(away) < 0.5
            cases = (
                (jnp.logical_and(even, after), near_mine),
                (jnp.logical_and(odd, before), near_theirs),
                (jnp.logical_and(odd, after), far_mine),
                (jnp.logical_and(even, before), far_theirs),
            )
            for case, ref in cases:

                @pl.when(case)
                def _(p=p, ref=ref):
                    for tile in range(tiles):
                        for a in range(stations):
                            put(p, a, tile, ref[tile, a].astype(WIDE))

            @pl.when(jnp.logical_and(odd, alone))
            def _(p=p):
                for tile in range(tiles):
                    for a in range(stations):
                        own = far_mine[tile, a]
                        back = turned_ref[tile, a].astype(WIDE)
                        hermitian(p, a, tile, own, back, own[:stations])

            @pl.when(jnp.logical_and(even, alone))
            def _(p=p):
                for tile in range(tiles):
                    for a in range(stations):
                        turn(a, far_theirs[tile, a].astype(WIDE), buf)
                    for a in range(stations):
                        theirs = far_theirs[tile, a].astype(WIDE)
                        back = buf[pl.ds(a * height, height), :]
                        hermitian(p, a, tile, theirs, back, -theirs[stations:])

    return pl.pallas_call(
        body,
        in_specs=[VMEM] * 6,
        out_specs=VMEM,
        out_shape=jax.ShapeDtypeStruct((pairs, stations, stations * tiles * 2, LANES), WIDE),
        scratch_shapes=[pltpu.VMEM((stations * height, LANES), WIDE)],
        compiler_params=limits(4),
        name="assemble",
    )(steps, *near, *far, turned)


def per_device(spectra, band_weight, station_order, pair_blocks):
    stations, _, windows, _, bins = spectra.shape
    tiles, pairs = bins // LANES, pair_blocks.shape[0]
    count, hours = lax.axis_size("sta"), lax.axis_size("hour")
    rows = spectra.reshape(stations, windows, 2, tiles, LANES)
    rows = rows.transpose(0, 1, 3, 2, 4).reshape(stations, windows, 2 * tiles, LANES)
    pieces, whole, steps = whiten(rows, band_weight.reshape(tiles, LANES), station_order, pair_blocks, hours)

    near_pairs = [(g + 1, g) for g in range(0, count, 2)]
    far_pairs = [((g + 1) % count, g) for g in range(1, count, 2)]

    def back(pairs):
        return [(j, i) for i, j in pairs]

    def to_owner(part, d, parity):
        if d == 0:
            return part
        moves = [
            (g * hours + h, g * hours + (h + d) % hours)
            for g in range(parity, count, 2)
            for h in range(hours)
        ]
        return lax.ppermute(part, ("sta", "hour"), moves)

    def after(value, *earlier):
        return lax.optimization_barrier((value, earlier))[0]

    dtypes = [jnp.bfloat16 if d else WIDE for d in ORDER]
    scale = 1.0 / (hours * windows)
    near_others = lax.ppermute(whole, "sta", near_pairs)
    far_others = [lax.ppermute(piece, "sta", far_pairs) for piece in pieces]
    mine = tiles // hours
    near_made, far_made = [], []
    for k in range(hours):
        batch, place = divmod(k, BATCH)
        near_made.append(near_product(pieces[batch], place, near_others, k, mine, windows, dtypes[k]))
    near_parts = [to_owner(part, d, 0) for part, d in zip(near_made, ORDER)]
    far_others[0] = after(far_others[0], *near_made)
    for k in range(hours):
        batch, place = divmod(k, BATCH)
        if k == hours - BATCH:
            near_mine, turned = add_hours(after(near_parts, *far_made), 0, scale)
            near_theirs = lax.ppermute(turned, "sta", back(near_pairs))
            far_others[batch] = after(far_others[batch], near_mine)
        far_made.append(far_product(whole, k, far_others[batch], place, mine, windows, dtypes[k]))
    far_parts = [to_owner(part, d, 1) for part, d in zip(far_made, ORDER)]
    far_mine, turned = add_hours(far_parts, 1, scale)
    far_theirs = lax.ppermute(turned, "sta", back(far_pairs))
    cross = assemble(steps, (near_mine, near_theirs), (far_mine, far_theirs), turned)
    cross = cross.reshape(pairs, stations, stations, tiles // hours, 2, LANES)
    return cross.transpose(0, 1, 2, 4, 3, 5).reshape(pairs, stations, stations, 2, bins // hours)


def solution(mesh):
    return jax.shard_map(
        per_device,
        mesh=mesh,
        in_specs=(P("sta", "hour", None, None, None), P(), P("sta", None), P("sta", None)),
        out_specs=P("sta", None, None, None, "hour"),
        check_vma=False,
    )
```

time: 52.1 us -> 60.5 us (1.16)
  the two profiles are of different devices: /device:TPU:1 before, /device:TPU:0 now
where the time goes in v5:
time: 60.5 us; the launch traced here: 60.2 us
  starting transfers between devices  24.3 us (40%)
  waiting for transfers between devices  20.1 us (33%)
  Pallas kernels  15.5 us (26%)
    ppermute x6, waiting for transfers between devices, to_owner(): return lax.ppermute(part, ('sta', 'hour'), moves)  12.8 us
    ppermute x6, starting transfers between devices, to_owner(): return lax.ppermute(part, ('sta', 'hour'), moves)  12.4 us
    pallas_call x8, Pallas kernels, product_call(): pl.pallas_call(body, in_specs=[VMEM] * len(operands), out_specs=VMEM, out...  10.1 us
    ppermute x2, starting transfers between devices, per_device(): far_others = [lax.ppermute(piece, 'sta', far_pairs) for piece in pieces]  8.07 us
    ppermute x1, waiting for transfers between devices, per_device(): far_theirs = lax.ppermute(turned, 'sta', back(far_pairs))  7.28 us
    pallas_call x1, Pallas kernels, whiten(): pl.pallas_call(body, in_specs=[hbm] * 4, out_specs=[VMEM] * (batches + 2)...  3.59 us
    pallas_call x1, Pallas kernels, assemble(): pl.pallas_call(body, in_specs=[VMEM] * 6, out_specs=VMEM, out_shape=jax.S...  1.31 us
    ppermute x1, starting transfers between devices, per_device(): near_theirs = lax.ppermute(turned, 'sta', back(near_pairs))  1.31 us
  transfers between devices with their start and end apart: 11, of which 2 were waited for; matrix products, arithmetic and copies ran while one was open for 0% of the time, Pallas kernels for 18%

profile of v5, /device:TPU:0, one launch (start us, length us, event | category | flops | bytes accessed | tf_op | source)
XLA Modules:
  0.0 60.2 jit_solution(13175239660450277028)
XLA Ops:
  0.0 3.6 %whiten.1 = (bf16[121,32,128]{2,1,0:T(8,128)(2,1)S(1)}, bf16[121,32,128]{2,1,0:T(8,128)(2,1)S(1)}, bf16[241,32,128]{2,1,0:T(8,128)(2,1)S(1)}, f32[2,8,128]{2,1,0:T(8,128)S(1)}) custom-call(s32[1,16]{1,0:T(1,128)} %order_hbm.1, s32[2,2]{1,0:T(2,128)} %pairs_hbm.1, f32[8,128]{1,0:T(8,128)} %bitcast.12, bf16[16,30,16,128]{3,2,1,0:T(8,128)(2,1)} %bitcast.11), custom_call_target="tpu_custom_call" | custom-call | tf_op jit(solution)/shard_map/whiten/pallas_call | solution.py:102
  3.6 1.3 %collective-permute-start = (bf16[241,32,128]{2,1,0:T(8,128)(2,1)S(1)}, bf16[241,32,128]{2,1,0:T(8,128)(2,1)S(1)}, u32[]{:S(2)}, u32[]{:S(2)}) collective-permute-start(bf16[241,32,128]{2,1,0:T(8,128)(2,1)S(1)} %get-tuple-element.21.own_ref), channel_id=1, source_target_pairs={{4,0},{12,8},{20,16},{28,24},{5,1},{13,9},{21,17},{29,25},{6,2},{1... | collective-permute-start | bytes 5922824 | tf_op jit(solution)/shard_map/ppermute | solution.py:356
  4.9 6.7 %collective-permute-start.4 = (bf16[121,32,128]{2,1,0:T(8,128)(2,1)S(1)}, bf16[121,32,128]{2,1,0:T(8,128)(2,1)S(1)}, u32[]{:S(2)}, u32[]{:S(2)}) collective-permute-start(bf16[121,32,128]{2,1,0:T(8,128)(2,1)S(1)} %get-tuple-element.20.own_ref), channel_id=1, source_target_pairs={{8,4},{16,12},{24,20},{0,28},{9,5},{17,13},{25,21},{1,29},{10,6},{... | collective-permute-start | bytes 2973704 | tf_op jit(solution)/shard_map/ppermute | solution.py:357
  11.6 1.4 %collective-permute-start.8 = (bf16[121,32,128]{2,1,0:T(8,128)(2,1)S(1)}, bf16[121,32,128]{2,1,0:T(8,128)(2,1)S(1)}, u32[]{:S(2)}, u32[]{:S(2)}) collective-permute-start(bf16[121,32,128]{2,1,0:T(8,128)(2,1)S(1)} %get-tuple-element.22.own_ref), channel_id=1, source_target_pairs={{8,4},{16,12},{24,20},{0,28},{9,5},{17,13},{25,21},{1,29},{10,6},{... | collective-permute-start | bytes 2973704 | tf_op jit(solution)/shard_map/ppermute | solution.py:357
  13.0 0.0 collective-permute-done.other_ref
  13.0 2.4 %products.10 = bf16[2,16,32,128]{3,2,1,0:T(8,128)(2,1)S(1)} custom-call(bf16[121,32,128]{2,1,0:T(8,128)(2,1)S(1)} %get-tuple-element.22.own_ref, bf16[241,32,128]{2,1,0:T(8,128)(2,1)S(1)} %collective-permute-done.other_ref), custom_call_target="tpu_custom_call" | custom-call | flops 15728640 | bytes 1048576 | tf_op jit(solution)/shard_map/products/pallas_call | solution.py:156
  15.4 5.5 %collective-permute-start.3 = (bf16[2,16,32,128]{3,2,1,0:T(8,128)(2,1)S(1)}, bf16[2,16,32,128]{3,2,1,0:T(8,128)(2,1)S(1)}, u32[]{:S(2)}, u32[]{:S(2)}) collective-permute-start(bf16[2,16,32,128]{3,2,1,0:T(8,128)(2,1)S(1)} %products.10), channel_id=1, source_target_pairs={{0,3},{1,0},{2,1},{3,2},{8,11},{9,8},{10,9},{11,10},{16,19},{17,16... | collective-permute-start | bytes 786440 | tf_op jit(solution)/shard_map/ppermute | solution.py:349
  20.9 2.4 %products.9 = bf16[2,16,32,128]{3,2,1,0:T(8,128)(2,1)S(1)} custom-call(bf16[121,32,128]{2,1,0:T(8,128)(2,1)S(1)} %get-tuple-element.20.own_ref, bf16[241,32,128]{2,1,0:T(8,128)(2,1)S(1)} %collective-permute-done.other_ref), custom_call_target="tpu_custom_call" | custom-call | flops 15728640 | bytes 1048576 | tf_op jit(solution)/shard_map/products/pallas_call | solution.py:156
  23.3 1.9 %collective-permute-start.2 = (bf16[2,16,32,128]{3,2,1,0:T(8,128)(2,1)S(1)}, bf16[2,16,32,128]{3,2,1,0:T(8,128)(2,1)S(1)}, u32[]{:S(2)}, u32[]{:S(2)}) collective-permute-start(bf16[2,16,32,128]{3,2,1,0:T(8,128)(2,1)S(1)} %products.9), channel_id=1, source_target_pairs={{0,1},{1,2},{2,3},{3,0},{8,9},{9,10},{10,11},{11,8},{16,17},{17,18... | collective-permute-start | bytes 786440 | tf_op jit(solution)/shard_map/ppermute | solution.py:349
  25.2 2.4 %products.8 = bf16[2,16,32,128]{3,2,1,0:T(8,128)(2,1)S(1)} custom-call(bf16[121,32,128]{2,1,0:T(8,128)(2,1)S(1)} %get-tuple-element.20.own_ref, bf16[241,32,128]{2,1,0:T(8,128)(2,1)S(1)} %collective-permute-done.other_ref), custom_call_target="tpu_custom_call" | custom-call | flops 15728640 | bytes 1048576 | tf_op jit(solution)/shard_map/products/pallas_call | solution.py:156
  27.6 2.9 %collective-permute-start.1 = (bf16[2,16,32,128]{3,2,1,0:T(8,128)(2,1)S(1)}, bf16[2,16,32,128]{3,2,1,0:T(8,128)(2,1)S(1)}, u32[]{:S(2)}, u32[]{:S(2)}) collective-permute-start(bf16[2,16,32,128]{3,2,1,0:T(8,128)(2,1)S(1)} %products.8), channel_id=1, source_target_pairs={{0,2},{1,3},{2,0},{3,1},{8,10},{9,11},{10,8},{11,9},{16,18},{17,19... | collective-permute-start | bytes 786440 | tf_op jit(solution)/shard_map/ppermute | solution.py:349
  30.5 2.4 %products.11.refs_3_ = f32[2,16,32,128]{3,2,1,0:T(8,128)S(1)} custom-call(bf16[121,32,128]{2,1,0:T(8,128)(2,1)S(1)} %get-tuple-element.22.own_ref, bf16[241,32,128]{2,1,0:T(8,128)(2,1)S(1)} %collective-permute-done.other_ref), custom_call_target="tpu_custom_call" | custom-call | flops 15728640 | bytes 1048576 | tf_op jit(solution)/shard_map/products/pallas_call | solution.py:156
  32.9 0.0 collective-permute-done.4.other_ref
  32.9 0.1 products.13
  33.1 0.7 %collective-permute-start.7 = (bf16[2,16,32,128]{3,2,1,0:T(8,128)(2,1)S(1)}, bf16[2,16,32,128]{3,2,1,0:T(8,128)(2,1)S(1)}, u32[]{:S(2)}, u32[]{:S(2)}) collective-permute-start(bf16[2,16,32,128]{3,2,1,0:T(8,128)(2,1)S(1)} %products.13), channel_id=1, source_target_pairs={{4,5},{5,6},{6,7},{7,4},{12,13},{13,14},{14,15},{15,12},{20,21},{2... | collective-permute-start | bytes 786440 | tf_op jit(solution)/shard_map/ppermute | solution.py:349
  33.8 0.1 products.12
  33.9 0.0 collective-permute-done.3.refs_2_
  33.9 0.7 %collective-permute-start.6 = (bf16[2,16,32,128]{3,2,1,0:T(8,128)(2,1)S(1)}, bf16[2,16,32,128]{3,2,1,0:T(8,128)(2,1)S(1)}, u32[]{:S(2)}, u32[]{:S(2)}) collective-permute-start(bf16[2,16,32,128]{3,2,1,0:T(8,128)(2,1)S(1)} %products.12), channel_id=1, source_target_pairs={{4,6},{5,7},{6,4},{7,5},{12,14},{13,15},{14,12},{15,13},{20,22},{2... | collective-permute-start | bytes 786440 | tf_op jit(solution)/shard_map/ppermute | solution.py:349
  34.6 0.0 collective-permute-done.2.refs_1_
  34.6 12.8 %collective-permute-done.1.refs_0_ = bf16[2,16,32,128]{3,2,1,0:T(8,128)(2,1)S(1)} collective-permute-done((bf16[2,16,32,128]{3,2,1,0:T(8,128)(2,1)S(1)}, bf16[2,16,32,128]{3,2,1,0:T(8,128)(2,1)S(1)}, u32[]{:S(2)}, u32[]{:S(2)}) %collective-permute-start.1) | collective-permute-done | bytes 262176 | tf_op jit(solution)/shard_map/ppermute | solution.py:349
  47.4 0.5 add_hours.2
  47.9 0.0 collective-permute-done.8.other_ref
  47.9 0.1 products.14
  48.1 0.7 %collective-permute-start.9 = (bf16[2,16,32,128]{3,2,1,0:T(8,128)(2,1)S(1)}, bf16[2,16,32,128]{3,2,1,0:T(8,128)(2,1)S(1)}, u32[]{:S(2)}, u32[]{:S(2)}) collective-permute-start(bf16[2,16,32,128]{3,2,1,0:T(8,128)(2,1)S(1)} %products.14), channel_id=1, source_target_pairs={{4,7},{5,4},{6,5},{7,6},{12,15},{13,12},{14,13},{15,14},{20,23},{2... | collective-permute-start | bytes 786440 | tf_op jit(solution)/shard_map/ppermute | solution.py:349
  48.8 1.3 %collective-permute-start.5 = (bf16[2,16,32,128]{3,2,1,0:T(8,128)(2,1)S(1)}, bf16[2,16,32,128]{3,2,1,0:T(8,128)(2,1)S(1)}, u32[]{:S(2)}, u32[]{:S(2)}) collective-permute-start(bf16[2,16,32,128]{3,2,1,0:T(8,128)(2,1)S(1)} %get-tuple-element.29), channel_id=1, source_target_pairs={{0,4},{8,12},{16,20},{24,28},{1,5},{9,13},{17,21},{25,29},{2,6},{1... | collective-permute-start | bytes 786440 | tf_op jit(solution)/shard_map/ppermute | solution.py:369
  50.1 0.1 products.15.refs_3_
  50.2 0.0 collective-permute-done.7.refs_1_
  50.2 0.0 collective-permute-done.6.refs_0_
  50.2 0.0 collective-permute-done.9.refs_2_
  50.3 1.3 %collective-permute-start.10 = (bf16[2,16,32,128]{3,2,1,0:T(8,128)(2,1)S(1)}, bf16[2,16,32,128]{3,2,1,0:T(8,128)(2,1)S(1)}, u32[]{:S(2)}, u32[]{:S(2)}) collective-permute-start(bf16[2,16,32,128]{3,2,1,0:T(8,128)(2,1)S(1)} %get-tuple-element.32.turned_ref), channel_id=1, source_target_pairs={{4,8},{12,16},{20,24},{28,0},{5,9},{13,17},{21,25},{29,1},{6,10},{... | collective-permute-start | bytes 786440 | tf_op jit(solution)/shard_map/ppermute | solution.py:374
  51.6 0.0 collective-permute-done.5.near_theirs
  51.6 7.3 %collective-permute-done.10.far_theirs = bf16[2,16,32,128]{3,2,1,0:T(8,128)(2,1)S(1)} collective-permute-done((bf16[2,16,32,128]{3,2,1,0:T(8,128)(2,1)S(1)}, bf16[2,16,32,128]{3,2,1,0:T(8,128)(2,1)S(1)}, u32[]{:S(2)}, u32[]{:S(2)}) %collective-permute-start.10) | collective-permute-done | bytes 262176 | tf_op jit(solution)/shard_map/ppermute | solution.py:374
  58.9 1.3 %assemble.1 = f32[2,16,64,128]{3,2,1,0:T(8,128)} custom-call(f32[2,8,128]{2,1,0:T(8,128)S(1)} %get-tuple-element.19.steps_ref, f32[2,16,32,128]{3,2,1,0:T(8,128)S(1)} %get-tuple-element.28.near_mine, bf16[2,16,32,128]{3,2,1,0:T(8,128)(2,1)S(1)} %collective-permute-done.5.near_theirs, f32[2,16,32,128]{3,2,1,0:T(8,128)S(1)} %get-tuple-element.31.far_mine, ...), custom_call_target="tpu_custom_call" | custom-call | tf_op jit(solution)/shard_map/assemble/pallas_call | solution.py:316
  (1 shorter events, 0.0 us)
Async XLA Ops:
  3.6 9.4 %collective-permute-start = (bf16[241,32,128]{2,1,0:T(8,128)(2,1)S(1)}, bf16[241,32,128]{2,1,0:T(8,128)(2,1)S(1)}, u32[]{:S(2)}, u32[]{:S(2)}) collective-permute-start(bf16[241,32,128]{2,1,0:T(8,128)(2,1)S(1)} %get-tuple-element.21.own_ref), channel_id=1, source_target_pairs={{4,0},{12,8},{20,16},{28,24},{5,1},{13,9},{21,17},{29,25},{6,2},{1... | collective-permute-start | bytes 5922824 | tf_op jit(solution)/shard_map/ppermute | solution.py:356
  4.9 28.0 %collective-permute-start.4 = (bf16[121,32,128]{2,1,0:T(8,128)(2,1)S(1)}, bf16[121,32,128]{2,1,0:T(8,128)(2,1)S(1)}, u32[]{:S(2)}, u32[]{:S(2)}) collective-permute-start(bf16[121,32,128]{2,1,0:T(8,128)(2,1)S(1)} %get-tuple-element.20.own_ref), channel_id=1, source_target_pairs={{8,4},{16,12},{24,20},{0,28},{9,5},{17,13},{25,21},{1,29},{10,6},{... | collective-permute-start | bytes 2973704 | tf_op jit(solution)/shard_map/ppermute | solution.py:357
  11.6 36.3 %collective-permute-start.8 = (bf16[121,32,128]{2,1,0:T(8,128)(2,1)S(1)}, bf16[121,32,128]{2,1,0:T(8,128)(2,1)S(1)}, u32[]{:S(2)}, u32[]{:S(2)}) collective-permute-start(bf16[121,32,128]{2,1,0:T(8,128)(2,1)S(1)} %get-tuple-element.22.own_ref), channel_id=1, source_target_pairs={{8,4},{16,12},{24,20},{0,28},{9,5},{17,13},{25,21},{1,29},{10,6},{... | collective-permute-start | bytes 2973704 | tf_op jit(solution)/shard_map/ppermute | solution.py:357
  15.4 18.5 %collective-permute-start.3 = (bf16[2,16,32,128]{3,2,1,0:T(8,128)(2,1)S(1)}, bf16[2,16,32,128]{3,2,1,0:T(8,128)(2,1)S(1)}, u32[]{:S(2)}, u32[]{:S(2)}) collective-permute-start(bf16[2,16,32,128]{3,2,1,0:T(8,128)(2,1)S(1)} %products.10), channel_id=1, source_target_pairs={{0,3},{1,0},{2,1},{3,2},{8,11},{9,8},{10,9},{11,10},{16,19},{17,16... | collective-permute-start | bytes 786440 | tf_op jit(solution)/shard_map/ppermute | solution.py:349
  23.3 11.3 %collective-permute-start.2 = (bf16[2,16,32,128]{3,2,1,0:T(8,128)(2,1)S(1)}, bf16[2,16,32,128]{3,2,1,0:T(8,128)(2,1)S(1)}, u32[]{:S(2)}, u32[]{:S(2)}) collective-permute-start(bf16[2,16,32,128]{3,2,1,0:T(8,128)(2,1)S(1)} %products.9), channel_id=1, source_target_pairs={{0,1},{1,2},{2,3},{3,0},{8,9},{9,10},{10,11},{11,8},{16,17},{17,18... | collective-permute-start | bytes 786440 | tf_op jit(solution)/shard_map/ppermute | solution.py:349
  27.6 19.8 %collective-permute-start.1 = (bf16[2,16,32,128]{3,2,1,0:T(8,128)(2,1)S(1)}, bf16[2,16,32,128]{3,2,1,0:T(8,128)(2,1)S(1)}, u32[]{:S(2)}, u32[]{:S(2)}) collective-permute-start(bf16[2,16,32,128]{3,2,1,0:T(8,128)(2,1)S(1)} %products.8), channel_id=1, source_target_pairs={{0,2},{1,3},{2,0},{3,1},{8,10},{9,11},{10,8},{11,9},{16,18},{17,19... | collective-permute-start | bytes 786440 | tf_op jit(solution)/shard_map/ppermute | solution.py:349
  33.1 17.1 %collective-permute-start.7 = (bf16[2,16,32,128]{3,2,1,0:T(8,128)(2,1)S(1)}, bf16[2,16,32,128]{3,2,1,0:T(8,128)(2,1)S(1)}, u32[]{:S(2)}, u32[]{:S(2)}) collective-permute-start(bf16[2,16,32,128]{3,2,1,0:T(8,128)(2,1)S(1)} %products.13), channel_id=1, source_target_pairs={{4,5},{5,6},{6,7},{7,4},{12,13},{13,14},{14,15},{15,12},{20,21},{2... | collective-permute-start | bytes 786440 | tf_op jit(solution)/shard_map/ppermute | solution.py:349
  33.9 16.3 %collective-permute-start.6 = (bf16[2,16,32,128]{3,2,1,0:T(8,128)(2,1)S(1)}, bf16[2,16,32,128]{3,2,1,0:T(8,128)(2,1)S(1)}, u32[]{:S(2)}, u32[]{:S(2)}) collective-permute-start(bf16[2,16,32,128]{3,2,1,0:T(8,128)(2,1)S(1)} %products.12), channel_id=1, source_target_pairs={{4,6},{5,7},{6,4},{7,5},{12,14},{13,15},{14,12},{15,13},{20,22},{2... | collective-permute-start | bytes 786440 | tf_op jit(solution)/shard_map/ppermute | solution.py:349
  48.1 2.2 %collective-permute-start.9 = (bf16[2,16,32,128]{3,2,1,0:T(8,128)(2,1)S(1)}, bf16[2,16,32,128]{3,2,1,0:T(8,128)(2,1)S(1)}, u32[]{:S(2)}, u32[]{:S(2)}) collective-permute-start(bf16[2,16,32,128]{3,2,1,0:T(8,128)(2,1)S(1)} %products.14), channel_id=1, source_target_pairs={{4,7},{5,4},{6,5},{7,6},{12,15},{13,12},{14,13},{15,14},{20,23},{2... | collective-permute-start | bytes 786440 | tf_op jit(solution)/shard_map/ppermute | solution.py:349
  48.8 2.8 %collective-permute-start.5 = (bf16[2,16,32,128]{3,2,1,0:T(8,128)(2,1)S(1)}, bf16[2,16,32,128]{3,2,1,0:T(8,128)(2,1)S(1)}, u32[]{:S(2)}, u32[]{:S(2)}) collective-permute-start(bf16[2,16,32,128]{3,2,1,0:T(8,128)(2,1)S(1)} %get-tuple-element.29), channel_id=1, source_target_pairs={{0,4},{8,12},{16,20},{24,28},{1,5},{9,13},{17,21},{25,29},{2,6},{1... | collective-permute-start | bytes 786440 | tf_op jit(solution)/shard_map/ppermute | solution.py:369
  50.3 8.6 %collective-permute-start.10 = (bf16[2,16,32,128]{3,2,1,0:T(8,128)(2,1)S(1)}, bf16[2,16,32,128]{3,2,1,0:T(8,128)(2,1)S(1)}, u32[]{:S(2)}, u32[]{:S(2)}) collective-permute-start(bf16[2,16,32,128]{3,2,1,0:T(8,128)(2,1)S(1)} %get-tuple-element.32.turned_ref), channel_id=1, source_target_pairs={{4,8},{12,16},{20,24},{28,0},{5,9},{13,17},{21,25},{29,1},{6,10},{... | collective-permute-start | bytes 786440 | tf_op jit(solution)/shard_map/ppermute | solution.py:374

commit v6 on v4

--- a/solution.py
+++ b/solution.py
@@ -319,13 +319,15 @@
     far_made = []
     for k in range(hours):
         batch, place = divmod(k, BATCH)
-        if k == (hours // BATCH - 1) * BATCH:
-            near_mine, turned = add_hours(after(near_parts, *far_made), scale)
-            near_theirs = lax.ppermute(turned, "sta", on_chip)
-            far_others[batch] = after(far_others[batch], near_mine)
+        if place == 0 and k:
+            far_others[batch] = after(far_others[batch], *far_made)
+        if k == 1:
+            far_others[batch] = after(far_others[batch], near_parts[0], far_made[0])
         far_made.append(far_product(far, k, far_others[batch], near[batch], place, windows, dtypes[k]))
     far_parts = [to_owner(part, d) for part, d in zip(far_made, ORDER)]
-    far_mine, turned = add_hours(far_parts, scale)
+    near_mine, turned = add_hours(after(near_parts[::-1], *far_made), scale)
+    near_theirs = lax.ppermute(turned, "sta", on_chip)
+    far_mine, turned = add_hours(after(far_parts[::-1], near_mine), scale)
     far_theirs = lax.ppermute(turned, "sta", across)
     cross = assemble(steps, (near_mine, near_theirs), (far_mine, far_theirs), turned)
     cross = cross.reshape(pairs, stations, stations, tiles // hours, 2, LANES)

time: 52.1 us -> 51.1 us (0.981)
  the two profiles are of different devices: /device:TPU:1 before, /device:TPU:3 now
where the time goes in v6:
time: 51.1 us; the launch traced here: 51 us
  starting transfers between devices  22.5 us (44%)
  Pallas kernels  15.3 us (30%)
  waiting for transfers between devices  13 us (25%)
    ppermute x6, starting transfers between devices, to_owner(): lax.ppermute(part, 'hour', [(h, (h + d) % hours) for h in range(hours)])  10.7 us
    pallas_call x8, Pallas kernels, product_call(): pl.pallas_call(body, in_specs=[VMEM] * len(operands), out_specs=VMEM, out...  9.98 us
    ppermute x2, starting transfers between devices, per_device(): far_others = [lax.ppermute(one, 'sta', across) for one in near]  6.45 us
    ppermute x2, waiting for transfers between devices, per_device(): far_others = [lax.ppermute(one, 'sta', across) for one in near]  5.27 us
    ppermute x1, starting transfers between devices, per_device(): far_theirs = lax.ppermute(turned, 'sta', across)  4.48 us
    ppermute x6, waiting for transfers between devices, to_owner(): lax.ppermute(part, 'hour', [(h, (h + d) % hours) for h in range(hours)])  3.92 us
    ppermute x1, waiting for transfers between devices, per_device(): far_theirs = lax.ppermute(turned, 'sta', across)  3.77 us
    pallas_call x1, Pallas kernels, whiten(): pl.pallas_call(body, in_specs=[hbm] * 4, out_specs=[VMEM] * (batches + 2)...  3.53 us
  transfers between devices with their start and end apart: 11, of which 4 were waited for; matrix products, arithmetic and copies ran while one was open for 0% of the time, Pallas kernels for 21%

profile of v6, /device:TPU:3, one launch (start us, length us, event | category | flops | bytes accessed | tf_op | source)
XLA Modules:
  0.0 51.0 jit_solution(11560657086303252774)
XLA Ops:
  0.0 3.5 %whiten.1 = (bf16[60,32,128]{2,1,0:T(8,128)(2,1)S(1)}, bf16[60,32,128]{2,1,0:T(8,128)(2,1)S(1)}, bf16[121,32,128]{2,1,0:T(8,128)(2,1)S(1)}, f32[2,8,128]{2,1,0:T(8,128)S(1)}) custom-call(s32[1,16]{1,0:T(1,128)} %order_hbm.1, s32[2,2]{1,0:T(2,128)} %pairs_hbm.1, f32[8,128]{1,0:T(8,128)} %bitcast.12, bf16[16,30,16,128]{3,2,1,0:T(8,128)(2,1)} %bitcast.11), custom_call_target="tpu_custom_call" | custom-call | tf_op jit(solution)/shard_map/whiten/pallas_call | solution.py:93
  3.5 0.7 %collective-permute-start = (bf16[121,32,128]{2,1,0:T(8,128)(2,1)S(1)}, bf16[121,32,128]{2,1,0:T(8,128)(2,1)S(1)}, u32[]{:S(2)}, u32[]{:S(2)}) collective-permute-start(bf16[121,32,128]{2,1,0:T(8,128)(2,1)S(1)} %get-tuple-element.26.own_ref), channel_id=1, source_target_pairs={{0,4},{4,0},{8,12},{12,8},{16,20},{20,16},{24,28},{28,24},{1,5},{5... | collective-permute-start | bytes 2973704 | tf_op jit(solution)/shard_map/ppermute | solution.py:308
  4.3 3.0 %collective-permute-start.4 = (bf16[60,32,128]{2,1,0:T(8,128)(2,1)S(1)}, bf16[60,32,128]{2,1,0:T(8,128)(2,1)S(1)}, u32[]{:S(2)}, u32[]{:S(2)}) collective-permute-start(bf16[60,32,128]{2,1,0:T(8,128)(2,1)S(1)} %get-tuple-element.27.own_ref.near_ref), channel_id=1, source_target_pairs={{4,8},{8,4},{12,16},{16,12},{20,24},{24,20},{5,9},{9,5},{13,17},{1... | collective-permute-start | bytes 1474568 | tf_op jit(solution)/shard_map/ppermute | solution.py:309
  7.3 3.4 %collective-permute-start.5 = (bf16[60,32,128]{2,1,0:T(8,128)(2,1)S(1)}, bf16[60,32,128]{2,1,0:T(8,128)(2,1)S(1)}, u32[]{:S(2)}, u32[]{:S(2)}) collective-permute-start(bf16[60,32,128]{2,1,0:T(8,128)(2,1)S(1)} %get-tuple-element.25.own_ref.near_ref), channel_id=1, source_target_pairs={{4,8},{8,4},{12,16},{16,12},{20,24},{24,20},{5,9},{9,5},{13,17},{1... | collective-permute-start | bytes 1474568 | tf_op jit(solution)/shard_map/ppermute | solution.py:309
  10.7 0.0 collective-permute-done.other_ref
  10.8 1.2 %products.11 = bf16[16,32,128]{2,1,0:T(8,128)(2,1)S(1)} custom-call(bf16[60,32,128]{2,1,0:T(8,128)(2,1)S(1)} %get-tuple-element.27.own_ref.near_ref, bf16[121,32,128]{2,1,0:T(8,128)(2,1)S(1)} %collective-permute-done.other_ref), custom_call_target="tpu_custom_call" | custom-call | flops 7864320 | bytes 524288 | tf_op jit(solution)/shard_map/products/pallas_call | solution.py:146
  12.0 2.4 %collective-permute-start.3 = (bf16[16,32,128]{2,1,0:T(8,128)(2,1)S(1)}, bf16[16,32,128]{2,1,0:T(8,128)(2,1)S(1)}, u32[]{:S(2)}, u32[]{:S(2)}) collective-permute-start(bf16[16,32,128]{2,1,0:T(8,128)(2,1)S(1)} %products.11), channel_id=1, source_target_pairs={{0,2},{1,3},{2,0},{3,1},{4,6},{5,7},{6,4},{7,5},{8,10},{9,11},{10,... | collective-permute-start | bytes 393224 | tf_op jit(solution)/shard_map/ppermute | solution.py:303
  14.3 1.2 %products.10 = bf16[16,32,128]{2,1,0:T(8,128)(2,1)S(1)} custom-call(bf16[60,32,128]{2,1,0:T(8,128)(2,1)S(1)} %get-tuple-element.27.own_ref.near_ref, bf16[121,32,128]{2,1,0:T(8,128)(2,1)S(1)} %collective-permute-done.other_ref), custom_call_target="tpu_custom_call" | custom-call | flops 7864320 | bytes 524288 | tf_op jit(solution)/shard_map/products/pallas_call | solution.py:146
  15.5 1.3 %collective-permute-start.2 = (bf16[16,32,128]{2,1,0:T(8,128)(2,1)S(1)}, bf16[16,32,128]{2,1,0:T(8,128)(2,1)S(1)}, u32[]{:S(2)}, u32[]{:S(2)}) collective-permute-start(bf16[16,32,128]{2,1,0:T(8,128)(2,1)S(1)} %products.10), channel_id=1, source_target_pairs={{0,1},{1,2},{2,3},{3,0},{4,5},{5,6},{6,7},{7,4},{8,9},{9,10},{10,1... | collective-permute-start | bytes 393224 | tf_op jit(solution)/shard_map/ppermute | solution.py:303
  16.9 1.2 %products.9 = bf16[16,32,128]{2,1,0:T(8,128)(2,1)S(1)} custom-call(bf16[60,32,128]{2,1,0:T(8,128)(2,1)S(1)} %get-tuple-element.25.own_ref.near_ref, bf16[121,32,128]{2,1,0:T(8,128)(2,1)S(1)} %collective-permute-done.other_ref), custom_call_target="tpu_custom_call" | custom-call | flops 7864320 | bytes 524288 | tf_op jit(solution)/shard_map/products/pallas_call | solution.py:146
  18.1 2.0 %collective-permute-start.1 = (bf16[16,32,128]{2,1,0:T(8,128)(2,1)S(1)}, bf16[16,32,128]{2,1,0:T(8,128)(2,1)S(1)}, u32[]{:S(2)}, u32[]{:S(2)}) collective-permute-start(bf16[16,32,128]{2,1,0:T(8,128)(2,1)S(1)} %products.9), channel_id=1, source_target_pairs={{0,3},{1,0},{2,1},{3,2},{4,7},{5,4},{6,5},{7,6},{8,11},{9,8},{10,9... | collective-permute-start | bytes 393224 | tf_op jit(solution)/shard_map/ppermute | solution.py:303
  20.1 1.2 %products.8.refs_0_ = f32[16,32,128]{2,1,0:T(8,128)S(1)} custom-call(bf16[60,32,128]{2,1,0:T(8,128)(2,1)S(1)} %get-tuple-element.25.own_ref.near_ref, bf16[121,32,128]{2,1,0:T(8,128)(2,1)S(1)} %collective-permute-done.other_ref), custom_call_target="tpu_custom_call" | custom-call | flops 7864320 | bytes 524288 | tf_op jit(solution)/shard_map/products/pallas_call | solution.py:146
  21.3 0.0 collective-permute-done.4.other_ref
  21.3 1.3 %products.12 = bf16[16,32,128]{2,1,0:T(8,128)(2,1)S(1)} custom-call(bf16[121,32,128]{2,1,0:T(8,128)(2,1)S(1)} %get-tuple-element.26.own_ref, bf16[60,32,128]{2,1,0:T(8,128)(2,1)S(1)} %collective-permute-done.4.other_ref, bf16[60,32,128]{2,1,0:T(8,128)(2,1)S(1)} %get-tuple-element.27.own_ref.near_ref), custom_call_target="tpu_custom_call" | custom-call | flops 7864320 | bytes 524288 | tf_op jit(solution)/shard_map/products/pallas_call | solution.py:146
  22.6 1.6 %collective-permute-start.9 = (bf16[16,32,128]{2,1,0:T(8,128)(2,1)S(1)}, bf16[16,32,128]{2,1,0:T(8,128)(2,1)S(1)}, u32[]{:S(2)}, u32[]{:S(2)}) collective-permute-start(bf16[16,32,128]{2,1,0:T(8,128)(2,1)S(1)} %products.12), channel_id=1, source_target_pairs={{0,2},{1,3},{2,0},{3,1},{4,6},{5,7},{6,4},{7,5},{8,10},{9,11},{10,... | collective-permute-start | bytes 393224 | tf_op jit(solution)/shard_map/ppermute | solution.py:303
  24.2 0.0 collective-permute-done.3.refs_3_
  24.2 1.3 %products.13 = bf16[16,32,128]{2,1,0:T(8,128)(2,1)S(1)} custom-call(bf16[121,32,128]{2,1,0:T(8,128)(2,1)S(1)} %get-tuple-element.26.own_ref, bf16[60,32,128]{2,1,0:T(8,128)(2,1)S(1)} %collective-permute-done.4.other_ref, bf16[60,32,128]{2,1,0:T(8,128)(2,1)S(1)} %get-tuple-element.27.own_ref.near_ref), custom_call_target="tpu_custom_call" | custom-call | flops 7864320 | bytes 524288 | tf_op jit(solution)/shard_map/products/pallas_call | solution.py:146
  25.5 5.3 %collective-permute-done.5.other_ref = bf16[60,32,128]{2,1,0:T(8,128)(2,1)S(1)} collective-permute-done((bf16[60,32,128]{2,1,0:T(8,128)(2,1)S(1)}, bf16[60,32,128]{2,1,0:T(8,128)(2,1)S(1)}, u32[]{:S(2)}, u32[]{:S(2)}) %collective-permute-start.5) | collective-permute-done | bytes 491552 | tf_op jit(solution)/shard_map/ppermute | solution.py:309
  30.8 1.3 %products.14 = bf16[16,32,128]{2,1,0:T(8,128)(2,1)S(1)} custom-call(bf16[121,32,128]{2,1,0:T(8,128)(2,1)S(1)} %get-tuple-element.26.own_ref, bf16[60,32,128]{2,1,0:T(8,128)(2,1)S(1)} %collective-permute-done.5.other_ref, bf16[60,32,128]{2,1,0:T(8,128)(2,1)S(1)} %get-tuple-element.25.own_ref.near_ref), custom_call_target="tpu_custom_call" | custom-call | flops 7864320 | bytes 524288 | tf_op jit(solution)/shard_map/products/pallas_call | solution.py:146
  32.1 3.4 %collective-permute-start.7 = (bf16[16,32,128]{2,1,0:T(8,128)(2,1)S(1)}, bf16[16,32,128]{2,1,0:T(8,128)(2,1)S(1)}, u32[]{:S(2)}, u32[]{:S(2)}) collective-permute-start(bf16[16,32,128]{2,1,0:T(8,128)(2,1)S(1)} %products.14), channel_id=1, source_target_pairs={{0,3},{1,0},{2,1},{3,2},{4,7},{5,4},{6,5},{7,6},{8,11},{9,8},{10,9... | collective-permute-start | bytes 393224 | tf_op jit(solution)/shard_map/ppermute | solution.py:303
  35.5 0.0 collective-permute-start.8
  35.5 1.3 %products.15.refs_0_ = f32[16,32,128]{2,1,0:T(8,128)S(1)} custom-call(bf16[121,32,128]{2,1,0:T(8,128)(2,1)S(1)} %get-tuple-element.26.own_ref, bf16[60,32,128]{2,1,0:T(8,128)(2,1)S(1)} %collective-permute-done.5.other_ref, bf16[60,32,128]{2,1,0:T(8,128)(2,1)S(1)} %get-tuple-element.25.own_ref.near_ref), custom_call_target="tpu_custom_call" | custom-call | flops 7864320 | bytes 524288 | tf_op jit(solution)/shard_map/products/pallas_call | solution.py:146
  36.8 0.0 collective-permute-done.2.refs_2_
  36.8 0.0 collective-permute-done.1.refs_1_
  36.8 0.3 add_hours.2
  37.1 0.1 collective-permute-start.6
  37.2 0.0 collective-permute-done.9.refs_3_
  37.2 1.4 %collective-permute-done.7.refs_1_ = bf16[16,32,128]{2,1,0:T(8,128)(2,1)S(1)} collective-permute-done((bf16[16,32,128]{2,1,0:T(8,128)(2,1)S(1)}, bf16[16,32,128]{2,1,0:T(8,128)(2,1)S(1)}, u32[]{:S(2)}, u32[]{:S(2)}) %collective-permute-start.7) | collective-permute-done | bytes 131104 | tf_op jit(solution)/shard_map/ppermute | solution.py:303
  38.6 2.5 %collective-permute-done.8.refs_2_ = bf16[16,32,128]{2,1,0:T(8,128)(2,1)S(1)} collective-permute-done((bf16[16,32,128]{2,1,0:T(8,128)(2,1)S(1)}, bf16[16,32,128]{2,1,0:T(8,128)(2,1)S(1)}, u32[]{:S(2)}, u32[]{:S(2)}) %collective-permute-start.8) | collective-permute-done | bytes 131104 | tf_op jit(solution)/shard_map/ppermute | solution.py:303
  41.1 0.3 add_hours.3
  41.4 4.5 %collective-permute-start.10 = (bf16[16,32,128]{2,1,0:T(8,128)(2,1)S(1)}, bf16[16,32,128]{2,1,0:T(8,128)(2,1)S(1)}, u32[]{:S(2)}, u32[]{:S(2)}) collective-permute-start(bf16[16,32,128]{2,1,0:T(8,128)(2,1)S(1)} %get-tuple-element.42.turned_ref), channel_id=1, source_target_pairs={{4,8},{8,4},{12,16},{16,12},{20,24},{24,20},{5,9},{9,5},{13,17},{1... | collective-permute-start | bytes 393224 | tf_op jit(solution)/shard_map/ppermute | solution.py:331
  45.9 0.0 collective-permute-done.6.near_theirs
  45.9 3.8 %collective-permute-done.10.far_theirs = bf16[16,32,128]{2,1,0:T(8,128)(2,1)S(1)} collective-permute-done((bf16[16,32,128]{2,1,0:T(8,128)(2,1)S(1)}, bf16[16,32,128]{2,1,0:T(8,128)(2,1)S(1)}, u32[]{:S(2)}, u32[]{:S(2)}) %collective-permute-start.10) | collective-permute-done | bytes 131104 | tf_op jit(solution)/shard_map/ppermute | solution.py:331
  49.7 1.3 %assemble.1 = f32[2,16,64,128]{3,2,1,0:T(8,128)} custom-call(f32[2,8,128]{2,1,0:T(8,128)S(1)} %get-tuple-element.24.steps_ref, f32[16,32,128]{2,1,0:T(8,128)S(1)} %get-tuple-element.35.near_mine, bf16[16,32,128]{2,1,0:T(8,128)(2,1)S(1)} %collective-permute-done.6.near_theirs, f32[16,32,128]{2,1,0:T(8,128)S(1)} %get-tuple-element.41.far_mine, ...), custom_call_target="tpu_custom_call" | custom-call | tf_op jit(solution)/shard_map/assemble/pallas_call | solution.py:281
Async XLA Ops:
  3.5 7.2 %collective-permute-start = (bf16[121,32,128]{2,1,0:T(8,128)(2,1)S(1)}, bf16[121,32,128]{2,1,0:T(8,128)(2,1)S(1)}, u32[]{:S(2)}, u32[]{:S(2)}) collective-permute-start(bf16[121,32,128]{2,1,0:T(8,128)(2,1)S(1)} %get-tuple-element.26.own_ref), channel_id=1, source_target_pairs={{0,4},{4,0},{8,12},{12,8},{16,20},{20,16},{24,28},{28,24},{1,5},{5... | collective-permute-start | bytes 2973704 | tf_op jit(solution)/shard_map/ppermute | solution.py:308
  4.3 17.0 %collective-permute-start.4 = (bf16[60,32,128]{2,1,0:T(8,128)(2,1)S(1)}, bf16[60,32,128]{2,1,0:T(8,128)(2,1)S(1)}, u32[]{:S(2)}, u32[]{:S(2)}) collective-permute-start(bf16[60,32,128]{2,1,0:T(8,128)(2,1)S(1)} %get-tuple-element.27.own_ref.near_ref), channel_id=1, source_target_pairs={{4,8},{8,4},{12,16},{16,12},{20,24},{24,20},{5,9},{9,5},{13,17},{1... | collective-permute-start | bytes 1474568 | tf_op jit(solution)/shard_map/ppermute | solution.py:309
  7.3 23.5 %collective-permute-start.5 = (bf16[60,32,128]{2,1,0:T(8,128)(2,1)S(1)}, bf16[60,32,128]{2,1,0:T(8,128)(2,1)S(1)}, u32[]{:S(2)}, u32[]{:S(2)}) collective-permute-start(bf16[60,32,128]{2,1,0:T(8,128)(2,1)S(1)} %get-tuple-element.25.own_ref.near_ref), channel_id=1, source_target_pairs={{4,8},{8,4},{12,16},{16,12},{20,24},{24,20},{5,9},{9,5},{13,17},{1... | collective-permute-start | bytes 1474568 | tf_op jit(solution)/shard_map/ppermute | solution.py:309
  12.0 12.3 %collective-permute-start.3 = (bf16[16,32,128]{2,1,0:T(8,128)(2,1)S(1)}, bf16[16,32,128]{2,1,0:T(8,128)(2,1)S(1)}, u32[]{:S(2)}, u32[]{:S(2)}) collective-permute-start(bf16[16,32,128]{2,1,0:T(8,128)(2,1)S(1)} %products.11), channel_id=1, source_target_pairs={{0,2},{1,3},{2,0},{3,1},{4,6},{5,7},{6,4},{7,5},{8,10},{9,11},{10,... | collective-permute-start | bytes 393224 | tf_op jit(solution)/shard_map/ppermute | solution.py:303
  15.5 21.3 %collective-permute-start.2 = (bf16[16,32,128]{2,1,0:T(8,128)(2,1)S(1)}, bf16[16,32,128]{2,1,0:T(8,128)(2,1)S(1)}, u32[]{:S(2)}, u32[]{:S(2)}) collective-permute-start(bf16[16,32,128]{2,1,0:T(8,128)(2,1)S(1)} %products.10), channel_id=1, source_target_pairs={{0,1},{1,2},{2,3},{3,0},{4,5},{5,6},{6,7},{7,4},{8,9},{9,10},{10,1... | collective-permute-start | bytes 393224 | tf_op jit(solution)/shard_map/ppermute | solution.py:303
  18.1 18.8 %collective-permute-start.1 = (bf16[16,32,128]{2,1,0:T(8,128)(2,1)S(1)}, bf16[16,32,128]{2,1,0:T(8,128)(2,1)S(1)}, u32[]{:S(2)}, u32[]{:S(2)}) collective-permute-start(bf16[16,32,128]{2,1,0:T(8,128)(2,1)S(1)} %products.9), channel_id=1, source_target_pairs={{0,3},{1,0},{2,1},{3,2},{4,7},{5,4},{6,5},{7,6},{8,11},{9,8},{10,9... | collective-permute-start | bytes 393224 | tf_op jit(solution)/shard_map/ppermute | solution.py:303
  22.6 14.6 %collective-permute-start.9 = (bf16[16,32,128]{2,1,0:T(8,128)(2,1)S(1)}, bf16[16,32,128]{2,1,0:T(8,128)(2,1)S(1)}, u32[]{:S(2)}, u32[]{:S(2)}) collective-permute-start(bf16[16,32,128]{2,1,0:T(8,128)(2,1)S(1)} %products.12), channel_id=1, source_target_pairs={{0,2},{1,3},{2,0},{3,1},{4,6},{5,7},{6,4},{7,5},{8,10},{9,11},{10,... | collective-permute-start | bytes 393224 | tf_op jit(solution)/shard_map/ppermute | solution.py:303
  32.1 6.5 %collective-permute-start.7 = (bf16[16,32,128]{2,1,0:T(8,128)(2,1)S(1)}, bf16[16,32,128]{2,1,0:T(8,128)(2,1)S(1)}, u32[]{:S(2)}, u32[]{:S(2)}) collective-permute-start(bf16[16,32,128]{2,1,0:T(8,128)(2,1)S(1)} %products.14), channel_id=1, source_target_pairs={{0,3},{1,0},{2,1},{3,2},{4,7},{5,4},{6,5},{7,6},{8,11},{9,8},{10,9... | collective-permute-start | bytes 393224 | tf_op jit(solution)/shard_map/ppermute | solution.py:303
  35.5 5.6 %collective-permute-start.8 = (bf16[16,32,128]{2,1,0:T(8,128)(2,1)S(1)}, bf16[16,32,128]{2,1,0:T(8,128)(2,1)S(1)}, u32[]{:S(2)}, u32[]{:S(2)}) collective-permute-start(bf16[16,32,128]{2,1,0:T(8,128)(2,1)S(1)} %products.13), channel_id=1, source_target_pairs={{0,1},{1,2},{2,3},{3,0},{4,5},{5,6},{6,7},{7,4},{8,9},{9,10},{10,1... | collective-permute-start | bytes 393224 | tf_op jit(solution)/shard_map/ppermute | solution.py:303
  37.1 8.8 %collective-permute-start.6 = (bf16[16,32,128]{2,1,0:T(8,128)(2,1)S(1)}, bf16[16,32,128]{2,1,0:T(8,128)(2,1)S(1)}, u32[]{:S(2)}, u32[]{:S(2)}) collective-permute-start(bf16[16,32,128]{2,1,0:T(8,128)(2,1)S(1)} %get-tuple-element.36), channel_id=1, source_target_pairs={{0,4},{4,0},{8,12},{12,8},{16,20},{20,16},{24,28},{28,24},{1,5},{5... | collective-permute-start | bytes 393224 | tf_op jit(solution)/shard_map/ppermute | solution.py:329
  41.4 8.3 %collective-permute-start.10 = (bf16[16,32,128]{2,1,0:T(8,128)(2,1)S(1)}, bf16[16,32,128]{2,1,0:T(8,128)(2,1)S(1)}, u32[]{:S(2)}, u32[]{:S(2)}) collective-permute-start(bf16[16,32,128]{2,1,0:T(8,128)(2,1)S(1)} %get-tuple-element.42.turned_ref), channel_id=1, source_target_pairs={{4,8},{8,4},{12,16},{16,12},{20,24},{24,20},{5,9},{9,5},{13,17},{1... | collective-permute-start | bytes 393224 | tf_op jit(solution)/shard_map/ppermute | solution.py:331

commit v7 on v6

--- a/solution.py
+++ b/solution.py
@@ -306,7 +306,7 @@
         return lax.optimization_barrier((value, earlier))[0]
 
     near_others = lax.ppermute(far, "sta", on_chip)
-    far_others = [lax.ppermute(one, "sta", across) for one in near]
+    far_others = [lax.ppermute(near[0], "sta", across)]
     dtypes = [jnp.bfloat16 if d else WIDE for d in ORDER]
     scale = 1.0 / (hours * windows)
 
@@ -314,6 +314,7 @@
         near_product(near[k // BATCH], k % BATCH, near_others, k, windows, dtypes[k])
         for k in range(hours)
     ]
+    far_others.append(lax.ppermute(after(near[1], *near_made[:1]), "sta", across))
     near_parts = [to_owner(part, d) for part, d in zip(near_made, ORDER)]
     far_others[0] = after(far_others[0], *near_made)
     far_made = []

time: 51.1 us -> 47.5 us (0.930); the launches traced: 51 us -> 46.7 us
  waiting for transfers between devices: 13 us -> 7.86 us
  starting transfers between devices: 22.5 us -> 23.3 us
    ppermute x6, waiting for transfers between devices: 3.92 us -> 0.35 us  [to_owner(): lax.ppermute(part, 'hour', [(h, (h + d) % hours) for h in range(hours)])]
    ppermute x2, waiting for transfers between devices: 5.27 us -> 3.72 us  [the longest x1 3.72 us: per_device(): lax.ppermute(after(near[1], *near_made[:1]), 'sta', across)]
    ppermute x6, starting transfers between devices: 10.7 us -> 12.3 us  [to_owner(): lax.ppermute(part, 'hour', [(h, (h + d) % hours) for h in range(hours)])]
    ppermute x1, starting transfers between devices: 4.48 us -> 3.79 us  [per_device(): far_theirs = lax.ppermute(turned, 'sta', across)]
  transfers between devices with their start and end apart: 11 -> 11, of which waited for: 4 -> 3; matrix products, arithmetic and copies ran while one was open for 0% -> 0% of each run, Pallas kernels for 21% -> 23%
where the time goes in v7:
time: 47.5 us; the launch traced here: 46.7 us
  starting transfers between devices  23.3 us (49%)
  Pallas kernels  15.3 us (32%)
  waiting for transfers between devices  7.86 us (17%)
    ppermute x6, starting transfers between devices, to_owner(): lax.ppermute(part, 'hour', [(h, (h + d) % hours) for h in range(hours)])  12.3 us
    pallas_call x8, Pallas kernels, product_call(): pl.pallas_call(body, in_specs=[VMEM] * len(operands), out_specs=VMEM, out...  9.97 us
    ppermute x1, starting transfers between devices, per_device(): far_theirs = lax.ppermute(turned, 'sta', across)  3.79 us
    ppermute x1, waiting for transfers between devices, per_device(): far_theirs = lax.ppermute(turned, 'sta', across)  3.77 us
    ppermute x1, waiting for transfers between devices, per_device(): lax.ppermute(after(near[1], *near_made[:1]), 'sta', across)  3.72 us
    pallas_call x1, Pallas kernels, whiten(): pl.pallas_call(body, in_specs=[hbm] * 4, out_specs=[VMEM] * (batches + 2)...  3.53 us
    ppermute x1, starting transfers between devices, per_device(): lax.ppermute(after(near[1], *near_made[:1]), 'sta', across)  3.43 us
    ppermute x1, starting transfers between devices, per_device(): far_others = [lax.ppermute(near[0], 'sta', across)]  3.02 us
  transfers between devices with their start and end apart: 11, of which 3 were waited for; matrix products, arithmetic and copies ran while one was open for 0% of the time, Pallas kernels for 23%

profile of v7, /device:TPU:3, one launch (start us, length us, event | category | flops | bytes accessed | tf_op | source)
XLA Modules:
  0.0 46.7 jit_solution(240102716004766923)
XLA Ops:
  0.0 3.5 %whiten.1 = (bf16[60,32,128]{2,1,0:T(8,128)(2,1)S(1)}, bf16[60,32,128]{2,1,0:T(8,128)(2,1)S(1)}, bf16[121,32,128]{2,1,0:T(8,128)(2,1)S(1)}, f32[2,8,128]{2,1,0:T(8,128)S(1)}) custom-call(s32[1,16]{1,0:T(1,128)} %order_hbm.1, s32[2,2]{1,0:T(2,128)} %pairs_hbm.1, f32[8,128]{1,0:T(8,128)} %bitcast.12, bf16[16,30,16,128]{3,2,1,0:T(8,128)(2,1)} %bitcast.11), custom_call_target="tpu_custom_call" | custom-call | tf_op jit(solution)/shard_map/whiten/pallas_call | solution.py:93
  3.5 0.7 %collective-permute-start = (bf16[121,32,128]{2,1,0:T(8,128)(2,1)S(1)}, bf16[121,32,128]{2,1,0:T(8,128)(2,1)S(1)}, u32[]{:S(2)}, u32[]{:S(2)}) collective-permute-start(bf16[121,32,128]{2,1,0:T(8,128)(2,1)S(1)} %get-tuple-element.27.own_ref), channel_id=1, source_target_pairs={{0,4},{4,0},{8,12},{12,8},{16,20},{20,16},{24,28},{28,24},{1,5},{5... | collective-permute-start | bytes 2973704 | tf_op jit(solution)/shard_map/ppermute | solution.py:308
  4.3 3.0 %collective-permute-start.4 = (bf16[60,32,128]{2,1,0:T(8,128)(2,1)S(1)}, bf16[60,32,128]{2,1,0:T(8,128)(2,1)S(1)}, u32[]{:S(2)}, u32[]{:S(2)}) collective-permute-start(bf16[60,32,128]{2,1,0:T(8,128)(2,1)S(1)} %get-tuple-element.28.own_ref.near_ref), channel_id=1, source_target_pairs={{4,8},{8,4},{12,16},{16,12},{20,24},{24,20},{5,9},{9,5},{13,17},{1... | collective-permute-start | bytes 1474568 | tf_op jit(solution)/shard_map/ppermute | solution.py:309
  7.3 0.0 collective-permute-done.other_ref
  7.3 1.2 %products.11 = bf16[16,32,128]{2,1,0:T(8,128)(2,1)S(1)} custom-call(bf16[60,32,128]{2,1,0:T(8,128)(2,1)S(1)} %get-tuple-element.28.own_ref.near_ref, bf16[121,32,128]{2,1,0:T(8,128)(2,1)S(1)} %collective-permute-done.other_ref), custom_call_target="tpu_custom_call" | custom-call | flops 7864320 | bytes 524288 | tf_op jit(solution)/shard_map/products/pallas_call | solution.py:146
  8.5 3.4 %collective-permute-start.5 = (bf16[60,32,128]{2,1,0:T(8,128)(2,1)S(1)}, bf16[60,32,128]{2,1,0:T(8,128)(2,1)S(1)}, u32[]{:S(2)}, u32[]{:S(2)}) collective-permute-start(bf16[60,32,128]{2,1,0:T(8,128)(2,1)S(1)} %get-tuple-element.31.own_ref.near_ref), channel_id=1, source_target_pairs={{4,8},{8,4},{12,16},{16,12},{20,24},{24,20},{5,9},{9,5},{13,17},{1... | collective-permute-start | bytes 1474568 | tf_op jit(solution)/shard_map/ppermute | solution.py:317
  12.0 2.4 %collective-permute-start.3 = (bf16[16,32,128]{2,1,0:T(8,128)(2,1)S(1)}, bf16[16,32,128]{2,1,0:T(8,128)(2,1)S(1)}, u32[]{:S(2)}, u32[]{:S(2)}) collective-permute-start(bf16[16,32,128]{2,1,0:T(8,128)(2,1)S(1)} %products.11), channel_id=1, source_target_pairs={{0,2},{1,3},{2,0},{3,1},{4,6},{5,7},{6,4},{7,5},{8,10},{9,11},{10,... | collective-permute-start | bytes 393224 | tf_op jit(solution)/shard_map/ppermute | solution.py:303
  14.3 1.2 %products.10 = bf16[16,32,128]{2,1,0:T(8,128)(2,1)S(1)} custom-call(bf16[60,32,128]{2,1,0:T(8,128)(2,1)S(1)} %get-tuple-element.28.own_ref.near_ref, bf16[121,32,128]{2,1,0:T(8,128)(2,1)S(1)} %collective-permute-done.other_ref), custom_call_target="tpu_custom_call" | custom-call | flops 7864320 | bytes 524288 | tf_op jit(solution)/shard_map/products/pallas_call | solution.py:146
  15.5 1.3 %collective-permute-start.2 = (bf16[16,32,128]{2,1,0:T(8,128)(2,1)S(1)}, bf16[16,32,128]{2,1,0:T(8,128)(2,1)S(1)}, u32[]{:S(2)}, u32[]{:S(2)}) collective-permute-start(bf16[16,32,128]{2,1,0:T(8,128)(2,1)S(1)} %products.10), channel_id=1, source_target_pairs={{0,1},{1,2},{2,3},{3,0},{4,5},{5,6},{6,7},{7,4},{8,9},{9,10},{10,1... | collective-permute-start | bytes 393224 | tf_op jit(solution)/shard_map/ppermute | solution.py:303
  16.9 1.2 %products.9 = bf16[16,32,128]{2,1,0:T(8,128)(2,1)S(1)} custom-call(bf16[60,32,128]{2,1,0:T(8,128)(2,1)S(1)} %get-tuple-element.31.own_ref.near_ref, bf16[121,32,128]{2,1,0:T(8,128)(2,1)S(1)} %collective-permute-done.other_ref), custom_call_target="tpu_custom_call" | custom-call | flops 7864320 | bytes 524288 | tf_op jit(solution)/shard_map/products/pallas_call | solution.py:146
  18.1 2.0 %collective-permute-start.1 = (bf16[16,32,128]{2,1,0:T(8,128)(2,1)S(1)}, bf16[16,32,128]{2,1,0:T(8,128)(2,1)S(1)}, u32[]{:S(2)}, u32[]{:S(2)}) collective-permute-start(bf16[16,32,128]{2,1,0:T(8,128)(2,1)S(1)} %products.9), channel_id=1, source_target_pairs={{0,3},{1,0},{2,1},{3,2},{4,7},{5,4},{6,5},{7,6},{8,11},{9,8},{10,9... | collective-permute-start | bytes 393224 | tf_op jit(solution)/shard_map/ppermute | solution.py:303
  20.1 1.2 %products.8.refs_0_ = f32[16,32,128]{2,1,0:T(8,128)S(1)} custom-call(bf16[60,32,128]{2,1,0:T(8,128)(2,1)S(1)} %get-tuple-element.31.own_ref.near_ref, bf16[121,32,128]{2,1,0:T(8,128)(2,1)S(1)} %collective-permute-done.other_ref), custom_call_target="tpu_custom_call" | custom-call | flops 7864320 | bytes 524288 | tf_op jit(solution)/shard_map/products/pallas_call | solution.py:146
  21.3 0.0 collective-permute-done.4.other_ref
  21.3 1.3 %products.12 = bf16[16,32,128]{2,1,0:T(8,128)(2,1)S(1)} custom-call(bf16[121,32,128]{2,1,0:T(8,128)(2,1)S(1)} %get-tuple-element.27.own_ref, bf16[60,32,128]{2,1,0:T(8,128)(2,1)S(1)} %collective-permute-done.4.other_ref, bf16[60,32,128]{2,1,0:T(8,128)(2,1)S(1)} %get-tuple-element.28.own_ref.near_ref), custom_call_target="tpu_custom_call" | custom-call | flops 7864320 | bytes 524288 | tf_op jit(solution)/shard_map/products/pallas_call | solution.py:146
  22.6 1.6 %collective-permute-start.9 = (bf16[16,32,128]{2,1,0:T(8,128)(2,1)S(1)}, bf16[16,32,128]{2,1,0:T(8,128)(2,1)S(1)}, u32[]{:S(2)}, u32[]{:S(2)}) collective-permute-start(bf16[16,32,128]{2,1,0:T(8,128)(2,1)S(1)} %products.12), channel_id=1, source_target_pairs={{0,2},{1,3},{2,0},{3,1},{4,6},{5,7},{6,4},{7,5},{8,10},{9,11},{10,... | collective-permute-start | bytes 393224 | tf_op jit(solution)/shard_map/ppermute | solution.py:303
  24.2 0.0 collective-permute-done.3.refs_3_
  24.2 1.3 %products.13 = bf16[16,32,128]{2,1,0:T(8,128)(2,1)S(1)} custom-call(bf16[121,32,128]{2,1,0:T(8,128)(2,1)S(1)} %get-tuple-element.27.own_ref, bf16[60,32,128]{2,1,0:T(8,128)(2,1)S(1)} %collective-permute-done.4.other_ref, bf16[60,32,128]{2,1,0:T(8,128)(2,1)S(1)} %get-tuple-element.28.own_ref.near_ref), custom_call_target="tpu_custom_call" | custom-call | flops 7864320 | bytes 524288 | tf_op jit(solution)/shard_map/products/pallas_call | solution.py:146
  25.5 1.5 %collective-permute-start.8 = (bf16[16,32,128]{2,1,0:T(8,128)(2,1)S(1)}, bf16[16,32,128]{2,1,0:T(8,128)(2,1)S(1)}, u32[]{:S(2)}, u32[]{:S(2)}) collective-permute-start(bf16[16,32,128]{2,1,0:T(8,128)(2,1)S(1)} %products.13), channel_id=1, source_target_pairs={{0,1},{1,2},{2,3},{3,0},{4,5},{5,6},{6,7},{7,4},{8,9},{9,10},{10,1... | collective-permute-start | bytes 393224 | tf_op jit(solution)/shard_map/ppermute | solution.py:303
  27.1 3.7 %collective-permute-done.5.other_ref = bf16[60,32,128]{2,1,0:T(8,128)(2,1)S(1)} collective-permute-done((bf16[60,32,128]{2,1,0:T(8,128)(2,1)S(1)}, bf16[60,32,128]{2,1,0:T(8,128)(2,1)S(1)}, u32[]{:S(2)}, u32[]{:S(2)}) %collective-permute-start.5) | collective-permute-done | bytes 491552 | tf_op jit(solution)/shard_map/ppermute | solution.py:317
  30.8 1.3 %products.14 = bf16[16,32,128]{2,1,0:T(8,128)(2,1)S(1)} custom-call(bf16[121,32,128]{2,1,0:T(8,128)(2,1)S(1)} %get-tuple-element.27.own_ref, bf16[60,32,128]{2,1,0:T(8,128)(2,1)S(1)} %collective-permute-done.5.other_ref, bf16[60,32,128]{2,1,0:T(8,128)(2,1)S(1)} %get-tuple-element.31.own_ref.near_ref), custom_call_target="tpu_custom_call" | custom-call | flops 7864320 | bytes 524288 | tf_op jit(solution)/shard_map/products/pallas_call | solution.py:146
  32.1 3.4 %collective-permute-start.7 = (bf16[16,32,128]{2,1,0:T(8,128)(2,1)S(1)}, bf16[16,32,128]{2,1,0:T(8,128)(2,1)S(1)}, u32[]{:S(2)}, u32[]{:S(2)}) collective-permute-start(bf16[16,32,128]{2,1,0:T(8,128)(2,1)S(1)} %products.14), channel_id=1, source_target_pairs={{0,3},{1,0},{2,1},{3,2},{4,7},{5,4},{6,5},{7,6},{8,11},{9,8},{10,9... | collective-permute-start | bytes 393224 | tf_op jit(solution)/shard_map/ppermute | solution.py:303
  35.5 1.3 %products.15.refs_0_ = f32[16,32,128]{2,1,0:T(8,128)S(1)} custom-call(bf16[121,32,128]{2,1,0:T(8,128)(2,1)S(1)} %get-tuple-element.27.own_ref, bf16[60,32,128]{2,1,0:T(8,128)(2,1)S(1)} %collective-permute-done.5.other_ref, bf16[60,32,128]{2,1,0:T(8,128)(2,1)S(1)} %get-tuple-element.31.own_ref.near_ref), custom_call_target="tpu_custom_call" | custom-call | flops 7864320 | bytes 524288 | tf_op jit(solution)/shard_map/products/pallas_call | solution.py:146
  36.8 0.0 collective-permute-done.2.refs_2_
  36.8 0.0 collective-permute-done.1.refs_1_
  36.8 0.3 add_hours.2
  37.1 0.1 collective-permute-start.6
  37.2 0.0 collective-permute-done.9.refs_3_
  37.2 0.0 collective-permute-done.8.refs_2_
  37.2 0.3 collective-permute-done.7.refs_1_
  37.6 0.3 add_hours.3
  37.8 3.8 %collective-permute-start.10 = (bf16[16,32,128]{2,1,0:T(8,128)(2,1)S(1)}, bf16[16,32,128]{2,1,0:T(8,128)(2,1)S(1)}, u32[]{:S(2)}, u32[]{:S(2)}) collective-permute-start(bf16[16,32,128]{2,1,0:T(8,128)(2,1)S(1)} %get-tuple-element.44.turned_ref), channel_id=1, source_target_pairs={{4,8},{8,4},{12,16},{16,12},{20,24},{24,20},{5,9},{9,5},{13,17},{1... | collective-permute-start | bytes 393224 | tf_op jit(solution)/shard_map/ppermute | solution.py:332
  41.6 0.0 collective-permute-done.6.near_theirs
  41.6 3.8 %collective-permute-done.10.far_theirs = bf16[16,32,128]{2,1,0:T(8,128)(2,1)S(1)} collective-permute-done((bf16[16,32,128]{2,1,0:T(8,128)(2,1)S(1)}, bf16[16,32,128]{2,1,0:T(8,128)(2,1)S(1)}, u32[]{:S(2)}, u32[]{:S(2)}) %collective-permute-start.10) | collective-permute-done | bytes 131104 | tf_op jit(solution)/shard_map/ppermute | solution.py:332
  45.4 1.3 %assemble.1 = f32[2,16,64,128]{3,2,1,0:T(8,128)} custom-call(f32[2,8,128]{2,1,0:T(8,128)S(1)} %get-tuple-element.25.steps_ref, f32[16,32,128]{2,1,0:T(8,128)S(1)} %get-tuple-element.37.near_mine, bf16[16,32,128]{2,1,0:T(8,128)(2,1)S(1)} %collective-permute-done.6.near_theirs, f32[16,32,128]{2,1,0:T(8,128)S(1)} %get-tuple-element.43.far_mine, ...), custom_call_target="tpu_custom_call" | custom-call | tf_op jit(solution)/shard_map/assemble/pallas_call | solution.py:281
Async XLA Ops:
  3.5 3.8 %collective-permute-start = (bf16[121,32,128]{2,1,0:T(8,128)(2,1)S(1)}, bf16[121,32,128]{2,1,0:T(8,128)(2,1)S(1)}, u32[]{:S(2)}, u32[]{:S(2)}) collective-permute-start(bf16[121,32,128]{2,1,0:T(8,128)(2,1)S(1)} %get-tuple-element.27.own_ref), channel_id=1, source_target_pairs={{0,4},{4,0},{8,12},{12,8},{16,20},{20,16},{24,28},{28,24},{1,5},{5... | collective-permute-start | bytes 2973704 | tf_op jit(solution)/shard_map/ppermute | solution.py:308
  4.3 17.0 %collective-permute-start.4 = (bf16[60,32,128]{2,1,0:T(8,128)(2,1)S(1)}, bf16[60,32,128]{2,1,0:T(8,128)(2,1)S(1)}, u32[]{:S(2)}, u32[]{:S(2)}) collective-permute-start(bf16[60,32,128]{2,1,0:T(8,128)(2,1)S(1)} %get-tuple-element.28.own_ref.near_ref), channel_id=1, source_target_pairs={{4,8},{8,4},{12,16},{16,12},{20,24},{24,20},{5,9},{9,5},{13,17},{1... | collective-permute-start | bytes 1474568 | tf_op jit(solution)/shard_map/ppermute | solution.py:309
  8.5 22.3 %collective-permute-start.5 = (bf16[60,32,128]{2,1,0:T(8,128)(2,1)S(1)}, bf16[60,32,128]{2,1,0:T(8,128)(2,1)S(1)}, u32[]{:S(2)}, u32[]{:S(2)}) collective-permute-start(bf16[60,32,128]{2,1,0:T(8,128)(2,1)S(1)} %get-tuple-element.31.own_ref.near_ref), channel_id=1, source_target_pairs={{4,8},{8,4},{12,16},{16,12},{20,24},{24,20},{5,9},{9,5},{13,17},{1... | collective-permute-start | bytes 1474568 | tf_op jit(solution)/shard_map/ppermute | solution.py:317
  12.0 12.3 %collective-permute-start.3 = (bf16[16,32,128]{2,1,0:T(8,128)(2,1)S(1)}, bf16[16,32,128]{2,1,0:T(8,128)(2,1)S(1)}, u32[]{:S(2)}, u32[]{:S(2)}) collective-permute-start(bf16[16,32,128]{2,1,0:T(8,128)(2,1)S(1)} %products.11), channel_id=1, source_target_pairs={{0,2},{1,3},{2,0},{3,1},{4,6},{5,7},{6,4},{7,5},{8,10},{9,11},{10,... | collective-permute-start | bytes 393224 | tf_op jit(solution)/shard_map/ppermute | solution.py:303
  15.5 21.3 %collective-permute-start.2 = (bf16[16,32,128]{2,1,0:T(8,128)(2,1)S(1)}, bf16[16,32,128]{2,1,0:T(8,128)(2,1)S(1)}, u32[]{:S(2)}, u32[]{:S(2)}) collective-permute-start(bf16[16,32,128]{2,1,0:T(8,128)(2,1)S(1)} %products.10), channel_id=1, source_target_pairs={{0,1},{1,2},{2,3},{3,0},{4,5},{5,6},{6,7},{7,4},{8,9},{9,10},{10,1... | collective-permute-start | bytes 393224 | tf_op jit(solution)/shard_map/ppermute | solution.py:303
  18.1 18.8 %collective-permute-start.1 = (bf16[16,32,128]{2,1,0:T(8,128)(2,1)S(1)}, bf16[16,32,128]{2,1,0:T(8,128)(2,1)S(1)}, u32[]{:S(2)}, u32[]{:S(2)}) collective-permute-start(bf16[16,32,128]{2,1,0:T(8,128)(2,1)S(1)} %products.9), channel_id=1, source_target_pairs={{0,3},{1,0},{2,1},{3,2},{4,7},{5,4},{6,5},{7,6},{8,11},{9,8},{10,9... | collective-permute-start | bytes 393224 | tf_op jit(solution)/shard_map/ppermute | solution.py:303
  22.6 14.6 %collective-permute-start.9 = (bf16[16,32,128]{2,1,0:T(8,128)(2,1)S(1)}, bf16[16,32,128]{2,1,0:T(8,128)(2,1)S(1)}, u32[]{:S(2)}, u32[]{:S(2)}) collective-permute-start(bf16[16,32,128]{2,1,0:T(8,128)(2,1)S(1)} %products.12), channel_id=1, source_target_pairs={{0,2},{1,3},{2,0},{3,1},{4,6},{5,7},{6,4},{7,5},{8,10},{9,11},{10,... | collective-permute-start | bytes 393224 | tf_op jit(solution)/shard_map/ppermute | solution.py:303
  25.5 11.7 %collective-permute-start.8 = (bf16[16,32,128]{2,1,0:T(8,128)(2,1)S(1)}, bf16[16,32,128]{2,1,0:T(8,128)(2,1)S(1)}, u32[]{:S(2)}, u32[]{:S(2)}) collective-permute-start(bf16[16,32,128]{2,1,0:T(8,128)(2,1)S(1)} %products.13), channel_id=1, source_target_pairs={{0,1},{1,2},{2,3},{3,0},{4,5},{5,6},{6,7},{7,4},{8,9},{9,10},{10,1... | collective-permute-start | bytes 393224 | tf_op jit(solution)/shard_map/ppermute | solution.py:303
  32.1 5.4 %collective-permute-start.7 = (bf16[16,32,128]{2,1,0:T(8,128)(2,1)S(1)}, bf16[16,32,128]{2,1,0:T(8,128)(2,1)S(1)}, u32[]{:S(2)}, u32[]{:S(2)}) collective-permute-start(bf16[16,32,128]{2,1,0:T(8,128)(2,1)S(1)} %products.14), channel_id=1, source_target_pairs={{0,3},{1,0},{2,1},{3,2},{4,7},{5,4},{6,5},{7,6},{8,11},{9,8},{10,9... | collective-permute-start | bytes 393224 | tf_op jit(solution)/shard_map/ppermute | solution.py:303
  37.1 4.5 %collective-permute-start.6 = (bf16[16,32,128]{2,1,0:T(8,128)(2,1)S(1)}, bf16[16,32,128]{2,1,0:T(8,128)(2,1)S(1)}, u32[]{:S(2)}, u32[]{:S(2)}) collective-permute-start(bf16[16,32,128]{2,1,0:T(8,128)(2,1)S(1)} %get-tuple-element.38), channel_id=1, source_target_pairs={{0,4},{4,0},{8,12},{12,8},{16,20},{20,16},{24,28},{28,24},{1,5},{5... | collective-permute-start | bytes 393224 | tf_op jit(solution)/shard_map/ppermute | solution.py:330
  37.8 7.6 %collective-permute-start.10 = (bf16[16,32,128]{2,1,0:T(8,128)(2,1)S(1)}, bf16[16,32,128]{2,1,0:T(8,128)(2,1)S(1)}, u32[]{:S(2)}, u32[]{:S(2)}) collective-permute-start(bf16[16,32,128]{2,1,0:T(8,128)(2,1)S(1)} %get-tuple-element.44.turned_ref), channel_id=1, source_target_pairs={{4,8},{8,4},{12,16},{16,12},{20,24},{24,20},{5,9},{9,5},{13,17},{1... | collective-permute-start | bytes 393224 | tf_op jit(solution)/shard_map/ppermute | solution.py:332

commit v8 on v7

--- a/solution.py
+++ b/solution.py
@@ -8,7 +8,7 @@
 LANES = 128
 EPSILON = 1e-06
 BLOCK = 8
-ORDER = (2, 1, 3, 0)
+ORDER = (2, 3, 1, 0)
 BATCH = 2
 WIDE = jnp.float32
 VMEM = pl.BlockSpec(memory_space=pltpu.VMEM)
@@ -81,7 +81,7 @@
                         place = pl.ds(w * rows * stations + first + k, rows, stride=stations)
                         rowed[place, :] = x * factor * weight
             for k, d in enumerate(ORDER):
-                owner = lax.rem(here + d, hours)
+                owner = lax.bitwise_xor(here, d)
                 for w in range(step):
                     for tile, out, row in ((near, near_refs[k // BATCH], k % BATCH), (1 - near, far_ref, k)):
                         start = (w * tiles + owner * mine + tile) * height
@@ -117,27 +117,29 @@
 
 def unit(own_ref, own_row, other_ref, other_row, out_ref, wide):
     stations = own_ref.shape[1] // 2
-    windows = wide.shape[0]
+    windows, block = wide.shape[0], 4
     wide[...] = own_ref[pl.ds(own_row, windows)].astype(WIDE)
-    for first in range(0, stations, BLOCK):
+    for first in range(0, stations, block):
 
         def body(w, sums):
             other = other_ref[other_row + w].astype(WIDE)
             re, im = other[:stations], other[stations:]
+            gap = im - re
             new = []
-            for k in range(BLOCK):
+            for k in range(block):
                 a = first + k
                 a_re = jnp.broadcast_to(wide[w, a : a + 1, :], re.shape)
                 a_im = jnp.broadcast_to(wide[w, stations + a : stations + a + 1, :], re.shape)
-                new.append(sums[2 * k] + (a_re * re + a_im * im))
-                new.append(sums[2 * k + 1] + (a_re * im - a_im * re))
+                p, q, r = sums[3 * k : 3 * k + 3]
+                new += [p + a_re * re, q + a_im * im, r + (a_re + a_im) * gap]
             return tuple(new)
 
         zero = jnp.zeros((stations, LANES), WIDE)
-        sums = lax.fori_loop(0, windows, body, (zero,) * (2 * BLOCK), unroll=6)
-        for k in range(BLOCK):
-            out_ref[first + k, :stations] = sums[2 * k].astype(out_ref.dtype)
-            out_ref[first + k, stations:] = sums[2 * k + 1].astype(out_ref.dtype)
+        sums = lax.fori_loop(0, windows, body, (zero,) * (3 * block), unroll=windows)
+        for k in range(block):
+            p, q, r = sums[3 * k : 3 * k + 3]
+            out_ref[first + k, :stations] = (p + q).astype(out_ref.dtype)
+            out_ref[first + k, stations:] = (r + p - q).astype(out_ref.dtype)
 
 
 def product_call(body, operands, windows, dtype, scratch_shapes):
@@ -300,7 +302,7 @@
     across = [(g, h) for i in range(1, count - 1, 2) for g, h in ((i, i + 1), (i + 1, i))]
 
     def to_owner(part, d):
-        return lax.ppermute(part, "hour", [(h, (h + d) % hours) for h in range(hours)]) if d else part
+        return lax.ppermute(part, "hour", [(h, h ^ d) for h in range(hours)]) if d else part
 
     def after(value, *earlier):
         return lax.optimization_barrier((value, earlier))[0]

time: 47.5 us -> 46.7 us (0.983)
  waiting for transfers between devices: 7.86 us -> 12.2 us
  starting transfers between devices: 23.3 us -> 20.1 us
  Pallas kernels: 15.3 us -> 13.7 us
    ppermute x6, starting transfers between devices: 12.3 us -> 9.67 us  [to_owner(): lax.ppermute(part, 'hour', [(h, h ^ d) for h in range(hours)])]
    ppermute x1, waiting for transfers between devices: 0.01 us -> 2.43 us  [per_device(): far_others = [lax.ppermute(near[0], 'sta', across)]]
    ppermute x6, waiting for transfers between devices: 0.35 us -> 2.66 us  [to_owner(): lax.ppermute(part, 'hour', [(h, h ^ d) for h in range(hours)])]
    pallas_call x8, Pallas kernels: 9.97 us -> 8.25 us  [product_call(): pl.pallas_call(body, in_specs=[VMEM] * len(operands), out_specs=VMEM, out...]
    ppermute x1, waiting for transfers between devices: 3.72 us -> 3.05 us  [per_device(): lax.ppermute(after(near[1], *near_made[:1]), 'sta', across)]
    ppermute x1, starting transfers between devices: 3.79 us -> 3.13 us  [per_device(): far_theirs = lax.ppermute(turned, 'sta', across)]
  transfers between devices with their start and end apart: 11 -> 11, of which waited for: 3 -> 5; matrix products, arithmetic and copies ran while one was open for 0% -> 0% of each run, Pallas kernels for 23% -> 19%
where the time goes in v8:
time: 46.7 us; the launch traced here: 46.1 us
  starting transfers between devices  20.1 us (43%)
  Pallas kernels  13.7 us (29%)
  waiting for transfers between devices  12.2 us (26%)
    ppermute x6, starting transfers between devices, to_owner(): lax.ppermute(part, 'hour', [(h, h ^ d) for h in range(hours)])  9.67 us
    pallas_call x8, Pallas kernels, product_call(): pl.pallas_call(body, in_specs=[VMEM] * len(operands), out_specs=VMEM, out...  8.25 us
    ppermute x1, waiting for transfers between devices, per_device(): far_theirs = lax.ppermute(turned, 'sta', across)  4.04 us
    pallas_call x1, Pallas kernels, whiten(): pl.pallas_call(body, in_specs=[hbm] * 4, out_specs=[VMEM] * (batches + 2)...  3.58 us
    ppermute x1, starting transfers between devices, per_device(): lax.ppermute(after(near[1], *near_made[:1]), 'sta', across)  3.43 us
    ppermute x1, starting transfers between devices, per_device(): far_theirs = lax.ppermute(turned, 'sta', across)  3.13 us
    ppermute x1, waiting for transfers between devices, per_device(): lax.ppermute(after(near[1], *near_made[:1]), 'sta', across)  3.05 us
    ppermute x1, starting transfers between devices, per_device(): far_others = [lax.ppermute(near[0], 'sta', across)]  3.02 us
  transfers between devices with their start and end apart: 11, of which 5 were waited for; matrix products, arithmetic and copies ran while one was open for 0% of the time, Pallas kernels for 19%

profile of v8, /device:TPU:3, one launch (start us, length us, event | category | flops | bytes accessed | tf_op | source)
XLA Modules:
  0.0 46.1 jit_solution(9002173486600658654)
XLA Ops:
  0.0 3.6 %whiten.1 = (bf16[60,32,128]{2,1,0:T(8,128)(2,1)S(1)}, bf16[60,32,128]{2,1,0:T(8,128)(2,1)S(1)}, bf16[121,32,128]{2,1,0:T(8,128)(2,1)S(1)}, f32[2,8,128]{2,1,0:T(8,128)S(1)}) custom-call(s32[1,16]{1,0:T(1,128)} %order_hbm.1, s32[2,2]{1,0:T(2,128)} %pairs_hbm.1, f32[8,128]{1,0:T(8,128)} %bitcast.12, bf16[16,30,16,128]{3,2,1,0:T(8,128)(2,1)} %bitcast.11), custom_call_target="tpu_custom_call" | custom-call | tf_op jit(solution)/shard_map/whiten/pallas_call | solution.py:93
  3.6 0.7 %collective-permute-start = (bf16[121,32,128]{2,1,0:T(8,128)(2,1)S(1)}, bf16[121,32,128]{2,1,0:T(8,128)(2,1)S(1)}, u32[]{:S(2)}, u32[]{:S(2)}) collective-permute-start(bf16[121,32,128]{2,1,0:T(8,128)(2,1)S(1)} %get-tuple-element.27.own_ref), channel_id=1, source_target_pairs={{0,4},{4,0},{8,12},{12,8},{16,20},{20,16},{24,28},{28,24},{1,5},{5... | collective-permute-start | bytes 2973704 | tf_op jit(solution)/shard_map/ppermute | solution.py:310
  4.3 3.0 %collective-permute-start.4 = (bf16[60,32,128]{2,1,0:T(8,128)(2,1)S(1)}, bf16[60,32,128]{2,1,0:T(8,128)(2,1)S(1)}, u32[]{:S(2)}, u32[]{:S(2)}) collective-permute-start(bf16[60,32,128]{2,1,0:T(8,128)(2,1)S(1)} %get-tuple-element.28.own_ref.near_ref), channel_id=1, source_target_pairs={{4,8},{8,4},{12,16},{16,12},{20,24},{24,20},{5,9},{9,5},{13,17},{1... | collective-permute-start | bytes 1474568 | tf_op jit(solution)/shard_map/ppermute | solution.py:311
  7.4 0.0 collective-permute-done.other_ref
  7.4 1.0 %products.11 = bf16[16,32,128]{2,1,0:T(8,128)(2,1)S(1)} custom-call(bf16[60,32,128]{2,1,0:T(8,128)(2,1)S(1)} %get-tuple-element.28.own_ref.near_ref, bf16[121,32,128]{2,1,0:T(8,128)(2,1)S(1)} %collective-permute-done.other_ref), custom_call_target="tpu_custom_call" | custom-call | flops 7864320 | bytes 524288 | tf_op jit(solution)/shard_map/products/pallas_call | solution.py:148
  8.3 3.4 %collective-permute-start.5 = (bf16[60,32,128]{2,1,0:T(8,128)(2,1)S(1)}, bf16[60,32,128]{2,1,0:T(8,128)(2,1)S(1)}, u32[]{:S(2)}, u32[]{:S(2)}) collective-permute-start(bf16[60,32,128]{2,1,0:T(8,128)(2,1)S(1)} %get-tuple-element.31.own_ref.near_ref), channel_id=1, source_target_pairs={{4,8},{8,4},{12,16},{16,12},{20,24},{24,20},{5,9},{9,5},{13,17},{1... | collective-permute-start | bytes 1474568 | tf_op jit(solution)/shard_map/ppermute | solution.py:319
  11.8 2.4 %collective-permute-start.3 = (bf16[16,32,128]{2,1,0:T(8,128)(2,1)S(1)}, bf16[16,32,128]{2,1,0:T(8,128)(2,1)S(1)}, u32[]{:S(2)}, u32[]{:S(2)}) collective-permute-start(bf16[16,32,128]{2,1,0:T(8,128)(2,1)S(1)} %products.11), channel_id=1, source_target_pairs={{0,2},{1,3},{2,0},{3,1},{4,6},{5,7},{6,4},{7,5},{8,10},{9,11},{10,... | collective-permute-start | bytes 393224 | tf_op jit(solution)/shard_map/ppermute | solution.py:305
  14.1 0.9 %products.10 = bf16[16,32,128]{2,1,0:T(8,128)(2,1)S(1)} custom-call(bf16[60,32,128]{2,1,0:T(8,128)(2,1)S(1)} %get-tuple-element.28.own_ref.near_ref, bf16[121,32,128]{2,1,0:T(8,128)(2,1)S(1)} %collective-permute-done.other_ref), custom_call_target="tpu_custom_call" | custom-call | flops 7864320 | bytes 524288 | tf_op jit(solution)/shard_map/products/pallas_call | solution.py:148
  15.1 1.1 %collective-permute-start.2 = (bf16[16,32,128]{2,1,0:T(8,128)(2,1)S(1)}, bf16[16,32,128]{2,1,0:T(8,128)(2,1)S(1)}, u32[]{:S(2)}, u32[]{:S(2)}) collective-permute-start(bf16[16,32,128]{2,1,0:T(8,128)(2,1)S(1)} %products.10), channel_id=1, source_target_pairs={{0,3},{1,2},{2,1},{3,0},{4,7},{5,6},{6,5},{7,4},{8,11},{9,10},{10,... | collective-permute-start | bytes 393224 | tf_op jit(solution)/shard_map/ppermute | solution.py:305
  16.2 0.9 %products.9 = bf16[16,32,128]{2,1,0:T(8,128)(2,1)S(1)} custom-call(bf16[60,32,128]{2,1,0:T(8,128)(2,1)S(1)} %get-tuple-element.31.own_ref.near_ref, bf16[121,32,128]{2,1,0:T(8,128)(2,1)S(1)} %collective-permute-done.other_ref), custom_call_target="tpu_custom_call" | custom-call | flops 7864320 | bytes 524288 | tf_op jit(solution)/shard_map/products/pallas_call | solution.py:148
  17.2 0.3 collective-permute-start.1
  17.5 0.9 %products.8.refs_0_ = f32[16,32,128]{2,1,0:T(8,128)S(1)} custom-call(bf16[60,32,128]{2,1,0:T(8,128)(2,1)S(1)} %get-tuple-element.31.own_ref.near_ref, bf16[121,32,128]{2,1,0:T(8,128)(2,1)S(1)} %collective-permute-done.other_ref), custom_call_target="tpu_custom_call" | custom-call | flops 7864320 | bytes 524288 | tf_op jit(solution)/shard_map/products/pallas_call | solution.py:148
  18.4 2.4 %collective-permute-done.4.other_ref = bf16[60,32,128]{2,1,0:T(8,128)(2,1)S(1)} collective-permute-done((bf16[60,32,128]{2,1,0:T(8,128)(2,1)S(1)}, bf16[60,32,128]{2,1,0:T(8,128)(2,1)S(1)}, u32[]{:S(2)}, u32[]{:S(2)}) %collective-permute-start.4) | collective-permute-done | bytes 491552 | tf_op jit(solution)/shard_map/ppermute | solution.py:311
  20.9 1.1 %products.12 = bf16[16,32,128]{2,1,0:T(8,128)(2,1)S(1)} custom-call(bf16[121,32,128]{2,1,0:T(8,128)(2,1)S(1)} %get-tuple-element.27.own_ref, bf16[60,32,128]{2,1,0:T(8,128)(2,1)S(1)} %collective-permute-done.4.other_ref, bf16[60,32,128]{2,1,0:T(8,128)(2,1)S(1)} %get-tuple-element.28.own_ref.near_ref), custom_call_target="tpu_custom_call" | custom-call | flops 7864320 | bytes 524288 | tf_op jit(solution)/shard_map/products/pallas_call | solution.py:148
  21.9 2.1 %collective-permute-start.9 = (bf16[16,32,128]{2,1,0:T(8,128)(2,1)S(1)}, bf16[16,32,128]{2,1,0:T(8,128)(2,1)S(1)}, u32[]{:S(2)}, u32[]{:S(2)}) collective-permute-start(bf16[16,32,128]{2,1,0:T(8,128)(2,1)S(1)} %products.12), channel_id=1, source_target_pairs={{0,2},{1,3},{2,0},{3,1},{4,6},{5,7},{6,4},{7,5},{8,10},{9,11},{10,... | collective-permute-start | bytes 393224 | tf_op jit(solution)/shard_map/ppermute | solution.py:305
  24.0 0.0 collective-permute-done.3.refs_3_
  24.0 1.1 %products.13 = bf16[16,32,128]{2,1,0:T(8,128)(2,1)S(1)} custom-call(bf16[121,32,128]{2,1,0:T(8,128)(2,1)S(1)} %get-tuple-element.27.own_ref, bf16[60,32,128]{2,1,0:T(8,128)(2,1)S(1)} %collective-permute-done.4.other_ref, bf16[60,32,128]{2,1,0:T(8,128)(2,1)S(1)} %get-tuple-element.28.own_ref.near_ref), custom_call_target="tpu_custom_call" | custom-call | flops 7864320 | bytes 524288 | tf_op jit(solution)/shard_map/products/pallas_call | solution.py:148
  25.1 2.7 %collective-permute-start.8 = (bf16[16,32,128]{2,1,0:T(8,128)(2,1)S(1)}, bf16[16,32,128]{2,1,0:T(8,128)(2,1)S(1)}, u32[]{:S(2)}, u32[]{:S(2)}) collective-permute-start(bf16[16,32,128]{2,1,0:T(8,128)(2,1)S(1)} %products.13), channel_id=1, source_target_pairs={{0,3},{1,2},{2,1},{3,0},{4,7},{5,6},{6,5},{7,4},{8,11},{9,10},{10,... | collective-permute-start | bytes 393224 | tf_op jit(solution)/shard_map/ppermute | solution.py:305
  27.8 3.0 %collective-permute-done.5.other_ref = bf16[60,32,128]{2,1,0:T(8,128)(2,1)S(1)} collective-permute-done((bf16[60,32,128]{2,1,0:T(8,128)(2,1)S(1)}, bf16[60,32,128]{2,1,0:T(8,128)(2,1)S(1)}, u32[]{:S(2)}, u32[]{:S(2)}) %collective-permute-start.5) | collective-permute-done | bytes 491552 | tf_op jit(solution)/shard_map/ppermute | solution.py:319
  30.9 1.2 %products.14 = bf16[16,32,128]{2,1,0:T(8,128)(2,1)S(1)} custom-call(bf16[121,32,128]{2,1,0:T(8,128)(2,1)S(1)} %get-tuple-element.27.own_ref, bf16[60,32,128]{2,1,0:T(8,128)(2,1)S(1)} %collective-permute-done.5.other_ref, bf16[60,32,128]{2,1,0:T(8,128)(2,1)S(1)} %get-tuple-element.31.own_ref.near_ref), custom_call_target="tpu_custom_call" | custom-call | flops 7864320 | bytes 524288 | tf_op jit(solution)/shard_map/products/pallas_call | solution.py:148
  32.1 1.1 %collective-permute-start.7 = (bf16[16,32,128]{2,1,0:T(8,128)(2,1)S(1)}, bf16[16,32,128]{2,1,0:T(8,128)(2,1)S(1)}, u32[]{:S(2)}, u32[]{:S(2)}) collective-permute-start(bf16[16,32,128]{2,1,0:T(8,128)(2,1)S(1)} %products.14), channel_id=1, source_target_pairs={{0,1},{1,0},{2,3},{3,2},{4,5},{5,4},{6,7},{7,6},{8,9},{9,8},{10,11... | collective-permute-start | bytes 393224 | tf_op jit(solution)/shard_map/ppermute | solution.py:305
  33.2 1.1 %products.15.refs_0_ = f32[16,32,128]{2,1,0:T(8,128)S(1)} custom-call(bf16[121,32,128]{2,1,0:T(8,128)(2,1)S(1)} %get-tuple-element.27.own_ref, bf16[60,32,128]{2,1,0:T(8,128)(2,1)S(1)} %collective-permute-done.5.other_ref, bf16[60,32,128]{2,1,0:T(8,128)(2,1)S(1)} %get-tuple-element.31.own_ref.near_ref), custom_call_target="tpu_custom_call" | custom-call | flops 7864320 | bytes 524288 | tf_op jit(solution)/shard_map/products/pallas_call | solution.py:148
  34.3 0.0 collective-permute-done.2.refs_2_
  34.3 0.0 collective-permute-done.1.refs_1_
  34.3 0.3 add_hours.2
  34.6 0.1 collective-permute-start.6
  34.6 0.1 collective-permute-done.9.refs_3_
  34.8 0.0 collective-permute-done.8.refs_2_
  34.8 2.5 %collective-permute-done.7.refs_1_ = bf16[16,32,128]{2,1,0:T(8,128)(2,1)S(1)} collective-permute-done((bf16[16,32,128]{2,1,0:T(8,128)(2,1)S(1)}, bf16[16,32,128]{2,1,0:T(8,128)(2,1)S(1)}, u32[]{:S(2)}, u32[]{:S(2)}) %collective-permute-start.7) | collective-permute-done | bytes 131104 | tf_op jit(solution)/shard_map/ppermute | solution.py:305
  37.3 0.3 add_hours.3
  37.6 3.1 %collective-permute-start.10 = (bf16[16,32,128]{2,1,0:T(8,128)(2,1)S(1)}, bf16[16,32,128]{2,1,0:T(8,128)(2,1)S(1)}, u32[]{:S(2)}, u32[]{:S(2)}) collective-permute-start(bf16[16,32,128]{2,1,0:T(8,128)(2,1)S(1)} %get-tuple-element.44.turned_ref), channel_id=1, source_target_pairs={{4,8},{8,4},{12,16},{16,12},{20,24},{24,20},{5,9},{9,5},{13,17},{1... | collective-permute-start | bytes 393224 | tf_op jit(solution)/shard_map/ppermute | solution.py:334
  40.7 0.0 collective-permute-done.6.near_theirs
  40.7 4.0 %collective-permute-done.10.far_theirs = bf16[16,32,128]{2,1,0:T(8,128)(2,1)S(1)} collective-permute-done((bf16[16,32,128]{2,1,0:T(8,128)(2,1)S(1)}, bf16[16,32,128]{2,1,0:T(8,128)(2,1)S(1)}, u32[]{:S(2)}, u32[]{:S(2)}) %collective-permute-start.10) | collective-permute-done | bytes 131104 | tf_op jit(solution)/shard_map/ppermute | solution.py:334
  44.8 1.3 %assemble.1 = f32[2,16,64,128]{3,2,1,0:T(8,128)} custom-call(f32[2,8,128]{2,1,0:T(8,128)S(1)} %get-tuple-element.25.steps_ref, f32[16,32,128]{2,1,0:T(8,128)S(1)} %get-tuple-element.37.near_mine, bf16[16,32,128]{2,1,0:T(8,128)(2,1)S(1)} %collective-permute-done.6.near_theirs, f32[16,32,128]{2,1,0:T(8,128)S(1)} %get-tuple-element.43.far_mine, ...), custom_call_target="tpu_custom_call" | custom-call | tf_op jit(solution)/shard_map/assemble/pallas_call | solution.py:283
Async XLA Ops:
  3.6 3.8 %collective-permute-start = (bf16[121,32,128]{2,1,0:T(8,128)(2,1)S(1)}, bf16[121,32,128]{2,1,0:T(8,128)(2,1)S(1)}, u32[]{:S(2)}, u32[]{:S(2)}) collective-permute-start(bf16[121,32,128]{2,1,0:T(8,128)(2,1)S(1)} %get-tuple-element.27.own_ref), channel_id=1, source_target_pairs={{0,4},{4,0},{8,12},{12,8},{16,20},{20,16},{24,28},{28,24},{1,5},{5... | collective-permute-start | bytes 2973704 | tf_op jit(solution)/shard_map/ppermute | solution.py:310
  4.3 16.5 %collective-permute-start.4 = (bf16[60,32,128]{2,1,0:T(8,128)(2,1)S(1)}, bf16[60,32,128]{2,1,0:T(8,128)(2,1)S(1)}, u32[]{:S(2)}, u32[]{:S(2)}) collective-permute-start(bf16[60,32,128]{2,1,0:T(8,128)(2,1)S(1)} %get-tuple-element.28.own_ref.near_ref), channel_id=1, source_target_pairs={{4,8},{8,4},{12,16},{16,12},{20,24},{24,20},{5,9},{9,5},{13,17},{1... | collective-permute-start | bytes 1474568 | tf_op jit(solution)/shard_map/ppermute | solution.py:311
  8.3 22.5 %collective-permute-start.5 = (bf16[60,32,128]{2,1,0:T(8,128)(2,1)S(1)}, bf16[60,32,128]{2,1,0:T(8,128)(2,1)S(1)}, u32[]{:S(2)}, u32[]{:S(2)}) collective-permute-start(bf16[60,32,128]{2,1,0:T(8,128)(2,1)S(1)} %get-tuple-element.31.own_ref.near_ref), channel_id=1, source_target_pairs={{4,8},{8,4},{12,16},{16,12},{20,24},{24,20},{5,9},{9,5},{13,17},{1... | collective-permute-start | bytes 1474568 | tf_op jit(solution)/shard_map/ppermute | solution.py:319
  11.8 12.3 %collective-permute-start.3 = (bf16[16,32,128]{2,1,0:T(8,128)(2,1)S(1)}, bf16[16,32,128]{2,1,0:T(8,128)(2,1)S(1)}, u32[]{:S(2)}, u32[]{:S(2)}) collective-permute-start(bf16[16,32,128]{2,1,0:T(8,128)(2,1)S(1)} %products.11), channel_id=1, source_target_pairs={{0,2},{1,3},{2,0},{3,1},{4,6},{5,7},{6,4},{7,5},{8,10},{9,11},{10,... | collective-permute-start | bytes 393224 | tf_op jit(solution)/shard_map/ppermute | solution.py:305
  15.1 19.2 %collective-permute-start.2 = (bf16[16,32,128]{2,1,0:T(8,128)(2,1)S(1)}, bf16[16,32,128]{2,1,0:T(8,128)(2,1)S(1)}, u32[]{:S(2)}, u32[]{:S(2)}) collective-permute-start(bf16[16,32,128]{2,1,0:T(8,128)(2,1)S(1)} %products.10), channel_id=1, source_target_pairs={{0,3},{1,2},{2,1},{3,0},{4,7},{5,6},{6,5},{7,4},{8,11},{9,10},{10,... | collective-permute-start | bytes 393224 | tf_op jit(solution)/shard_map/ppermute | solution.py:305
  17.2 17.1 %collective-permute-start.1 = (bf16[16,32,128]{2,1,0:T(8,128)(2,1)S(1)}, bf16[16,32,128]{2,1,0:T(8,128)(2,1)S(1)}, u32[]{:S(2)}, u32[]{:S(2)}) collective-permute-start(bf16[16,32,128]{2,1,0:T(8,128)(2,1)S(1)} %products.9), channel_id=1, source_target_pairs={{0,1},{1,0},{2,3},{3,2},{4,5},{5,4},{6,7},{7,6},{8,9},{9,8},{10,11... | collective-permute-start | bytes 393224 | tf_op jit(solution)/shard_map/ppermute | solution.py:305
  21.9 12.8 %collective-permute-start.9 = (bf16[16,32,128]{2,1,0:T(8,128)(2,1)S(1)}, bf16[16,32,128]{2,1,0:T(8,128)(2,1)S(1)}, u32[]{:S(2)}, u32[]{:S(2)}) collective-permute-start(bf16[16,32,128]{2,1,0:T(8,128)(2,1)S(1)} %products.12), channel_id=1, source_target_pairs={{0,2},{1,3},{2,0},{3,1},{4,6},{5,7},{6,4},{7,5},{8,10},{9,11},{10,... | collective-permute-start | bytes 393224 | tf_op jit(solution)/shard_map/ppermute | solution.py:305
  25.1 9.7 %collective-permute-start.8 = (bf16[16,32,128]{2,1,0:T(8,128)(2,1)S(1)}, bf16[16,32,128]{2,1,0:T(8,128)(2,1)S(1)}, u32[]{:S(2)}, u32[]{:S(2)}) collective-permute-start(bf16[16,32,128]{2,1,0:T(8,128)(2,1)S(1)} %products.13), channel_id=1, source_target_pairs={{0,3},{1,2},{2,1},{3,0},{4,7},{5,6},{6,5},{7,4},{8,11},{9,10},{10,... | collective-permute-start | bytes 393224 | tf_op jit(solution)/shard_map/ppermute | solution.py:305
  32.1 5.2 %collective-permute-start.7 = (bf16[16,32,128]{2,1,0:T(8,128)(2,1)S(1)}, bf16[16,32,128]{2,1,0:T(8,128)(2,1)S(1)}, u32[]{:S(2)}, u32[]{:S(2)}) collective-permute-start(bf16[16,32,128]{2,1,0:T(8,128)(2,1)S(1)} %products.14), channel_id=1, source_target_pairs={{0,1},{1,0},{2,3},{3,2},{4,5},{5,4},{6,7},{7,6},{8,9},{9,8},{10,11... | collective-permute-start | bytes 393224 | tf_op jit(solution)/shard_map/ppermute | solution.py:305
  34.6 6.1 %collective-permute-start.6 = (bf16[16,32,128]{2,1,0:T(8,128)(2,1)S(1)}, bf16[16,32,128]{2,1,0:T(8,128)(2,1)S(1)}, u32[]{:S(2)}, u32[]{:S(2)}) collective-permute-start(bf16[16,32,128]{2,1,0:T(8,128)(2,1)S(1)} %get-tuple-element.38), channel_id=1, source_target_pairs={{0,4},{4,0},{8,12},{12,8},{16,20},{20,16},{24,28},{28,24},{1,5},{5... | collective-permute-start | bytes 393224 | tf_op jit(solution)/shard_map/ppermute | solution.py:332
  37.6 7.2 %collective-permute-start.10 = (bf16[16,32,128]{2,1,0:T(8,128)(2,1)S(1)}, bf16[16,32,128]{2,1,0:T(8,128)(2,1)S(1)}, u32[]{:S(2)}, u32[]{:S(2)}) collective-permute-start(bf16[16,32,128]{2,1,0:T(8,128)(2,1)S(1)} %get-tuple-element.44.turned_ref), channel_id=1, source_target_pairs={{4,8},{8,4},{12,16},{16,12},{20,24},{24,20},{5,9},{9,5},{13,17},{1... | collective-permute-start | bytes 393224 | tf_op jit(solution)/shard_map/ppermute | solution.py:334

commit v9 on v8

--- a/solution.py
+++ b/solution.py
@@ -235,18 +235,22 @@
     )(*parts)
 
 
-def assemble(steps, near, far, turned):
-    stations, height, _ = turned.shape
+def assemble(steps, near, far=None, turned=None, done=None):
+    operands = (steps, *near) if done is None else (done, steps, *far, turned)
+    stations, height, _ = operands[-1].shape
     pairs, tiles = steps.shape[0], 2
-
-    def body(steps_ref, near_mine, near_theirs, far_mine, far_theirs, turned_ref, out_ref):
+    shape = (pairs, stations, stations * tiles * 2, LANES)
+
+    def body(*refs):
+        out_ref, buf, sems = refs[len(operands) :]
+        steps_ref, mine_ref, theirs_ref, *turned_ref = refs[0 if done is None else 1 : len(operands)]
         first = near_tile()
         column = lax.broadcasted_iota(jnp.int32, (stations, LANES), 0)
 
         def put(p, a, tile, value):
             for part in range(2):
                 rows = value[part * stations : (part + 1) * stations]
-                out_ref[p, a, pl.ds(tile * 2 + part, stations, stride=2 * tiles), :] = rows
+                buf[p, a, pl.ds(tile * 2 + part, stations, stride=2 * tiles), :] = rows
 
         def hermitian(p, a, tile, above, below, middle):
             re = jnp.where(column > a, above[:stations], below[:stations])
@@ -255,39 +259,62 @@
             im = jnp.where(column == a, jnp.zeros_like(im), im)
             put(p, a, tile, jnp.concatenate([re, im], axis=0))
 
+        def store(p, part):
+            rows = pl.ds(part * stations // 2, stations // 2)
+            return pltpu.make_async_copy(buf.at[p, rows], out_ref.at[p, rows], sems.at[p, part])
+
+        def fill(p, one):
+            for part in range(2):
+                for a in range(part * stations // 2, (part + 1) * stations // 2):
+                    one(p, a)
+                store(p, part).start()
+
+        def edge(mine_tile):
+            def one(p, a):
+                put(p, a, mine_tile, mine_ref[a])
+                put(p, a, 1 - mine_tile, theirs_ref[a].astype(WIDE))
+
+            return one
+
+        def itself(p, a):
+            own, back = mine_ref[a], turned_ref[0][a].astype(WIDE)
+            hermitian(p, a, 1 - first, own, back, own[:stations])
+            hermitian(p, a, first, back, own, own[stations:])
+
+        written = []
         for p in range(pairs):
             away = jnp.max(steps_ref[p])
             alone = jnp.abs(away) < 0.5
             inside = jnp.logical_and((away > 0.5) == (first == 1), jnp.logical_not(alone))
-            outside = jnp.logical_not(jnp.logical_or(alone, inside))
-
-            @pl.when(inside)
+            if done is None:
+                pl.when(inside)(lambda p=p: fill(p, edge(first)))
+                written.append(inside)
+            else:
+                outside = jnp.logical_not(jnp.logical_or(alone, inside))
+                pl.when(outside)(lambda p=p: fill(p, edge(1 - first)))
+                pl.when(alone)(lambda p=p: fill(p, itself))
+                written.append(jnp.logical_not(inside))
+        for p in range(pairs):
+
+            @pl.when(written[p])
             def _(p=p):
-                for a in range(stations):
-                    put(p, a, first, near_mine[a])
-                    put(p, a, 1 - first, near_theirs[a].astype(WIDE))
-
-            @pl.when(outside)
-            def _(p=p):
-                for a in range(stations):
-                    put(p, a, 1 - first, far_mine[a])
-                    put(p, a, first, far_theirs[a].astype(WIDE))
-
-            @pl.when(alone)
-            def _(p=p):
-                for a in range(stations):
-                    own, back = far_mine[a], turned_ref[a].astype(WIDE)
-                    hermitian(p, a, 1 - first, own, back, own[:stations])
-                    hermitian(p, a, first, back, own, own[stations:])
-
+                for part in range(2):
+                    store(p, part).wait()
+
+    hbm = pl.BlockSpec(memory_space=pltpu.HBM)
+    specs = [VMEM] * len(operands)
+    if done is not None:
+        specs[0] = hbm
     return pl.pallas_call(
         body,
-        in_specs=[VMEM] * 6,
-        out_specs=VMEM,
-        out_shape=jax.ShapeDtypeStruct((pairs, stations, stations * tiles * 2, LANES), WIDE),
+        in_specs=specs,
+        out_specs=hbm,
+        out_shape=jax.ShapeDtypeStruct(shape, WIDE),
+        scratch_shapes=[pltpu.VMEM(shape, WIDE), pltpu.SemaphoreType.DMA((pairs, 2))],
+        input_output_aliases={} if done is None else {0: 0},
         compiler_params=limits(4),
         name="assemble",
-    )(steps, *near, *far, turned)
+    )(*operands)
 
 
 def per_device(spectra, band_weight, station_order, pair_blocks):
@@ -332,7 +359,8 @@
     near_theirs = lax.ppermute(turned, "sta", on_chip)
     far_mine, turned = add_hours(after(far_parts[::-1], near_mine), scale)
     far_theirs = lax.ppermute(turned, "sta", across)
-    cross = assemble(steps, (near_mine, near_theirs), (far_mine, far_theirs), turned)
+    cross = assemble(steps, (near_mine, near_theirs))
+    cross = assemble(steps, None, (far_mine, far_theirs), turned, cross)
     cross = cross.reshape(pairs, stations, stations, tiles // hours, 2, LANES)
     return cross.transpose(0, 1, 2, 4, 3, 5).reshape(pairs, stations, stations, 2, bins // hours)
 

time: 46.7 us -> 46.6 us (level)
  waiting for transfers between devices: 12.2 us -> 11.2 us
  Pallas kernels: 13.7 us -> 14.4 us
    ppermute x1, waiting for transfers between devices: 4.04 us -> 3.07 us  [per_device(): far_theirs = lax.ppermute(turned, 'sta', across)]
    pallas_call x1 -> x2, Pallas kernels: 1.3 us -> 2.05 us  [assemble(): pl.pallas_call(body, in_specs=specs, out_specs=hbm, out_shape=jax.ShapeDt...]
  transfers between devices with their start and end apart: 11 -> 11, of which waited for: 5 -> 5; matrix products, arithmetic and copies ran while one was open for 0% -> 0% of each run, Pallas kernels for 19% -> 21%
where the time goes in v9:
time: 46.6 us; the launch traced here: 46 us
  starting transfers between devices  20.1 us (43%)
  Pallas kernels  14.4 us (31%)
  waiting for transfers between devices  11.2 us (24%)
    ppermute x6, starting transfers between devices, to_owner(): lax.ppermute(part, 'hour', [(h, h ^ d) for h in range(hours)])  9.67 us
    pallas_call x8, Pallas kernels, product_call(): pl.pallas_call(body, in_specs=[VMEM] * len(operands), out_specs=VMEM, out...  8.25 us
    pallas_call x1, Pallas kernels, whiten(): pl.pallas_call(body, in_specs=[hbm] * 4, out_specs=[VMEM] * (batches + 2)...  3.58 us
    ppermute x1, starting transfers between devices, per_device(): lax.ppermute(after(near[1], *near_made[:1]), 'sta', across)  3.43 us
    ppermute x1, starting transfers between devices, per_device(): far_theirs = lax.ppermute(turned, 'sta', across)  3.13 us
    ppermute x1, waiting for transfers between devices, per_device(): far_theirs = lax.ppermute(turned, 'sta', across)  3.07 us
    ppermute x1, waiting for transfers between devices, per_device(): lax.ppermute(after(near[1], *near_made[:1]), 'sta', across)  3.05 us
    ppermute x1, starting transfers between devices, per_device(): far_others = [lax.ppermute(near[0], 'sta', across)]  3.02 us
  transfers between devices with their start and end apart: 11, of which 5 were waited for; matrix products, arithmetic and copies ran while one was open for 0% of the time, Pallas kernels for 21%

profile of v9, /device:TPU:3, one launch (start us, length us, event | category | flops | bytes accessed | tf_op | source)
XLA Modules:
  0.0 46.0 jit_solution(10204237386750667101)
XLA Ops:
  0.0 3.6 %whiten.1 = (bf16[60,32,128]{2,1,0:T(8,128)(2,1)S(1)}, bf16[60,32,128]{2,1,0:T(8,128)(2,1)S(1)}, bf16[121,32,128]{2,1,0:T(8,128)(2,1)S(1)}, f32[2,8,128]{2,1,0:T(8,128)S(1)}) custom-call(s32[1,16]{1,0:T(1,128)} %order_hbm.1, s32[2,2]{1,0:T(2,128)} %pairs_hbm.1, f32[8,128]{1,0:T(8,128)} %bitcast.12, bf16[16,30,16,128]{3,2,1,0:T(8,128)(2,1)} %bitcast.11), custom_call_target="tpu_custom_call" | custom-call | tf_op jit(solution)/shard_map/whiten/pallas_call | solution.py:93
  3.6 0.7 %collective-permute-start = (bf16[121,32,128]{2,1,0:T(8,128)(2,1)S(1)}, bf16[121,32,128]{2,1,0:T(8,128)(2,1)S(1)}, u32[]{:S(2)}, u32[]{:S(2)}) collective-permute-start(bf16[121,32,128]{2,1,0:T(8,128)(2,1)S(1)} %get-tuple-element.27.own_ref), channel_id=1, source_target_pairs={{0,4},{4,0},{8,12},{12,8},{16,20},{20,16},{24,28},{28,24},{1,5},{5... | collective-permute-start | bytes 2973704 | tf_op jit(solution)/shard_map/ppermute | solution.py:337
  4.3 3.0 %collective-permute-start.4 = (bf16[60,32,128]{2,1,0:T(8,128)(2,1)S(1)}, bf16[60,32,128]{2,1,0:T(8,128)(2,1)S(1)}, u32[]{:S(2)}, u32[]{:S(2)}) collective-permute-start(bf16[60,32,128]{2,1,0:T(8,128)(2,1)S(1)} %get-tuple-element.28.own_ref.near_ref), channel_id=1, source_target_pairs={{4,8},{8,4},{12,16},{16,12},{20,24},{24,20},{5,9},{9,5},{13,17},{1... | collective-permute-start | bytes 1474568 | tf_op jit(solution)/shard_map/ppermute | solution.py:338
  7.4 0.0 collective-permute-done.other_ref
  7.4 1.0 %products.11 = bf16[16,32,128]{2,1,0:T(8,128)(2,1)S(1)} custom-call(bf16[60,32,128]{2,1,0:T(8,128)(2,1)S(1)} %get-tuple-element.28.own_ref.near_ref, bf16[121,32,128]{2,1,0:T(8,128)(2,1)S(1)} %collective-permute-done.other_ref), custom_call_target="tpu_custom_call" | custom-call | flops 7864320 | bytes 524288 | tf_op jit(solution)/shard_map/products/pallas_call | solution.py:148
  8.3 3.4 %collective-permute-start.5 = (bf16[60,32,128]{2,1,0:T(8,128)(2,1)S(1)}, bf16[60,32,128]{2,1,0:T(8,128)(2,1)S(1)}, u32[]{:S(2)}, u32[]{:S(2)}) collective-permute-start(bf16[60,32,128]{2,1,0:T(8,128)(2,1)S(1)} %get-tuple-element.31.own_ref.near_ref), channel_id=1, source_target_pairs={{4,8},{8,4},{12,16},{16,12},{20,24},{24,20},{5,9},{9,5},{13,17},{1... | collective-permute-start | bytes 1474568 | tf_op jit(solution)/shard_map/ppermute | solution.py:346
  11.8 2.4 %collective-permute-start.3 = (bf16[16,32,128]{2,1,0:T(8,128)(2,1)S(1)}, bf16[16,32,128]{2,1,0:T(8,128)(2,1)S(1)}, u32[]{:S(2)}, u32[]{:S(2)}) collective-permute-start(bf16[16,32,128]{2,1,0:T(8,128)(2,1)S(1)} %products.11), channel_id=1, source_target_pairs={{0,2},{1,3},{2,0},{3,1},{4,6},{5,7},{6,4},{7,5},{8,10},{9,11},{10,... | collective-permute-start | bytes 393224 | tf_op jit(solution)/shard_map/ppermute | solution.py:332
  14.1 0.9 %products.10 = bf16[16,32,128]{2,1,0:T(8,128)(2,1)S(1)} custom-call(bf16[60,32,128]{2,1,0:T(8,128)(2,1)S(1)} %get-tuple-element.28.own_ref.near_ref, bf16[121,32,128]{2,1,0:T(8,128)(2,1)S(1)} %collective-permute-done.other_ref), custom_call_target="tpu_custom_call" | custom-call | flops 7864320 | bytes 524288 | tf_op jit(solution)/shard_map/products/pallas_call | solution.py:148
  15.1 1.1 %collective-permute-start.2 = (bf16[16,32,128]{2,1,0:T(8,128)(2,1)S(1)}, bf16[16,32,128]{2,1,0:T(8,128)(2,1)S(1)}, u32[]{:S(2)}, u32[]{:S(2)}) collective-permute-start(bf16[16,32,128]{2,1,0:T(8,128)(2,1)S(1)} %products.10), channel_id=1, source_target_pairs={{0,3},{1,2},{2,1},{3,0},{4,7},{5,6},{6,5},{7,4},{8,11},{9,10},{10,... | collective-permute-start | bytes 393224 | tf_op jit(solution)/shard_map/ppermute | solution.py:332
  16.2 0.9 %products.9 = bf16[16,32,128]{2,1,0:T(8,128)(2,1)S(1)} custom-call(bf16[60,32,128]{2,1,0:T(8,128)(2,1)S(1)} %get-tuple-element.31.own_ref.near_ref, bf16[121,32,128]{2,1,0:T(8,128)(2,1)S(1)} %collective-permute-done.other_ref), custom_call_target="tpu_custom_call" | custom-call | flops 7864320 | bytes 524288 | tf_op jit(solution)/shard_map/products/pallas_call | solution.py:148
  17.2 0.3 collective-permute-start.1
  17.5 0.9 %products.8.refs_0_ = f32[16,32,128]{2,1,0:T(8,128)S(1)} custom-call(bf16[60,32,128]{2,1,0:T(8,128)(2,1)S(1)} %get-tuple-element.31.own_ref.near_ref, bf16[121,32,128]{2,1,0:T(8,128)(2,1)S(1)} %collective-permute-done.other_ref), custom_call_target="tpu_custom_call" | custom-call | flops 7864320 | bytes 524288 | tf_op jit(solution)/shard_map/products/pallas_call | solution.py:148
  18.4 2.4 %collective-permute-done.4.other_ref = bf16[60,32,128]{2,1,0:T(8,128)(2,1)S(1)} collective-permute-done((bf16[60,32,128]{2,1,0:T(8,128)(2,1)S(1)}, bf16[60,32,128]{2,1,0:T(8,128)(2,1)S(1)}, u32[]{:S(2)}, u32[]{:S(2)}) %collective-permute-start.4) | collective-permute-done | bytes 491552 | tf_op jit(solution)/shard_map/ppermute | solution.py:338
  20.9 1.1 %products.12 = bf16[16,32,128]{2,1,0:T(8,128)(2,1)S(1)} custom-call(bf16[121,32,128]{2,1,0:T(8,128)(2,1)S(1)} %get-tuple-element.27.own_ref, bf16[60,32,128]{2,1,0:T(8,128)(2,1)S(1)} %collective-permute-done.4.other_ref, bf16[60,32,128]{2,1,0:T(8,128)(2,1)S(1)} %get-tuple-element.28.own_ref.near_ref), custom_call_target="tpu_custom_call" | custom-call | flops 7864320 | bytes 524288 | tf_op jit(solution)/shard_map/products/pallas_call | solution.py:148
  21.9 2.1 %collective-permute-start.9 = (bf16[16,32,128]{2,1,0:T(8,128)(2,1)S(1)}, bf16[16,32,128]{2,1,0:T(8,128)(2,1)S(1)}, u32[]{:S(2)}, u32[]{:S(2)}) collective-permute-start(bf16[16,32,128]{2,1,0:T(8,128)(2,1)S(1)} %products.12), channel_id=1, source_target_pairs={{0,2},{1,3},{2,0},{3,1},{4,6},{5,7},{6,4},{7,5},{8,10},{9,11},{10,... | collective-permute-start | bytes 393224 | tf_op jit(solution)/shard_map/ppermute | solution.py:332
  24.0 0.0 collective-permute-done.3.refs_3_
  24.0 1.1 %products.13 = bf16[16,32,128]{2,1,0:T(8,128)(2,1)S(1)} custom-call(bf16[121,32,128]{2,1,0:T(8,128)(2,1)S(1)} %get-tuple-element.27.own_ref, bf16[60,32,128]{2,1,0:T(8,128)(2,1)S(1)} %collective-permute-done.4.other_ref, bf16[60,32,128]{2,1,0:T(8,128)(2,1)S(1)} %get-tuple-element.28.own_ref.near_ref), custom_call_target="tpu_custom_call" | custom-call | flops 7864320 | bytes 524288 | tf_op jit(solution)/shard_map/products/pallas_call | solution.py:148
  25.1 2.7 %collective-permute-start.8 = (bf16[16,32,128]{2,1,0:T(8,128)(2,1)S(1)}, bf16[16,32,128]{2,1,0:T(8,128)(2,1)S(1)}, u32[]{:S(2)}, u32[]{:S(2)}) collective-permute-start(bf16[16,32,128]{2,1,0:T(8,128)(2,1)S(1)} %products.13), channel_id=1, source_target_pairs={{0,3},{1,2},{2,1},{3,0},{4,7},{5,6},{6,5},{7,4},{8,11},{9,10},{10,... | collective-permute-start | bytes 393224 | tf_op jit(solution)/shard_map/ppermute | solution.py:332
  27.8 3.0 %collective-permute-done.5.other_ref = bf16[60,32,128]{2,1,0:T(8,128)(2,1)S(1)} collective-permute-done((bf16[60,32,128]{2,1,0:T(8,128)(2,1)S(1)}, bf16[60,32,128]{2,1,0:T(8,128)(2,1)S(1)}, u32[]{:S(2)}, u32[]{:S(2)}) %collective-permute-start.5) | collective-permute-done | bytes 491552 | tf_op jit(solution)/shard_map/ppermute | solution.py:346
  30.9 1.2 %products.14 = bf16[16,32,128]{2,1,0:T(8,128)(2,1)S(1)} custom-call(bf16[121,32,128]{2,1,0:T(8,128)(2,1)S(1)} %get-tuple-element.27.own_ref, bf16[60,32,128]{2,1,0:T(8,128)(2,1)S(1)} %collective-permute-done.5.other_ref, bf16[60,32,128]{2,1,0:T(8,128)(2,1)S(1)} %get-tuple-element.31.own_ref.near_ref), custom_call_target="tpu_custom_call" | custom-call | flops 7864320 | bytes 524288 | tf_op jit(solution)/shard_map/products/pallas_call | solution.py:148
  32.1 1.1 %collective-permute-start.7 = (bf16[16,32,128]{2,1,0:T(8,128)(2,1)S(1)}, bf16[16,32,128]{2,1,0:T(8,128)(2,1)S(1)}, u32[]{:S(2)}, u32[]{:S(2)}) collective-permute-start(bf16[16,32,128]{2,1,0:T(8,128)(2,1)S(1)} %products.14), channel_id=1, source_target_pairs={{0,1},{1,0},{2,3},{3,2},{4,5},{5,4},{6,7},{7,6},{8,9},{9,8},{10,11... | collective-permute-start | bytes 393224 | tf_op jit(solution)/shard_map/ppermute | solution.py:332
  33.2 1.1 %products.15.refs_0_ = f32[16,32,128]{2,1,0:T(8,128)S(1)} custom-call(bf16[121,32,128]{2,1,0:T(8,128)(2,1)S(1)} %get-tuple-element.27.own_ref, bf16[60,32,128]{2,1,0:T(8,128)(2,1)S(1)} %collective-permute-done.5.other_ref, bf16[60,32,128]{2,1,0:T(8,128)(2,1)S(1)} %get-tuple-element.31.own_ref.near_ref), custom_call_target="tpu_custom_call" | custom-call | flops 7864320 | bytes 524288 | tf_op jit(solution)/shard_map/products/pallas_call | solution.py:148
  34.3 0.0 collective-permute-done.2.refs_2_
  34.3 0.0 collective-permute-done.1.refs_1_
  34.3 0.3 add_hours.2
  34.6 0.1 collective-permute-start.6
  34.6 0.1 collective-permute-done.9.refs_3_
  34.8 0.0 collective-permute-done.8.refs_2_
  34.8 2.5 %collective-permute-done.7.refs_1_ = bf16[16,32,128]{2,1,0:T(8,128)(2,1)S(1)} collective-permute-done((bf16[16,32,128]{2,1,0:T(8,128)(2,1)S(1)}, bf16[16,32,128]{2,1,0:T(8,128)(2,1)S(1)}, u32[]{:S(2)}, u32[]{:S(2)}) %collective-permute-start.7) | collective-permute-done | bytes 131104 | tf_op jit(solution)/shard_map/ppermute | solution.py:332
  37.3 0.3 add_hours.3
  37.6 3.1 %collective-permute-start.10 = (bf16[16,32,128]{2,1,0:T(8,128)(2,1)S(1)}, bf16[16,32,128]{2,1,0:T(8,128)(2,1)S(1)}, u32[]{:S(2)}, u32[]{:S(2)}) collective-permute-start(bf16[16,32,128]{2,1,0:T(8,128)(2,1)S(1)} %get-tuple-element.44.refs_4_), channel_id=1, source_target_pairs={{4,8},{8,4},{12,16},{16,12},{20,24},{24,20},{5,9},{9,5},{13,17},{1... | collective-permute-start | bytes 393224 | tf_op jit(solution)/shard_map/ppermute | solution.py:361
  40.7 0.0 collective-permute-done.6.refs_2_
  40.7 1.0 %assemble.2.refs_0_ = f32[2,16,64,128]{3,2,1,0:T(8,128)} custom-call(f32[2,8,128]{2,1,0:T(8,128)S(1)} %get-tuple-element.25.refs_0_.refs_1_, f32[16,32,128]{2,1,0:T(8,128)S(1)} %get-tuple-element.37.refs_1_, bf16[16,32,128]{2,1,0:T(8,128)(2,1)S(1)} %collective-permute-done.6.refs_2_), custom_call_target="tpu_custom_call" | custom-call | tf_op jit(solution)/shard_map/assemble/pallas_call | solution.py:308
  41.7 3.1 %collective-permute-done.10.refs_3_ = bf16[16,32,128]{2,1,0:T(8,128)(2,1)S(1)} collective-permute-done((bf16[16,32,128]{2,1,0:T(8,128)(2,1)S(1)}, bf16[16,32,128]{2,1,0:T(8,128)(2,1)S(1)}, u32[]{:S(2)}, u32[]{:S(2)}) %collective-permute-start.10) | collective-permute-done | bytes 131104 | tf_op jit(solution)/shard_map/ppermute | solution.py:361
  44.8 1.1 %assemble.3 = f32[2,16,64,128]{3,2,1,0:T(8,128)} custom-call(f32[2,16,64,128]{3,2,1,0:T(8,128)} %assemble.2.refs_0_, f32[2,8,128]{2,1,0:T(8,128)S(1)} %get-tuple-element.25.refs_0_.refs_1_, f32[16,32,128]{2,1,0:T(8,128)S(1)} %get-tuple-element.43.refs_2_, bf16[16,32,128]{2,1,0:T(8,128)(2,1)S(1)} %collective-permute-done.10.refs_3_, ...), custom_call_target="tpu_custom_call", output_to_operand_aliasing={{}: (0, {})} | custom-call | tf_op jit(solution)/shard_map/assemble/pallas_call | solution.py:308
Async XLA Ops:
  3.6 3.8 %collective-permute-start = (bf16[121,32,128]{2,1,0:T(8,128)(2,1)S(1)}, bf16[121,32,128]{2,1,0:T(8,128)(2,1)S(1)}, u32[]{:S(2)}, u32[]{:S(2)}) collective-permute-start(bf16[121,32,128]{2,1,0:T(8,128)(2,1)S(1)} %get-tuple-element.27.own_ref), channel_id=1, source_target_pairs={{0,4},{4,0},{8,12},{12,8},{16,20},{20,16},{24,28},{28,24},{1,5},{5... | collective-permute-start | bytes 2973704 | tf_op jit(solution)/shard_map/ppermute | solution.py:337
  4.3 16.5 %collective-permute-start.4 = (bf16[60,32,128]{2,1,0:T(8,128)(2,1)S(1)}, bf16[60,32,128]{2,1,0:T(8,128)(2,1)S(1)}, u32[]{:S(2)}, u32[]{:S(2)}) collective-permute-start(bf16[60,32,128]{2,1,0:T(8,128)(2,1)S(1)} %get-tuple-element.28.own_ref.near_ref), channel_id=1, source_target_pairs={{4,8},{8,4},{12,16},{16,12},{20,24},{24,20},{5,9},{9,5},{13,17},{1... | collective-permute-start | bytes 1474568 | tf_op jit(solution)/shard_map/ppermute | solution.py:338
  8.3 22.5 %collective-permute-start.5 = (bf16[60,32,128]{2,1,0:T(8,128)(2,1)S(1)}, bf16[60,32,128]{2,1,0:T(8,128)(2,1)S(1)}, u32[]{:S(2)}, u32[]{:S(2)}) collective-permute-start(bf16[60,32,128]{2,1,0:T(8,128)(2,1)S(1)} %get-tuple-element.31.own_ref.near_ref), channel_id=1, source_target_pairs={{4,8},{8,4},{12,16},{16,12},{20,24},{24,20},{5,9},{9,5},{13,17},{1... | collective-permute-start | bytes 1474568 | tf_op jit(solution)/shard_map/ppermute | solution.py:346
  11.8 12.3 %collective-permute-start.3 = (bf16[16,32,128]{2,1,0:T(8,128)(2,1)S(1)}, bf16[16,32,128]{2,1,0:T(8,128)(2,1)S(1)}, u32[]{:S(2)}, u32[]{:S(2)}) collective-permute-start(bf16[16,32,128]{2,1,0:T(8,128)(2,1)S(1)} %products.11), channel_id=1, source_target_pairs={{0,2},{1,3},{2,0},{3,1},{4,6},{5,7},{6,4},{7,5},{8,10},{9,11},{10,... | collective-permute-start | bytes 393224 | tf_op jit(solution)/shard_map/ppermute | solution.py:332
  15.1 19.2 %collective-permute-start.2 = (bf16[16,32,128]{2,1,0:T(8,128)(2,1)S(1)}, bf16[16,32,128]{2,1,0:T(8,128)(2,1)S(1)}, u32[]{:S(2)}, u32[]{:S(2)}) collective-permute-start(bf16[16,32,128]{2,1,0:T(8,128)(2,1)S(1)} %products.10), channel_id=1, source_target_pairs={{0,3},{1,2},{2,1},{3,0},{4,7},{5,6},{6,5},{7,4},{8,11},{9,10},{10,... | collective-permute-start | bytes 393224 | tf_op jit(solution)/shard_map/ppermute | solution.py:332
  17.2 17.1 %collective-permute-start.1 = (bf16[16,32,128]{2,1,0:T(8,128)(2,1)S(1)}, bf16[16,32,128]{2,1,0:T(8,128)(2,1)S(1)}, u32[]{:S(2)}, u32[]{:S(2)}) collective-permute-start(bf16[16,32,128]{2,1,0:T(8,128)(2,1)S(1)} %products.9), channel_id=1, source_target_pairs={{0,1},{1,0},{2,3},{3,2},{4,5},{5,4},{6,7},{7,6},{8,9},{9,8},{10,11... | collective-permute-start | bytes 393224 | tf_op jit(solution)/shard_map/ppermute | solution.py:332
  21.9 12.8 %collective-permute-start.9 = (bf16[16,32,128]{2,1,0:T(8,128)(2,1)S(1)}, bf16[16,32,128]{2,1,0:T(8,128)(2,1)S(1)}, u32[]{:S(2)}, u32[]{:S(2)}) collective-permute-start(bf16[16,32,128]{2,1,0:T(8,128)(2,1)S(1)} %products.12), channel_id=1, source_target_pairs={{0,2},{1,3},{2,0},{3,1},{4,6},{5,7},{6,4},{7,5},{8,10},{9,11},{10,... | collective-permute-start | bytes 393224 | tf_op jit(solution)/shard_map/ppermute | solution.py:332
  25.1 9.7 %collective-permute-start.8 = (bf16[16,32,128]{2,1,0:T(8,128)(2,1)S(1)}, bf16[16,32,128]{2,1,0:T(8,128)(2,1)S(1)}, u32[]{:S(2)}, u32[]{:S(2)}) collective-permute-start(bf16[16,32,128]{2,1,0:T(8,128)(2,1)S(1)} %products.13), channel_id=1, source_target_pairs={{0,3},{1,2},{2,1},{3,0},{4,7},{5,6},{6,5},{7,4},{8,11},{9,10},{10,... | collective-permute-start | bytes 393224 | tf_op jit(solution)/shard_map/ppermute | solution.py:332
  32.1 5.2 %collective-permute-start.7 = (bf16[16,32,128]{2,1,0:T(8,128)(2,1)S(1)}, bf16[16,32,128]{2,1,0:T(8,128)(2,1)S(1)}, u32[]{:S(2)}, u32[]{:S(2)}) collective-permute-start(bf16[16,32,128]{2,1,0:T(8,128)(2,1)S(1)} %products.14), channel_id=1, source_target_pairs={{0,1},{1,0},{2,3},{3,2},{4,5},{5,4},{6,7},{7,6},{8,9},{9,8},{10,11... | collective-permute-start | bytes 393224 | tf_op jit(solution)/shard_map/ppermute | solution.py:332
  34.6 6.1 %collective-permute-start.6 = (bf16[16,32,128]{2,1,0:T(8,128)(2,1)S(1)}, bf16[16,32,128]{2,1,0:T(8,128)(2,1)S(1)}, u32[]{:S(2)}, u32[]{:S(2)}) collective-permute-start(bf16[16,32,128]{2,1,0:T(8,128)(2,1)S(1)} %get-tuple-element.38), channel_id=1, source_target_pairs={{0,4},{4,0},{8,12},{12,8},{16,20},{20,16},{24,28},{28,24},{1,5},{5... | collective-permute-start | bytes 393224 | tf_op jit(solution)/shard_map/ppermute | solution.py:359
  37.6 7.2 %collective-permute-start.10 = (bf16[16,32,128]{2,1,0:T(8,128)(2,1)S(1)}, bf16[16,32,128]{2,1,0:T(8,128)(2,1)S(1)}, u32[]{:S(2)}, u32[]{:S(2)}) collective-permute-start(bf16[16,32,128]{2,1,0:T(8,128)(2,1)S(1)} %get-tuple-element.44.refs_4_), channel_id=1, source_target_pairs={{4,8},{8,4},{12,16},{16,12},{20,24},{24,20},{5,9},{9,5},{13,17},{1... | collective-permute-start | bytes 393224 | tf_op jit(solution)/shard_map/ppermute | solution.py:361
